TPU v7x, 32 devices: a whole 2x2x4 slice. The times are simulated.
32 devices in a mesh: dp: 8 (over z, x), ctx: 4 (over y, core).
Axes of the slice: x: 2, y: 2, z: 4, core: 2. Of those that a mesh axis runs over, the one named last changes fastest.
Arguments:
- q_short: bfloat16 [6144, 1024], P('dp', 'ctx'), may hold values from -64 to 64
- k_short: bfloat16 [6144, 1024], P('dp', 'ctx'), may hold values from -8 to 8
- v_short: bfloat16 [6144, 1024], P('dp', 'ctx'), may hold values from -6 to 6
- dout_short: bfloat16 [6144, 1024], P('dp', 'ctx'), may hold values from -6 to 6
- doc_lengths: int32 [8, 8], replicated, may hold values from 1 to 256, as said below
- doc_dest: int32 [8, 8], replicated, may hold values from 0 to 7, as said below
- q_long: bfloat16 [8, 512, 1024], P('dp', 'ctx'), may hold values from -64 to 64
- k_long: bfloat16 [8, 512, 1024], P('dp', 'ctx'), may hold values from -8 to 8
- v_long: bfloat16 [8, 512, 1024], P('dp', 'ctx'), may hold values from -6 to 6
- dout_long: bfloat16 [8, 512, 1024], P('dp', 'ctx'), may hold values from -6 to 6
- block_order: int32 [8], replicated, may hold values from 0 to 7, each once
Outputs:
- out_short: bfloat16 [7168, 1024], P('dp', 'ctx')
- dq_short: bfloat16 [6144, 1024], P('dp', 'ctx')
- dk_short: bfloat16 [6144, 1024], P('dp', 'ctx')
- dv_short: bfloat16 [6144, 1024], P('dp', 'ctx')
- out_long: bfloat16 [8, 512, 1024], P('dp', 'ctx')
- dq_long: bfloat16 [8, 512, 1024], P('dp', 'ctx')
- dk_long: bfloat16 [8, 512, 1024], P('dp', 'ctx')
- dv_long: bfloat16 [8, 512, 1024], P('dp', 'ctx')
Inputs may be any that keep to these rules, and one draw needn't show every extreme that they name: `doc_lengths`: row r lists in order the lengths of the documents packed on rank r; each row sums to 768. `doc_dest`: entry [r, j] is r, except that in each pair of ranks r and r + 4 exactly one assigns its last document to the other; such a document has at most 128 tokens, and some has exactly 128. `block_order`: A permutation.
All inputs are finite; a program needn't handle non-finite values.
Results may differ from a plain program's by a relative error of at most 0.015.
Values may be sent and summed in bfloat16 or wider, within the bound.
No kernel may reach another device: no remote copies, remote signals or barrier semaphores. Data moves between devices by JAX's collectives and lax.ppermute only.
A program may use at most 64 MiB of HBM per device.

v0:
```python
import jax
import jax.numpy as jnp
from jax import lax
from jax.sharding import PartitionSpec as P

HEAD_DIM = 128


NEG = -1e30


def shifted(value, axis, steps):
    count = lax.axis_size(axis)
    pairs = [(source, (source + steps) % count) for source in range(count)]
    return lax.ppermute(value, axis, pairs)


def dot_rows(left, right):
    return lax.dot_general(
        left, right, (((1,), (1,)), ((), ())), preferred_element_type=jnp.float32
    )


def dot_cols(left, right):
    return lax.dot_general(
        left, right, (((0,), (0,)), ((), ())), preferred_element_type=jnp.float32
    )


def column_of(array, head):
    return array[:, head * HEAD_DIM : (head + 1) * HEAD_DIM]


def attend_head(queries, keys, values, douts, mask, scale):
    scores = dot_rows(queries, keys) * scale
    scores = jnp.where(mask, scores, NEG)
    top = jnp.max(scores, axis=1, keepdims=True)
    lse = top + jnp.log(jnp.sum(jnp.exp(scores - top), axis=1, keepdims=True))
    probs = jnp.where(mask, jnp.exp(scores - lse), 0.0)
    weights = probs.astype(jnp.bfloat16)
    attended = jnp.dot(weights, values, preferred_element_type=jnp.float32).astype(jnp.bfloat16)
    dprobs = dot_rows(douts, values)
    delta = jnp.sum(douts.astype(jnp.float32) * attended.astype(jnp.float32), axis=1)
    score_grads = (probs * (dprobs - delta[:, None])).astype(jnp.bfloat16)
    grad_q = jnp.dot(score_grads, keys, preferred_element_type=jnp.float32) * scale
    return (attended, grad_q, score_grads, weights, lse[:, 0], delta)


def block_pass(queries, keys, values, douts, mask, scale):
    heads = queries.shape[1] // HEAD_DIM
    attended_list, query_list, key_list, value_list = ([], [], [], [])
    for head in range(heads):
        q_head = column_of(queries, head)
        d_head = column_of(douts, head)
        attended, grad_q, score_grads, weights, lse, delta = attend_head(
            q_head, column_of(keys, head), column_of(values, head), d_head, mask, scale
        )
        attended_list.append(attended)
        query_list.append(grad_q)
        key_list.append(dot_cols(score_grads, q_head) * scale)
        value_list.append(dot_cols(weights, d_head))
    join = lambda parts: jnp.concatenate(parts, axis=1)
    return (join(attended_list), join(query_list), join(key_list), join(value_list))


def band_attention(queries, keys, values, douts, doc_of, live, scale):
    token_count, width = queries.shape
    block = token_count // 3
    place = jnp.arange(token_count, dtype=jnp.int32)
    attended_parts = []
    query_parts = []
    grad_k = jnp.zeros((token_count, width), jnp.float32)
    grad_v = jnp.zeros((token_count, width), jnp.float32)
    for number in range(3):
        query_start = number * block
        query_end = query_start + block
        key_start = max(0, query_start - block)
        mask = doc_of[None, key_start:query_end] == doc_of[query_start:query_end, None]
        mask = mask & (place[None, key_start:query_end] <= place[query_start:query_end, None])
        mask = mask & live[query_start:query_end, None] & live[None, key_start:query_end]
        attended, grad_q, part_k, part_v = block_pass(
            queries[query_start:query_end],
            keys[key_start:query_end],
            values[key_start:query_end],
            douts[query_start:query_end],
            mask,
            scale,
        )
        attended_parts.append(attended)
        query_parts.append(grad_q)
        grad_k = grad_k.at[key_start:query_end].add(part_k)
        grad_v = grad_v.at[key_start:query_end].add(part_v)
    attended = jnp.concatenate(attended_parts, axis=0)
    grad_q = jnp.concatenate(query_parts, axis=0)
    return (
        attended,
        grad_q.astype(jnp.bfloat16),
        grad_k.astype(jnp.bfloat16),
        grad_v.astype(jnp.bfloat16),
    )


def front_align(block, count_in, rows, axis):
    padded = jnp.concatenate([block, jnp.zeros_like(block)], axis=axis)
    return lax.dynamic_slice_in_dim(padded, rows - count_in, rows, axis)


def positions(block_order, total, rows):
    half = rows // 2
    index = jnp.arange(total, dtype=jnp.int32)
    onehot = (
        (index // half)[:, None] == jnp.arange(block_order.shape[0], dtype=jnp.int32)[None, :]
    ).astype(jnp.int32)
    return jnp.sum(onehot * block_order[None, :], axis=1) * half + index % half


def shards(
    q_short,
    k_short,
    v_short,
    dout_short,
    doc_lengths,
    doc_dest,
    q_long,
    k_long,
    v_long,
    dout_long,
    block_order,
):
    scale = HEAD_DIM ** (-0.5)
    token_count, features = q_short.shape
    count = doc_lengths.shape[1]
    ranks = doc_lengths.shape[0]
    half = lax.axis_size("dp") // 2
    move_rows = token_count // 6
    rank = lax.axis_index("dp")
    partner = (rank + half) % ranks
    length_row = lax.dynamic_index_in_dim(doc_lengths, rank, 0, keepdims=False)
    dest_row = lax.dynamic_index_in_dim(doc_dest, rank, 0, keepdims=False)
    partner_lengths = lax.dynamic_index_in_dim(doc_lengths, partner, 0, keepdims=False)
    partner_dest = lax.dynamic_index_in_dim(doc_dest, partner, 0, keepdims=False)
    moves = dest_row[count - 1] != rank
    tail = length_row[count - 1]
    incoming = jnp.where(partner_dest[count - 1] != partner, partner_lengths[count - 1], 0)
    starts = jnp.cumsum(length_row) - length_row
    place = jnp.arange(token_count, dtype=jnp.int32)
    doc_of = jnp.sum((place[:, None] >= starts[None, :]).astype(jnp.int32), axis=1) - 1
    moved = moves & (place >= token_count - tail)
    tail_moved = moved[token_count - move_rows :]
    slots = jnp.arange(move_rows, dtype=jnp.int32)
    zero = jnp.zeros((), jnp.bfloat16)
    attended, grad_q, grad_k, grad_v = band_attention(
        q_short, k_short, v_short, dout_short, doc_of, jnp.ones((token_count,), bool), scale
    )
    outgoing = jnp.where(tail_moved[:, None], attended[token_count - move_rows :], zero)
    arrived = shifted(outgoing, "dp", half)
    received = front_align(arrived, incoming, move_rows, 0)
    received = jnp.where((slots < incoming)[:, None], received, zero)
    own = jnp.where(moved[:, None], zero, attended)
    out_short = jnp.concatenate([own, received], axis=0)
    dq_short = grad_q
    rows = q_long.shape[1]
    wide = q_long.shape[2]
    heads = wide // HEAD_DIM
    total = rows * lax.axis_size("ctx")
    place_all = positions(block_order, total, rows)
    place_own = lax.dynamic_slice_in_dim(place_all, lax.axis_index("ctx") * rows, rows)
    local_q = q_long[0]
    local_k = k_long[0]
    local_v = v_long[0]
    local_d = dout_long[0]
    own_mask = place_all[None, :] <= place_own[:, None]
    join = lambda parts: jnp.concatenate(parts, axis=1)
    all_k, all_v = (
        lax.all_gather(local_k, "ctx", axis=0, tiled=True),
        lax.all_gather(local_v, "ctx", axis=0, tiled=True),
    )
    attended_list, query_list, grad_list, weight_list = ([], [], [], [])
    for head in range(heads):
        attended, grad_q, score_grads, weights, lse, delta = attend_head(
            column_of(local_q, head),
            column_of(all_k, head),
            column_of(all_v, head),
            column_of(local_d, head),
            own_mask,
            scale,
        )
        attended_list.append(attended)
        query_list.append(grad_q)
        grad_list.append(score_grads)
        weight_list.append(weights)
    long_att = join(attended_list)
    long_q = join(query_list)
    key_parts = []
    value_parts = []
    for head in range(heads):
        grads_part = grad_list[head]
        weights_part = weight_list[head]
        key_parts.append(dot_cols(grads_part, column_of(local_q, head)) * scale)
        value_parts.append(dot_cols(weights_part, column_of(local_d, head)))
    summed = lax.psum_scatter(
        jnp.concatenate(key_parts + value_parts, axis=1), "ctx", scatter_dimension=0, tiled=True
    )
    long_k = summed[:, :wide]
    long_v = summed[:, wide:]
    out_long = long_att.reshape(1, rows, wide)
    dq_long = long_q.astype(jnp.bfloat16).reshape(1, rows, wide)
    dk_long = long_k.astype(jnp.bfloat16).reshape(1, rows, wide)
    dv_long = long_v.astype(jnp.bfloat16).reshape(1, rows, wide)
    return (out_short, dq_short, grad_k, grad_v, out_long, dq_long, dk_long, dv_long)


def solution(mesh):
    placed = (
        P("dp", "ctx"),
        P("dp", "ctx"),
        P("dp", "ctx"),
        P("dp", "ctx"),
        P(),
        P(),
        P("dp", "ctx", None),
        P("dp", "ctx", None),
        P("dp", "ctx", None),
        P("dp", "ctx", None),
        P(),
    )
    return jax.shard_map(
        shards,
        mesh=mesh,
        in_specs=placed,
        out_specs=(
            P("dp", "ctx"),
            P("dp", "ctx"),
            P("dp", "ctx"),
            P("dp", "ctx"),
            P("dp", "ctx", None),
            P("dp", "ctx", None),
            P("dp", "ctx", None),
            P("dp", "ctx", None),
        ),
        check_vma=False,
    )
```

profile of v0, /device:TPU:0, one launch (start us, length us, event | category | flops | bytes accessed | tf_op | source)
XLA Modules:
  0.0 138.3 jit_solution(7261635066943210378)
XLA Ops:
  8.0 1.3 constant_dynamic-slice_fusion.2
  11.6 1.7 %fusion.247 = (bf16[256,128]{1,0:T(8,128)(2,1)S(1)}, bf16[256,128]{1,0:T(8,128)(2,1)S(1)}, bf16[256,128]{1,0:T(8,128)(2,1)}, bf16[256,128]{1,0:T(8,128)(2,1)}, b...) fusion(bf16[768,256]{1,0:T(8,128)(2,1)} %param.26), kind=kLoop, calls=%fused_computation.402 | loop fusion | bytes 786432
  13.9 1.3 fusion.250
  15.7 1.3 fusion.251
  17.2 1.0 multiply_reduce_fusion
  19.8 4.1 %collective-permute-start = (bf16[128,256]{0,1:T(8,128)(2,1)}, bf16[128,256]{0,1:T(8,128)(2,1)}, u32[]{:S(2)}, u32[]{:S(2)}) collective-permute-start(bf16[128,256]{0,1:T(8,128)(2,1)} %fusion.139), channel_id=1, source_target_pairs={{0,16},{4,20},{8,24},{12,28},{16,0},{20,4},{24,8},{28,12},{1,17},{... | collective-permute-start | bytes 196616 | tf_op jit(solution)/shard_map/ppermute | solution.py:15
  27.0 1.0 fusion.210
  28.1 1.1 copy.44
  29.2 1.0 exponential_reduce_fusion.12
  30.3 1.2 fusion.201
  31.5 1.0 exponential_reduce_fusion.13
  32.6 1.9 %fusion.204 = f32[256,128]{0,1:T(8,128)} fusion(f32[256,256]{0,1:T(8,128)} %get-tuple-element.132, f32[256]{0:T(256)S(1)} %log_add_fusion.5, bf16[768,256]{1,0:T(8,128)(2,1)S(1)} %copy-done.29, s32[256]{0:T(256)S(1)} %slice.393, s32[256]{0:T(256)S(1)} %get-tuple-element.112), kind=kOutput, calls=%fused_computation.385 | convolution fusion | flops 17170432 | bytes 463872 | tf_op jit(solution)/shard_map/dot_general | solution.py:25
  35.5 1.7 %fusion.213 = f32[512,128]{0,1:T(8,128)} fusion(bf16[768,256]{1,0:T(8,128)(2,1)S(1)} %copy-done.29, f32[256,512]{1,0:T(8,128)S(1)} %get-tuple-element.126, f32[256]{0:T(256)S(1)} %log_add_fusion.2, s32[512]{0:T(512)} %copy-done.43, s32[512]{0:T(512)} %copy-done.47, s32[256]{0:T(256)} %copy-done.63, s32[256]{0:T(256)} %copy-done.68), kind=kOutput, calls=%fused_computation.392 | convolution fusion | flops 34340864 | bytes 859136 | tf_op jit(solution)/shard_map/dot_general | solution.py:25
  37.5 1.7 %fusion.216 = f32[512,128]{0,1:T(8,128)} fusion(bf16[768,256]{1,0:T(8,128)(2,1)S(1)} %copy-done.29, f32[256,512]{1,0:T(8,128)S(1)} %get-tuple-element.128, f32[256]{0:T(256)S(1)} %log_add_fusion.3, s32[512]{0:T(512)} %copy-done.43, s32[512]{0:T(512)S(1)} %copy-done.48, s32[256]{0:T(256)} %copy-done.63, s32[256]{0:T(256)S(1)} %copy-done.69), kind=kOutput, calls=%fused_computation.395 | convolution fusion | flops 34340864 | bytes 859136 | tf_op jit(solution)/shard_map/dot_general | solution.py:25
  39.3 1.0 select_maximum_fusion
  40.2 1.1 fusion.73
  41.6 1.2 fusion.263
  42.8 1.2 fusion.262
  44.0 1.2 fusion.261
  45.2 1.2 fusion.260
  46.4 1.2 fusion.259
  47.6 1.2 fusion.258
  48.8 1.2 fusion.257
  50.0 1.2 fusion.256
  57.1 1.3 constant_dynamic-update-slice_fusion.7
  58.4 1.2 constant_dynamic-update-slice_fusion.6
  59.7 1.2 constant_dynamic-update-slice_fusion.5
  60.9 1.2 constant_dynamic-update-slice_fusion.4
  62.1 1.2 constant_dynamic-update-slice_fusion.3
  63.3 1.2 constant_dynamic-update-slice_fusion.2
  64.5 1.2 constant_dynamic-update-slice_fusion.1
  65.7 1.2 constant_dynamic-update-slice_fusion
  71.5 0.9 fusion.19
  72.4 0.9 fusion.18
  73.3 0.9 fusion.17
  74.3 0.9 fusion.16
  76.1 0.9 fusion.14
  77.1 1.0 convolution_dynamic-update-slice_fusion.7
  78.1 1.0 convolution_dynamic-update-slice_fusion.6
  79.1 1.0 convolution_dynamic-update-slice_fusion.5
  80.0 1.0 convolution_dynamic-update-slice_fusion.4
  81.0 1.0 convolution_dynamic-update-slice_fusion.3
  82.0 1.0 convolution_dynamic-update-slice_fusion.2
  83.0 1.0 convolution_dynamic-update-slice_fusion.1
  84.0 1.0 convolution_dynamic-update-slice_fusion
  85.0 2.5 %multiply_reduce_fusion.5 = (f32[256]{0:T(256)}, bf16[256,128]{0,1:T(8,128)(2,1)}) fusion(bf16[256,128]{0,1:T(8,128)(2,1)} %copy.55, bf16[768,256]{1,0:T(8,128)(2,1)} %param.25, f32[256,256]{0,1:T(8,128)} %get-tuple-element.132, f32[256]{0:T(256)S(1)} %copy-done.60, s32[256]{0:T(256)} %copy-done.65, s32[256]{0:T(256)} %copy-done.71), kind=kOutput, calls=%fused_computation.224 | convolution fusion | flops 17334016 | bytes 464896 | tf_op jit(solution)/shard_map/dot_general | solution.py:41
  87.5 1.2 slice.420
  89.4 1.2 slice.421
  91.3 1.6 %copy.58 = bf16[256,128]{0,1:T(8,128)(2,1)} copy(bf16[256,128]{1,0:T(8,128)(2,1)} %get-tuple-element.108) | data formatting | bytes 131072
  95.4 1.2 fusion.40
  96.9 1.9 %multiply_reduce_fusion.4 = (f32[256]{0:T(256)S(1)}, bf16[256,128]{0,1:T(8,128)(2,1)}) fusion(bf16[256,128]{0,1:T(8,128)(2,1)} %copy.56, bf16[768,256]{1,0:T(8,128)(2,1)} %param.25, f32[256,256]{0,1:T(8,128)} %get-tuple-element.130, f32[256]{0:T(256)S(1)} %copy-done.57, s32[256]{0:T(256)} %copy-done.65, s32[256]{0:T(256)} %copy-done.71), kind=kOutput, calls=%fused_computation.223 | convolution fusion | flops 17334016 | bytes 464896 | tf_op jit(solution)/shard_map/dot_general | solution.py:41
  98.9 1.9 %fusion.41 = bf16[256,256]{0,1:T(8,128)(2,1)} fusion(f32[256,256]{0,1:T(8,128)} %get-tuple-element.130, f32[256]{0:T(256)S(1)} %get-tuple-element.141, f32[256]{0:T(256)} %copy-done.56, bf16[768,256]{1,0:T(8,128)(2,1)} %param.25, bf16[768,256]{1,0:T(8,128)(2,1)S(1)} %copy-done.30, s32[256]{0:T(256)} %copy-done.65, s32[256]{0:T(256)} %copy-done.71), kind=kOutput, calls=%fused_computation.105 | convolution fusion | flops 17301504 | bytes 530432 | tf_op jit(solution)/shard_map/dot_general | solution.py:19
  100.7 1.1 convolution_multiply_fusion.30
  102.0 2.0 %multiply_reduce_fusion.2 = (f32[256]{0:T(256)S(1)}, bf16[256,128]{0,1:T(8,128)(2,1)}) fusion(bf16[256,128]{0,1:T(8,128)(2,1)S(1)} %copy-done.40, bf16[768,256]{1,0:T(8,128)(2,1)} %param.25, f32[256,512]{1,0:T(8,128)S(1)} %copy-done.9, f32[256]{0:T(256)} %copy-done.58, s32[256]{0:T(256)} %copy-done.63, s32[512]{0:T(512)S(1)} %copy-done.44, ...), kind=kOutput, calls=%fused_computation.221 | convolution fusion | flops 34504448 | bytes 794624 | tf_op jit(solution)/shard_map/dot_general | solution.py:41
  104.0 1.2 fusion.10
  105.5 1.0 multiply_reduce_fusion.3
  108.1 1.1 convolution_multiply_fusion.21
  110.5 1.2 fusion.46
  111.6 1.2 fusion.47
  114.7 1.1 maximum_select_fusion
  116.0 1.0 copy.45
  117.0 1.8 %copy.49 = bf16[1,128,1024]{2,1,0:T(8,128)(2,1)} copy(bf16[1,128,1024]{1,2,0:T(8,128)(2,1)} %bitcast.108) | data formatting | bytes 524288
  121.7 7.1 %reduce-scatter.2.cloned.1.call-done = f32[128,2048]{0,1:T(8,128)} async-done(((f32[512,2048]{0,1:T(8,128)}), f32[128,2048]{0,1:T(8,128)}) %reduce-scatter.2.cloned.1.call-update) | async-done | bytes 1048592 | tf_op jit(solution)/shard_map/reduce_scatter | solution.py:201
  128.8 1.3 convert.71
  (291 shorter events, 32.5 us)
Async XLA Ops:
  7.2 16.8 %copy-start = (bf16[768,256]{1,0:T(8,128)(2,1)S(1)}, bf16[768,256]{1,0:T(8,128)(2,1)}, u32[]{:S(2)}) copy-start(bf16[768,256]{1,0:T(8,128)(2,1)} %param.24) | copy-start | bytes 1179652
  7.2 16.8 %copy-start.27 = (bf16[768,256]{1,0:T(8,128)(2,1)S(1)}, bf16[768,256]{1,0:T(8,128)(2,1)}, u32[]{:S(2)}) copy-start(bf16[768,256]{1,0:T(8,128)(2,1)} %param.23) | copy-start | bytes 1179652
  7.2 10.0 %copy-start.83 = (bf16[768,256]{1,0:T(8,128)(2,1)S(1)}, bf16[768,256]{1,0:T(8,128)(2,1)}, u32[]{:S(2)}) copy-start(bf16[768,256]{1,0:T(8,128)(2,1)} %param.25) | copy-start | bytes 1179652
  7.2 34.3 %all-gather.5.cloned.1.call-start = ((), (), s32[]{:S(2)}) async-start(), calls=%async_computation.2 | async-start | bytes 1310720 | tf_op jit(solution)/shard_map/all_gather | solution.py:175
  7.9 49.2 %all-gather.7.cloned.1.call-start = ((), (), s32[]{:S(2)}) async-start(), calls=%async_computation.3 | async-start | bytes 1310720 | tf_op jit(solution)/shard_map/all_gather | solution.py:176
  10.2 16.0 %copy-start.68 = (s32[256]{0:T(256)}, s32[256]{0:T(256)S(1)}, u32[]{:S(2)}) copy-start(s32[256]{0:T(256)S(1)} %get-tuple-element.114) | copy-start | bytes 3076
  10.2 16.7 %copy-start.66 = (s32[256]{0:T(256)}, s32[256]{0:T(256)S(1)}, u32[]{:S(2)}) copy-start(s32[256]{0:T(256)S(1)} %get-tuple-element.113) | copy-start | bytes 3076
  10.2 22.3 %copy-start.71 = (s32[256]{0:T(256)}, s32[256]{0:T(256)S(1)}, u32[]{:S(2)}) copy-start(s32[256]{0:T(256)S(1)} %get-tuple-element.112) | copy-start | bytes 3076
  10.2 15.9 %copy-start.47 = (s32[512]{0:T(512)}, s32[512]{0:T(512)S(1)}, u32[]{:S(2)}) copy-start(s32[512]{0:T(512)S(1)} %get-tuple-element.115) | copy-start | bytes 6148
  10.3 16.7 %copy-start.45 = (s32[512]{0:T(512)}, s32[512]{0:T(512)S(1)}, u32[]{:S(2)}) copy-start(s32[512]{0:T(512)S(1)} %get-tuple-element.116) | copy-start | bytes 6148
  10.3 16.6 %copy-start.61 = (s32[256]{0:T(256)}, s32[256]{0:T(256)S(1)}, u32[]{:S(2)}) copy-start(s32[256]{0:T(256)S(1)} %slice.413) | copy-start | bytes 3076
  10.3 16.6 %copy-start.41 = (s32[512]{0:T(512)}, s32[512]{0:T(512)S(1)}, u32[]{:S(2)}) copy-start(s32[512]{0:T(512)S(1)} %slice.412) | copy-start | bytes 6148
  15.2 11.4 %copy-start.2 = (f32[256,512]{1,0:T(8,128)}, f32[256,512]{1,0:T(8,128)S(1)}, u32[]{:S(2)}) copy-start(f32[256,512]{1,0:T(8,128)S(1)} %get-tuple-element.122) | copy-start | bytes 1572868
  15.4 11.2 %copy-start.29 = (bf16[768,256]{1,0:T(8,128)(2,1)S(1)}, bf16[768,256]{1,0:T(8,128)(2,1)}, u32[]{:S(2)}) copy-start(bf16[768,256]{1,0:T(8,128)(2,1)} %param.26) | copy-start | bytes 1179652
  16.9 11.1 %copy-start.4 = (f32[256,512]{1,0:T(8,128)}, f32[256,512]{1,0:T(8,128)S(1)}, u32[]{:S(2)}) copy-start(f32[256,512]{1,0:T(8,128)S(1)} %get-tuple-element.124) | copy-start | bytes 1572868
  17.2 10.8 %copy-start.72 = (s32[8]{0:T(128)S(1)}, s32[8]{0:T(128)}, u32[]{:S(2)}) copy-start(s32[8]{0:T(128)} %param.33) | copy-start | bytes 100
  17.2 10.9 %copy-start.52 = (f32[256]{0:T(256)}, f32[256]{0:T(256)S(1)}, u32[]{:S(2)}) copy-start(f32[256]{0:T(256)S(1)} %log_add_fusion) | copy-start | bytes 3076
  17.2 10.9 %copy-start.50 = (f32[256]{0:T(256)}, f32[256]{0:T(256)S(1)}, u32[]{:S(2)}) copy-start(f32[256]{0:T(256)S(1)} %log_add_fusion.1) | copy-start | bytes 3076
  19.8 96.1 %collective-permute-start = (bf16[128,256]{0,1:T(8,128)(2,1)}, bf16[128,256]{0,1:T(8,128)(2,1)}, u32[]{:S(2)}, u32[]{:S(2)}) collective-permute-start(bf16[128,256]{0,1:T(8,128)(2,1)} %fusion.139), channel_id=1, source_target_pairs={{0,16},{4,20},{8,24},{12,28},{16,0},{20,4},{24,8},{28,12},{1,17},{... | collective-permute-start | bytes 196616 | tf_op jit(solution)/shard_map/ppermute | solution.py:15
  23.9 104.9 %reduce-scatter.2.cloned.1.call-start = ((), (), s32[]{:S(2)}) async-start(), calls=%async_computation.1 | async-start | bytes 5242880 | tf_op jit(solution)/shard_map/reduce_scatter | solution.py:201
  23.9 10.5 %copy-start.63 = (s32[256]{0:T(256)}, s32[256]{0:T(256)S(1)}, u32[]{:S(2)}) copy-start(s32[256]{0:T(256)S(1)} %slice.403) | copy-start | bytes 3076
  24.0 10.5 %copy-start.43 = (s32[512]{0:T(512)}, s32[512]{0:T(512)S(1)}, u32[]{:S(2)}) copy-start(s32[512]{0:T(512)S(1)} %slice.402) | copy-start | bytes 6148
  24.0 10.5 %copy-start.65 = (s32[256]{0:T(256)}, s32[256]{0:T(256)S(1)}, u32[]{:S(2)}) copy-start(s32[256]{0:T(256)S(1)} %slice.393) | copy-start | bytes 3076
  26.2 13.0 %copy-start.8 = (f32[256,512]{1,0:T(8,128)}, f32[256,512]{1,0:T(8,128)S(1)}, u32[]{:S(2)}) copy-start(f32[256,512]{1,0:T(8,128)S(1)} %get-tuple-element.126) | copy-start | bytes 1572868
  26.6 13.7 %copy-start.6 = (f32[256,512]{1,0:T(8,128)}, f32[256,512]{1,0:T(8,128)S(1)}, u32[]{:S(2)}) copy-start(f32[256,512]{1,0:T(8,128)S(1)} %get-tuple-element.128) | copy-start | bytes 1572868
  26.9 10.5 %copy-start.48 = (s32[512]{0:T(512)S(1)}, s32[512]{0:T(512)}, u32[]{:S(2)}) copy-start(s32[512]{0:T(512)} %copy-done.47) | copy-start | bytes 6148
  27.0 10.5 %copy-start.69 = (s32[256]{0:T(256)S(1)}, s32[256]{0:T(256)}, u32[]{:S(2)}) copy-start(s32[256]{0:T(256)} %copy-done.68) | copy-start | bytes 3076
  37.5 12.5 %copy-start.54 = (f32[256]{0:T(256)}, f32[256]{0:T(256)S(1)}, u32[]{:S(2)}) copy-start(f32[256]{0:T(256)S(1)} %log_add_fusion.3) | copy-start | bytes 3076
  57.1 10.6 %copy-start.73 = (f32[128]{0:T(128)S(1)}, f32[128]{0:T(128)}, u32[]{:S(2)}) copy-start(f32[128]{0:T(128)} %log_add_fusion.6) | copy-start | bytes 1540
  57.1 10.6 %copy-start.82 = (bf16[1,512,1024]{2,1,0:T(8,128)(2,1)S(1)}, bf16[1,512,1024]{2,1,0:T(8,128)(2,1)}, u32[]{:S(2)}) copy-start(bf16[1,512,1024]{2,1,0:T(8,128)(2,1)} %all-gather.7.cloned.1.call-done) | copy-start | bytes 3145732
  57.1 10.8 %copy-start.81 = (f32[128]{0:T(128)S(1)}, f32[128]{0:T(128)}, u32[]{:S(2)}) copy-start(f32[128]{0:T(128)} %log_add_fusion.13) | copy-start | bytes 1540
  57.1 11.0 %copy-start.80 = (f32[128]{0:T(128)S(1)}, f32[128]{0:T(128)}, u32[]{:S(2)}) copy-start(f32[128]{0:T(128)} %log_add_fusion.12) | copy-start | bytes 1540
  57.1 11.3 %copy-start.79 = (f32[128]{0:T(128)S(1)}, f32[128]{0:T(128)}, u32[]{:S(2)}) copy-start(f32[128]{0:T(128)} %log_add_fusion.11) | copy-start | bytes 1540
  57.1 11.5 %copy-start.78 = (f32[128]{0:T(128)S(1)}, f32[128]{0:T(128)}, u32[]{:S(2)}) copy-start(f32[128]{0:T(128)} %log_add_fusion.10) | copy-start | bytes 1540
  57.1 11.7 %copy-start.77 = (f32[128]{0:T(128)S(1)}, f32[128]{0:T(128)}, u32[]{:S(2)}) copy-start(f32[128]{0:T(128)} %log_add_fusion.9) | copy-start | bytes 1540
  58.4 10.7 %copy-start.76 = (f32[128]{0:T(128)S(1)}, f32[128]{0:T(128)}, u32[]{:S(2)}) copy-start(f32[128]{0:T(128)} %log_add_fusion.8) | copy-start | bytes 1540
  59.7 9.7 %copy-start.75 = (f32[128]{0:T(128)S(1)}, f32[128]{0:T(128)}, u32[]{:S(2)}) copy-start(f32[128]{0:T(128)} %log_add_fusion.7) | copy-start | bytes 1540
  67.9 10.2 %copy-start.10 = (bf16[128,512]{1,0:T(8,128)(2,1)}, bf16[128,512]{1,0:T(8,128)(2,1)S(1)}, u32[]{:S(2)}) copy-start(bf16[128,512]{1,0:T(8,128)(2,1)S(1)} %fusion.39) | copy-start | bytes 393220
  68.1 10.9 %copy-start.22 = (bf16[128,512]{1,0:T(8,128)(2,1)}, bf16[128,512]{1,0:T(8,128)(2,1)S(1)}, u32[]{:S(2)}) copy-start(bf16[128,512]{1,0:T(8,128)(2,1)S(1)} %fusion.32) | copy-start | bytes 393220
  68.4 11.7 %copy-start.24 = (bf16[128,512]{1,0:T(8,128)(2,1)}, bf16[128,512]{1,0:T(8,128)(2,1)S(1)}, u32[]{:S(2)}) copy-start(bf16[128,512]{1,0:T(8,128)(2,1)S(1)} %fusion.33) | copy-start | bytes 393220
  68.6 13.4 %copy-start.20 = (bf16[128,512]{1,0:T(8,128)(2,1)}, bf16[128,512]{1,0:T(8,128)(2,1)S(1)}, u32[]{:S(2)}) copy-start(bf16[128,512]{1,0:T(8,128)(2,1)S(1)} %fusion.34) | copy-start | bytes 393220
  68.9 14.1 %copy-start.18 = (bf16[128,512]{1,0:T(8,128)(2,1)}, bf16[128,512]{1,0:T(8,128)(2,1)S(1)}, u32[]{:S(2)}) copy-start(bf16[128,512]{1,0:T(8,128)(2,1)S(1)} %fusion.35) | copy-start | bytes 393220
  69.1 14.9 %copy-start.16 = (bf16[128,512]{1,0:T(8,128)(2,1)}, bf16[128,512]{1,0:T(8,128)(2,1)S(1)}, u32[]{:S(2)}) copy-start(bf16[128,512]{1,0:T(8,128)(2,1)S(1)} %fusion.36) | copy-start | bytes 393220
  69.1 14.8 %copy-start.74 = (f32[128]{0:T(128)S(1)}, f32[128]{0:T(128)}, u32[]{:S(2)}) copy-start(f32[128]{0:T(128)} %log_add_fusion.6) | copy-start | bytes 1540
  69.4 14.6 %copy-start.12 = (bf16[128,512]{1,0:T(8,128)(2,1)}, bf16[128,512]{1,0:T(8,128)(2,1)S(1)}, u32[]{:S(2)}) copy-start(bf16[128,512]{1,0:T(8,128)(2,1)S(1)} %fusion.37) | copy-start | bytes 393220
  69.6 14.3 %copy-start.14 = (bf16[128,512]{1,0:T(8,128)(2,1)}, bf16[128,512]{1,0:T(8,128)(2,1)S(1)}, u32[]{:S(2)}) copy-start(bf16[128,512]{1,0:T(8,128)(2,1)S(1)} %fusion.38) | copy-start | bytes 393220
  79.0 13.8 %copy-start.35 = (bf16[256,128]{1,0:T(8,128)(2,1)S(1)}, bf16[256,128]{1,0:T(8,128)(2,1)}, u32[]{:S(2)}) copy-start(bf16[256,128]{1,0:T(8,128)(2,1)} %get-tuple-element.109) | copy-start | bytes 196612
  79.0 14.6 %copy-start.34 = (bf16[256,128]{1,0:T(8,128)(2,1)S(1)}, bf16[256,128]{1,0:T(8,128)(2,1)}, u32[]{:S(2)}) copy-start(bf16[256,128]{1,0:T(8,128)(2,1)} %get-tuple-element.110) | copy-start | bytes 196612
  83.0 12.4 %copy-start.30 = (bf16[768,256]{1,0:T(8,128)(2,1)S(1)}, bf16[768,256]{1,0:T(8,128)(2,1)}, u32[]{:S(2)}) copy-start(bf16[768,256]{1,0:T(8,128)(2,1)} %param.26) | copy-start | bytes 1179652
  84.0 12.7 %copy-start.28 = (bf16[768,256]{1,0:T(8,128)(2,1)S(1)}, bf16[768,256]{1,0:T(8,128)(2,1)}, u32[]{:S(2)}) copy-start(bf16[768,256]{1,0:T(8,128)(2,1)} %param.23) | copy-start | bytes 1179652
  85.0 11.9 %copy-start.57 = (f32[256]{0:T(256)S(1)}, f32[256]{0:T(256)}, u32[]{:S(2)}) copy-start(f32[256]{0:T(256)} %copy-done.56) | copy-start | bytes 3076
  85.0 16.9 %copy-start.9 = (f32[256,512]{1,0:T(8,128)S(1)}, f32[256,512]{1,0:T(8,128)}, u32[]{:S(2)}) copy-start(f32[256,512]{1,0:T(8,128)} %copy-done.8) | copy-start | bytes 1572868
  85.0 16.9 %copy-start.44 = (s32[512]{0:T(512)S(1)}, s32[512]{0:T(512)}, u32[]{:S(2)}) copy-start(s32[512]{0:T(512)} %copy-done.43) | copy-start | bytes 6148
  94.4 11.0 %copy-start.7 = (f32[256,512]{1,0:T(8,128)S(1)}, f32[256,512]{1,0:T(8,128)}, u32[]{:S(2)}) copy-start(f32[256,512]{1,0:T(8,128)} %copy-done.6) | copy-start | bytes 1572868
  94.4 11.0 %copy-start.39 = (bf16[256,128]{0,1:T(8,128)(2,1)S(1)}, bf16[256,128]{0,1:T(8,128)(2,1)}, u32[]{:S(2)}) copy-start(bf16[256,128]{0,1:T(8,128)(2,1)} %copy.57) | copy-start | bytes 196612
  94.4 11.0 %copy-start.49 = (s32[512]{0:T(512)S(1)}, s32[512]{0:T(512)}, u32[]{:S(2)}) copy-start(s32[512]{0:T(512)} %copy-done.47) | copy-start | bytes 6148
  94.4 11.0 %copy-start.55 = (f32[256]{0:T(256)S(1)}, f32[256]{0:T(256)}, u32[]{:S(2)}) copy-start(f32[256]{0:T(256)} %copy-done.54) | copy-start | bytes 3076
  94.5 11.0 %copy-start.64 = (s32[256]{0:T(256)S(1)}, s32[256]{0:T(256)}, u32[]{:S(2)}) copy-start(s32[256]{0:T(256)} %copy-done.63) | copy-start | bytes 3076
  94.5 11.0 %copy-start.70 = (s32[256]{0:T(256)S(1)}, s32[256]{0:T(256)}, u32[]{:S(2)}) copy-start(s32[256]{0:T(256)} %copy-done.68) | copy-start | bytes 3076
  94.5 11.0 %copy-start.84 = (bf16[768,256]{1,0:T(8,128)(2,1)S(1)}, bf16[768,256]{1,0:T(8,128)(2,1)}, u32[]{:S(2)}) copy-start(bf16[768,256]{1,0:T(8,128)(2,1)} %param.25) | copy-start | bytes 1179652
  95.4 11.1 %copy-start.31 = (bf16[768,256]{1,0:T(8,128)(2,1)S(1)}, bf16[768,256]{1,0:T(8,128)(2,1)}, u32[]{:S(2)}) copy-start(bf16[768,256]{1,0:T(8,128)(2,1)} %param.26) | copy-start | bytes 1179652
  109.5 9.5 %copy-start.25 = (bf16[128,512]{1,0:T(8,128)(2,1)S(1)}, bf16[128,512]{1,0:T(8,128)(2,1)}, u32[]{:S(2)}) copy-start(bf16[128,512]{1,0:T(8,128)(2,1)} %copy-done.24) | copy-start | bytes 393220
  109.5 9.7 %copy-start.21 = (bf16[128,512]{1,0:T(8,128)(2,1)S(1)}, bf16[128,512]{1,0:T(8,128)(2,1)}, u32[]{:S(2)}) copy-start(bf16[128,512]{1,0:T(8,128)(2,1)} %copy-done.20) | copy-start | bytes 393220
  110.5 9.3 %copy-start.17 = (bf16[128,512]{1,0:T(8,128)(2,1)S(1)}, bf16[128,512]{1,0:T(8,128)(2,1)}, u32[]{:S(2)}) copy-start(bf16[128,512]{1,0:T(8,128)(2,1)} %copy-done.16) | copy-start | bytes 393220
  (27 other events, 185.5 us)
Sparse Core Ops, SparseCore 0:
  9.6 19.4 all-gather.4
  30.6 16.6 all-gather.6
  85.1 43.6 reduce-scatter.1
where the time goes:
time: 140 us; the launch traced here: 138 us
  matrix products  72.3 us (52%)
  local copies, waits for them, and re-layouts  21 us (15%)
  between operations  17.9 us (13%)
  other arithmetic  15.1 us (11%)
  waiting for transfers between devices  7.87 us (6%)
  starting transfers between devices  4.18 us (3%)
    dot_general x28, matrix products, dot_cols(): lax.dot_general(left, right, (((0,), (0,)), ((), ())), preferred_element_...  26.5 us
    dot_general x28, matrix products, dot_rows(): lax.dot_general(left, right, (((1,), (1,)), ((), ())), preferred_element_...  21.5 us
    dot_general x14, matrix products, attend_head(): jnp.dot(weights, values, preferred_element_type=jnp.float32)  19.1 us
    unnamed x190, local copies, waits for them, and re-layouts  15.9 us
    reduce_scatter x1, waiting for transfers between devices, shards(): lax.psum_scatter(jnp.concatenate(key_parts + value_parts, axis=1), 'ctx',...  7.13 us
    dot_general x14, matrix products, attend_head(): jnp.dot(score_grads, keys, preferred_element_type=jnp.float32) * scale  5.19 us
    reduce_sum x14, other arithmetic, attend_head(): lse = top + jnp.log(jnp.sum(jnp.exp(scores - top), axis=1, keepdims=True))  4.48 us
    add x14, other arithmetic, attend_head(): lse = top + jnp.log(jnp.sum(jnp.exp(scores - top), axis=1, keepdims=True))  4.4 us
  transfers between devices with their start and end apart: 4, of which 1 were waited for; matrix products, arithmetic and copies ran while one was open for 75% of the time, Pallas kernels for 0%

commit v1 on v0

v1 whole, which is shorter than its diff:
```python
import functools

import jax
import jax.numpy as jnp
from jax import lax
from jax.experimental import pallas as pl
from jax.experimental.pallas import tpu as pltpu
from jax.sharding import PartitionSpec as P


HEAD_DIM = 128
NEG = -1e30
LOG2E = 1.4426950408889634


def dot_rows(left, right):
    return lax.dot_general(
        left, right, (((1,), (1,)), ((), ())), preferred_element_type=jnp.float32
    )


def dot(left, right):
    return jnp.dot(left, right, preferred_element_type=jnp.float32)


def score_stage(queries, douts, keys, values):
    return dot_rows(keys, queries), dot_rows(values, douts)


def softmax_stage(scores, dprobs, tile, columns, mask_tile, scale):
    key_tiles = scores.shape[0] // tile
    weight_cols = []
    grad_cols = []
    for b, (first, last) in enumerate(columns):
        lanes = slice(b * tile, (b + 1) * tile)
        s_tiles = []
        top = None
        for j in range(first, last):
            s = mask_tile(scores[j * tile : (j + 1) * tile, lanes], j, b)
            s_tiles.append(s)
            part = jnp.max(s, axis=0, keepdims=True)
            top = part if top is None else jnp.maximum(top, part)
        e_tiles = [jnp.exp2((s - top) * (scale * LOG2E)) for s in s_tiles]
        total = sum(jnp.sum(e, axis=0, keepdims=True) for e in e_tiles)
        inverse = 1.0 / total
        p_tiles = [e * inverse for e in e_tiles]
        d_tiles = [dprobs[j * tile : (j + 1) * tile, lanes] for j in range(first, last)]
        delta = sum(jnp.sum(p * d, axis=0, keepdims=True) for p, d in zip(p_tiles, d_tiles))
        w_tiles = [p.astype(jnp.bfloat16) for p in p_tiles]
        g_tiles = [(p * (d - delta)).astype(jnp.bfloat16) for p, d in zip(p_tiles, d_tiles)]
        zero = jnp.zeros((tile, tile), jnp.bfloat16)
        before = [zero] * first
        after = [zero] * (key_tiles - last)
        weight_cols.append(jnp.concatenate(before + w_tiles + after, axis=0))
        grad_cols.append(jnp.concatenate(before + g_tiles + after, axis=0))
    return jnp.concatenate(weight_cols, axis=1), jnp.concatenate(grad_cols, axis=1)


def product_stage(weights, grads, queries, douts, keys_t, values_t, scale):
    attended = dot(values_t, weights).astype(jnp.bfloat16).T
    grad_q = (dot(keys_t, grads) * scale).astype(jnp.bfloat16).T
    return attended, grad_q, dot(grads, queries), dot(weights, douts)


def staged(blocks, scores_of, softmax_of, products_of, ahead=1):
    scores = {}
    for step in range(blocks + ahead):
        if step < blocks:
            scores[step] = scores_of(step)
        if step >= ahead:
            block = step - ahead
            products_of(block, *softmax_of(block, *scores.pop(block)))


def causal(s, tile):
    key = lax.broadcasted_iota(jnp.int32, (tile, tile), 0)
    query = lax.broadcasted_iota(jnp.int32, (tile, tile), 1)
    return jnp.where(key <= query, s, NEG)


def short_kernel(head, heads, lengths, dests, q_hbm, k_hbm, v_hbm, d_hbm, *rest):
    if head > 0:
        rest = rest[5:]
    else:
        order, rest = rest[0], rest[1:]
    out_hbm, dq_hbm, dk_hbm, dv_hbm = rest[:4]
    rest = rest[4:]
    if head == 0:
        (tail_ref, table_ref), rest = rest[:2], rest[2:]
        for index in range(order.shape[0]):
            table_ref[index : index + 1, :] = jnp.full((1, table_ref.shape[1]), order[index], jnp.int32)
    held, made, in_sem, out_sem = rest[:4]
    scale = HEAD_DIM ** (-0.5)
    tokens = q_hbm.shape[0]
    tile = tokens // 6
    span = 2 * tile
    rank = lax.axis_index("dp")
    count = lengths.shape[1]
    column = pl.ds(head * HEAD_DIM, HEAD_DIM)

    loads = [
        pltpu.make_async_copy(ref.at[:, column], held.at[slot], in_sem.at[slot])
        for slot, ref in enumerate((q_hbm, k_hbm, v_hbm, d_hbm))
    ]
    for load in loads:
        load.start()
    others = []
    if head == 0:
        ends, end_sem = rest[4:]
        for other in range(1, heads):
            columns = pl.ds(other * HEAD_DIM, HEAD_DIM)
            for slot, ref in enumerate((q_hbm, k_hbm, v_hbm)):
                others.append(
                    pltpu.make_async_copy(
                        ref.at[pl.ds(tokens - 3 * tile, 3 * tile), columns],
                        ends.at[other - 1, slot],
                        end_sem.at[len(others)],
                    )
                )
        for load in others:
            load.start()

    place = lax.broadcasted_iota(jnp.int32, (1, tokens), 1)
    start = jnp.zeros((1, tokens), jnp.int32)
    begin = jnp.int32(0)
    for j in range(count - 1):
        begin = begin + lengths[rank, j]
        start = jnp.where(place >= begin, begin, start)
    tail = lengths[rank, count - 1]
    moves = dests[rank, count - 1] != rank
    stores = []

    def store(slot, low, high, target):
        copy = pltpu.make_async_copy(
            made.at[slot, pl.ds(low, high - low), :],
            target.at[pl.ds(low, high - low), column],
            out_sem.at[len(stores)],
        )
        copy.start()
        stores.append(copy)

    for load in loads:
        load.wait()
    q_ref, k_ref, v_ref, d_ref = [held.at[slot] for slot in range(4)]
    keys_t = k_ref[...].T
    values_t = v_ref[...].T
    blocks = tokens // span
    pending = {}

    def key_low(block):
        return max(0, (block - 1) * span)

    def sent(last):
        to = lax.broadcasted_iota(jnp.int32, (tile, tile), 0)
        come = lax.broadcasted_iota(jnp.int32, (tile, tile), 1)
        pick = (come == to + (tile - tail)) & moves & (to < tail)
        return dot(pick.astype(jnp.float32).astype(jnp.bfloat16), last).astype(jnp.bfloat16)

    def scores_of(block):
        low = block * span
        keys = slice(key_low(block), low + span)
        return score_stage(q_ref[low : low + span, :], d_ref[low : low + span, :], k_ref[keys, :], v_ref[keys, :])

    def softmax_of(block, scores, dprobs):
        low = block * span
        offset = (low - key_low(block)) // tile

        def mask_tile(s, j, b):
            key = lax.broadcasted_iota(jnp.int32, (tile, tile), 0)
            first = start[:, low + b * tile : low + (b + 1) * tile] - (key_low(block) + j * tile)
            allowed = key >= first
            if j == offset + b:
                query = lax.broadcasted_iota(jnp.int32, (tile, tile), 1)
                allowed = allowed & (key <= query)
            return jnp.where(allowed, s, NEG)

        columns = [(max(0, offset + b - 2), offset + b + 1) for b in range(2)]
        return softmax_stage(scores, dprobs, tile, columns, mask_tile, scale)

    def products_of(block, weights, grads):
        low = block * span
        high = low + span
        keys = slice(key_low(block), high)
        attended, grad_q, grad_k, grad_v = product_stage(
            weights,
            grads,
            q_ref[low:high, :],
            d_ref[low:high, :],
            keys_t[:, keys],
            values_t[:, keys],
            scale,
        )
        made[1, low:high, :] = grad_q
        store(1, low, high, dq_hbm)
        if high == tokens:
            last = attended[tile:, :]
            row = lax.broadcasted_iota(jnp.int32, (tile, 1), 0)
            kept = jnp.logical_not(moves & (row >= tile - tail))
            made[0, low : low + tile, :] = attended[:tile, :]
            made[0, low + tile : tokens, :] = jnp.where(kept, last, jnp.zeros_like(last))
            if head == 0:
                tail_ref[0] = sent(last)
        else:
            made[0, low:high, :] = attended
        store(0, low, high, out_hbm)
        if block > 0:
            done_k = pending["k"] + grad_k[:span]
            done_v = pending["v"] + grad_v[:span]
            made[2, low - span : low, :] = (done_k * scale).astype(jnp.bfloat16)
            made[3, low - span : low, :] = done_v.astype(jnp.bfloat16)
            store(2, low - span, low, dk_hbm)
            store(3, low - span, low, dv_hbm)
        pending["k"] = grad_k[-span:]
        pending["v"] = grad_v[-span:]
        if high == tokens:
            made[2, low:high, :] = (pending["k"] * scale).astype(jnp.bfloat16)
            made[3, low:high, :] = pending["v"].astype(jnp.bfloat16)
            store(2, low, high, dk_hbm)
            store(3, low, high, dv_hbm)

    staged(blocks, scores_of, softmax_of, products_of)
    for load in others:
        load.wait()
    if head == 0:
        for other in range(1, heads):
            scores = dot_rows(ends[other - 1, 1], ends[other - 1, 0, 2 * tile :, :])
            key = lax.broadcasted_iota(jnp.int32, scores.shape, 0)
            query = lax.broadcasted_iota(jnp.int32, scores.shape, 1) + 2 * tile
            first = start[:, tokens - tile :] - (tokens - 3 * tile)
            scores = jnp.where((key >= first) & (key <= query), scores, NEG)
            grown = jnp.exp2((scores - jnp.max(scores, axis=0, keepdims=True)) * (scale * LOG2E))
            weights = (grown * (1.0 / jnp.sum(grown, axis=0, keepdims=True))).astype(jnp.bfloat16)
            tail_ref[other] = sent(dot(weights.T, ends[other - 1, 2]).astype(jnp.bfloat16))
    for copy in stores:
        copy.wait()


def short_attention(head, heads, lengths, dests, arrays, before, after, order=None):
    tokens, width = arrays[0].shape
    move = tokens // 6
    blocks = 3
    smem = pl.BlockSpec(memory_space=pltpu.SMEM)
    hbm = pl.BlockSpec(memory_space=pltpu.HBM)
    vmem = pl.BlockSpec(memory_space=pltpu.VMEM)
    wide = jax.ShapeDtypeStruct((tokens, width), jnp.bfloat16)
    first = before is None
    extra = [order] if first else list(before[:4]) + [after]
    tile = move
    return pl.pallas_call(
        functools.partial(short_kernel, head, heads),
        in_specs=[smem] * 2 + [hbm] * 4 + ([smem] if first else [hbm] * 4 + [pl.BlockSpec(memory_space=pl.ANY)]),
        out_specs=[hbm] * 4 + ([vmem] * 2 if first else []),
        out_shape=[jax.ShapeDtypeStruct((tokens + move, width), jnp.bfloat16), wide, wide, wide]
        + (
            [
                jax.ShapeDtypeStruct((heads, move, HEAD_DIM), jnp.bfloat16),
                jax.ShapeDtypeStruct((order.shape[0], HEAD_DIM), jnp.int32),
            ]
            if first
            else []
        ),
        scratch_shapes=[
            pltpu.VMEM((4, tokens, HEAD_DIM), jnp.bfloat16),
            pltpu.VMEM((4, tokens, HEAD_DIM), jnp.bfloat16),
            pltpu.SemaphoreType.DMA((4,)),
            pltpu.SemaphoreType.DMA((4 * blocks,)),
        ]
        + (
            [
                pltpu.VMEM((max(heads - 1, 1), 3, 3 * tile, HEAD_DIM), jnp.bfloat16),
                pltpu.SemaphoreType.DMA((max(3 * heads - 3, 1),)),
            ]
            if first
            else []
        ),
        input_output_aliases={} if first else {6 + i: i for i in range(4)},
        compiler_params=pltpu.CompilerParams(vmem_limit_bytes=16 << 20),
        cost_estimate=pl.CostEstimate(flops=10**9, bytes_accessed=3 * 10**6, transcendentals=0),
    )(lengths, dests, *arrays, *extra)


def peer_order(ways):
    return [step for step in range(2, ways)] + [1]


def pack_kernel(head, ways, q_ref, k_ref, v_ref, d_ref, *rest):
    steps = peer_order(ways) + [0]
    outs, sem = rest[: len(steps)], rest[-1]
    own = lax.axis_index("ctx")
    per = q_ref.shape[2] // ways
    copies = []
    for out, step in zip(outs, steps):
        column = pl.multiple_of((own ^ step) * per + head * HEAD_DIM, HEAD_DIM)
        for slot, ref in enumerate((q_ref, k_ref, v_ref, d_ref)):
            copies.append(
                pltpu.make_async_copy(
                    ref.at[0, :, pl.ds(column, HEAD_DIM)], out.at[slot], sem.at[len(copies)]
                )
            )
    for copy in copies:
        copy.start()
    for copy in copies:
        copy.wait()


def pack(head, ways, arrays):
    rows = arrays[0].shape[1]
    return pl.pallas_call(
        functools.partial(pack_kernel, head, ways),
        in_specs=[pl.BlockSpec(memory_space=pltpu.HBM)] * 4,
        out_specs=[pl.BlockSpec(memory_space=pltpu.VMEM)] * ways,
        out_shape=[jax.ShapeDtypeStruct((4, rows, HEAD_DIM), jnp.bfloat16)] * ways,
        scratch_shapes=[pltpu.SemaphoreType.DMA((4 * ways,))],
        compiler_params=pltpu.CompilerParams(vmem_limit_bytes=8 << 20),
        cost_estimate=pl.CostEstimate(flops=0, bytes_accessed=2 * 10**6, transcendentals=0),
    )(*[pltpu.with_memory_space_constraint(array, pltpu.HBM) for array in arrays])


def long_kernel(ways, linked, order, *rest):
    rest = rest[linked:]
    steps = peer_order(ways) + [0]
    arrived = rest[:ways]
    outs = rest[ways : 2 * ways]
    held, made = rest[2 * ways + linked :]
    scale = HEAD_DIM ** (-0.5)
    own = lax.axis_index("ctx")
    rows = arrived[0].shape[1]
    half = rows // 2
    total = rows * ways

    def spot(device, part):
        return pl.ds(pl.multiple_of(order[device * 2 + part, 0] * half, half), half)

    for buffer, step in zip(arrived, steps):
        for part in range(2):
            piece = slice(part * half, (part + 1) * half)
            for slot in range(4):
                held[slot, spot(own ^ step, part), :] = buffer[slot, piece, :]

    tile = HEAD_DIM
    span = 2 * tile
    blocks = total // span
    keys_t = held[1].T
    values_t = held[2].T
    sum_k = [None] * blocks
    sum_v = [None] * blocks

    def scores_of(block):
        low, high = block * span, (block + 1) * span
        return score_stage(held[0, low:high, :], held[3, low:high, :], held[1, :high, :], held[2, :high, :])

    def softmax_of(block, scores, dprobs):
        first = block * span // tile

        def mask_tile(s, j, b):
            return causal(s, tile) if j == first + b else s

        columns = [(0, first + b + 1) for b in range(span // tile)]
        return softmax_stage(scores, dprobs, tile, columns, mask_tile, scale)

    def products_of(block, weights, grads):
        low, high = block * span, (block + 1) * span
        attended, grad_q, grad_k, grad_v = product_stage(
            weights, grads, held[0, low:high, :], held[3, low:high, :], keys_t[:, :high], values_t[:, :high], scale
        )
        made[0, low:high, :] = attended
        made[1, low:high, :] = grad_q
        for part in range(block + 1):
            piece = slice(part * span, (part + 1) * span)
            sum_k[part] = grad_k[piece] if sum_k[part] is None else sum_k[part] + grad_k[piece]
            sum_v[part] = grad_v[piece] if sum_v[part] is None else sum_v[part] + grad_v[piece]

    staged(blocks, scores_of, softmax_of, products_of)
    for part in range(blocks):
        piece = slice(part * span, (part + 1) * span)
        made[2, piece, :] = (sum_k[part] * scale).astype(jnp.bfloat16)
        made[3, piece, :] = sum_v[part].astype(jnp.bfloat16)

    for out, step in zip(outs, steps):
        for part in range(2):
            piece = slice(part * half, (part + 1) * half)
            for slot in range(4):
                out[slot, piece, :] = made[slot, spot(own ^ step, part), :]


def long_attention(ways, order, arrived, linked=()):
    anywhere = [pl.BlockSpec(memory_space=pl.ANY)] * len(linked)
    rows = arrived[0].shape[1]
    piece = jax.ShapeDtypeStruct((4, rows, HEAD_DIM), jnp.bfloat16)
    vmem = pl.BlockSpec(memory_space=pltpu.VMEM)
    return pl.pallas_call(
        functools.partial(long_kernel, ways, len(linked)),
        in_specs=[vmem] + anywhere + [vmem] * ways,
        out_specs=[vmem] * ways + anywhere,
        out_shape=[piece] * ways + [jax.ShapeDtypeStruct(x.shape, x.dtype) for x in linked],
        scratch_shapes=[
            pltpu.VMEM((4, rows * ways, HEAD_DIM), jnp.bfloat16),
            pltpu.VMEM((4, rows * ways, HEAD_DIM), jnp.bfloat16),
        ],
        input_output_aliases={1 + i: ways + i for i in range(len(linked))},
        compiler_params=pltpu.CompilerParams(vmem_limit_bytes=16 << 20),
        cost_estimate=pl.CostEstimate(flops=10**9, bytes_accessed=3 * 10**6, transcendentals=0),
    )(order, *linked, *arrived)


def join_kernel(ways, head, last, *refs):
    steps = peer_order(ways) + [0]
    pieces = refs[:ways]
    refs = refs[ways:]
    if last:
        received, refs = refs[0], refs[1:]
    if head > 0:
        refs = refs[4 + int(last) :]
    outs, refs = refs[:4], refs[4:]
    sem = refs[-1]
    own = lax.axis_index("ctx")
    per = outs[0].shape[2] // ways
    copies = []
    for piece, step in zip(pieces, steps):
        column = pl.multiple_of((own ^ step) * per + head * HEAD_DIM, HEAD_DIM)
        for slot, out in enumerate(outs):
            copies.append(
                pltpu.make_async_copy(
                    piece.at[slot], out.at[0, :, pl.ds(column, HEAD_DIM)], sem.at[len(copies)]
                )
            )
    if last:
        short_out = refs[0]
        heads, move, _ = received.shape
        for other in range(heads):
            copies.append(
                pltpu.make_async_copy(
                    received.at[other],
                    short_out.at[pl.ds(short_out.shape[0] - move, move), pl.ds(other * HEAD_DIM, HEAD_DIM)],
                    sem.at[len(copies)],
                )
            )
    for copy in copies:
        copy.start()
    for copy in copies:
        copy.wait()


def join(ways, head, pieces, outs, shape, received=None, short_out=None):
    last = received is not None
    vmem = pl.BlockSpec(memory_space=pltpu.VMEM)
    hbm = pl.BlockSpec(memory_space=pltpu.HBM)
    operands = list(pieces)
    in_specs = [vmem] * ways
    out_shape = [jax.ShapeDtypeStruct(shape, jnp.bfloat16)] * 4
    aliases = {}
    if last:
        operands.append(received)
        in_specs.append(vmem)
        out_shape.append(jax.ShapeDtypeStruct(short_out.shape, jnp.bfloat16))
    old = ([] if outs is None else list(outs)) + ([short_out] if last else [])
    first_out = 0 if outs is not None else 4
    for index, value in enumerate(old):
        aliases[len(operands)] = first_out + index
        operands.append(value)
        in_specs.append(hbm)
    return pl.pallas_call(
        functools.partial(join_kernel, ways, head, last),
        in_specs=in_specs,
        out_specs=[hbm] * len(out_shape),
        out_shape=out_shape,
        scratch_shapes=[pltpu.SemaphoreType.DMA((4 * ways + 2,))],
        input_output_aliases=aliases,
        compiler_params=pltpu.CompilerParams(vmem_limit_bytes=8 << 20),
        cost_estimate=pl.CostEstimate(flops=0, bytes_accessed=10**6, transcendentals=0),
    )(*operands)


def shards(
    q_short,
    k_short,
    v_short,
    dout_short,
    doc_lengths,
    doc_dest,
    q_long,
    k_long,
    v_long,
    dout_long,
    block_order,
):
    ways = lax.axis_size("ctx")
    ranks = lax.axis_size("dp")
    steps = peer_order(ways)
    heads_each = q_long.shape[2] // HEAD_DIM // ways
    arrays = (q_long, k_long, v_long, dout_long)

    def swap(value, step):
        return lax.ppermute(value, "ctx", [(i, i ^ step) for i in range(ways)])

    arrived = []
    for head in range(heads_each):
        packed = pack(head, ways, arrays)
        arrived.append([swap(value, step) for value, step in zip(packed, steps)] + [packed[-1]])
    shorts = (q_short, k_short, v_short, dout_short)
    short_heads = q_short.shape[1] // HEAD_DIM
    short = short_attention(0, short_heads, doc_lengths, doc_dest, shorts, None, None, block_order)
    (tail, table), short = short[4:], short[:4]
    pieces = []
    for head in range(heads_each):
        made = long_attention(ways, table, arrived[head], (tail,) if head == 0 else ())
        if head == 0:
            tail = made[-1]
            received = lax.ppermute(tail, "dp", [(i, (i + ranks // 2) % ranks) for i in range(ranks)])
        pieces.append([swap(value, step) for value, step in zip(made[: ways - 1], steps)] + [made[ways - 1]])
    for head in range(1, short_heads):
        short = short_attention(head, short_heads, doc_lengths, doc_dest, shorts, short, pieces[-1][-1])
    outs = None
    for head in range(heads_each - 1):
        outs = join(ways, head, pieces[head], outs, q_long.shape)
    out_long, dq_long, dk_long, dv_long, out_short = join(
        ways, heads_each - 1, pieces[-1], outs, q_long.shape, received, short[0]
    )
    dq_short, dk_short, dv_short = short[1:]
    return (out_short, dq_short, dk_short, dv_short, out_long, dq_long, dk_long, dv_long)


def solution(mesh):
    flat = P("dp", "ctx")
    deep = P("dp", "ctx", None)

    return jax.shard_map(
        shards,
        mesh=mesh,
        in_specs=(flat,) * 4 + (P(), P()) + (deep,) * 4 + (P(),),
        out_specs=(flat,) * 4 + (deep,) * 4,
        check_vma=False,
    )
```

time: 140 us -> 30.7 us (0.22); the launches traced: 138 us -> 30.5 us
  matrix products: 72.3 us -> 0 us
  local copies, waits for them, and re-layouts: 21 us -> 0.03 us
  between operations: 17.9 us -> 0.79 us
  other arithmetic: 15.1 us -> 0 us
  Pallas kernels: 0 us -> 12.5 us
  starting transfers between devices: 4.18 us -> 12.6 us
  waiting for transfers between devices: 7.87 us -> 4.64 us
    dot_general x84 -> x0, matrix products: 72.3 us -> none  [the longest x28 26.5 us: dot_cols(): lax.dot_general(left, right, (((0,), (0,)), ((), ())), preferred_element_...]
    unnamed x190 -> x14, local copies, waits for them, and re-layouts: 15.9 us -> 0.03 us
    pallas_call x0 -> x8, Pallas kernels: none -> 12.5 us  [the longest x2 5.93 us: short_attention(): pl.pallas_call(functools.partial(short_kernel, head, heads), in_specs=[sm...]
    ppermute x1 -> x13, starting transfers between devices: 4.06 us -> 12.6 us  [the longest x12 9.98 us: swap(): return lax.ppermute(value, 'ctx', [(i, i ^ step) for i in range(ways)])]
    reduce_scatter x1 -> x0, waiting for transfers between devices: 7.13 us -> none  [shards(): lax.psum_scatter(jnp.concatenate(key_parts + value_parts, axis=1), 'ctx',...]
    reduce_sum x17 -> x0, other arithmetic: 4.74 us -> none  [the longest x14 4.48 us: attend_head(): lse = top + jnp.log(jnp.sum(jnp.exp(scores - top), axis=1, keepdims=True))]
    ppermute x1 -> x13, waiting for transfers between devices: 0.01 us -> 4.64 us  [the longest x12 4.18 us: swap(): return lax.ppermute(value, 'ctx', [(i, i ^ step) for i in range(ways)])]
    add x15 -> x0, other arithmetic: 4.41 us -> none  [the longest x14 4.4 us: attend_head(): lse = top + jnp.log(jnp.sum(jnp.exp(scores - top), axis=1, keepdims=True))]
  transfers between devices with their start and end apart: 4 -> 13, of which waited for: 1 -> 3; matrix products, arithmetic and copies ran while one was open for 75% -> 0% of each run, Pallas kernels for 0% -> 34%
where the time goes in v1:
time: 30.7 us; the launch traced here: 30.5 us
  starting transfers between devices  12.6 us (41%)
  Pallas kernels  12.5 us (41%)
  waiting for transfers between devices  4.64 us (15%)
  between operations  0.79 us (3%)
    ppermute x12, starting transfers between devices, swap(): return lax.ppermute(value, 'ctx', [(i, i ^ step) for i in range(ways)])  9.98 us
    pallas_call x2, Pallas kernels, short_attention(): pl.pallas_call(functools.partial(short_kernel, head, heads), in_specs=[sm...  5.93 us
    ppermute x12, waiting for transfers between devices, swap(): return lax.ppermute(value, 'ctx', [(i, i ^ step) for i in range(ways)])  4.18 us
    ppermute x1, starting transfers between devices, shards(): lax.ppermute(tail, 'dp', [(i, (i + ranks // 2) % ranks) for i in range(ra...  2.59 us
    pallas_call x2, Pallas kernels, pack(): pl.pallas_call(functools.partial(pack_kernel, head, ways), in_specs=[pl.B...  2.37 us
    pallas_call x2, Pallas kernels, long_attention(): pl.pallas_call(functools.partial(long_kernel, ways, len(linked)), in_spec...  2.24 us
    pallas_call x2, Pallas kernels, join(): pl.pallas_call(functools.partial(join_kernel, ways, head, last), in_specs...  1.91 us
  transfers between devices with their start and end apart: 13, of which 3 were waited for; matrix products, arithmetic and copies ran while one was open for 0% of the time, Pallas kernels for 34%

profile of v1, /device:TPU:0, one launch (start us, length us, event | category | flops | bytes accessed | tf_op | source)
XLA Modules:
  0.0 30.5 jit_solution(2603942436114230040)
XLA Ops:
  0.6 0.0 copy-start.2
  0.6 0.0 copy-start.3
  0.7 1.2 %shard_map.173 = (bf16[4,128,128]{2,1,0:T(8,128)(2,1)S(1)}, bf16[4,128,128]{2,1,0:T(8,128)(2,1)S(1)}, bf16[4,128,128]{2,1,0:T(8,128)(2,1)S(1)}, bf16[4,128,128]{2,1,0:T(8,128)(2,1)S(1)}) custom-call(bf16[1,128,1024]{2,1,0:T(8,128)(2,1)} %q_ref.3, bf16[1,128,1024]{2,1,0:T(8,128)(2,1)} %k_ref.3, bf16[1,128,1024]{2,1,0:T(8,128)(2,1)} %v_ref.3, ...), custom_call_target="tpu_custom_call" | custom-call | bytes 2000000 | tf_op jit(solution)/shard_map/pallas_call | solution.py:308
  1.9 3.1 %collective-permute-start.6 = (bf16[4,128,128]{2,1,0:T(8,128)(2,1)S(1)}, bf16[4,128,128]{2,1,0:T(8,128)(2,1)S(1)}, u32[]{:S(2)}, u32[]{:S(2)}) collective-permute-start(bf16[4,128,128]{2,1,0:T(8,128)(2,1)S(1)} %get-tuple-element.54), channel_id=1, source_target_pairs={{0,2},{1,3},{2,0},{3,1},{4,6},{5,7},{6,4},{7,5},{8,10},{9,11},{10,... | collective-permute-start | bytes 393224 | tf_op jit(solution)/shard_map/ppermute | solution.py:494
  4.9 0.0 collective-permute-start.7
  5.0 0.0 copy-start
  5.0 0.0 copy-start.1
  5.0 0.0 copy-start.4
  5.0 0.0 copy-start.5
  5.0 0.2 collective-permute-start.8
  5.2 1.1 %shard_map.171 = (bf16[4,128,128]{2,1,0:T(8,128)(2,1)S(1)}, bf16[4,128,128]{2,1,0:T(8,128)(2,1)S(1)}, bf16[4,128,128]{2,1,0:T(8,128)(2,1)S(1)}, bf16[4,128,128]{2,1,0:T(8,128)(2,1)S(1)}) custom-call(bf16[1,128,1024]{2,1,0:T(8,128)(2,1)} %q_ref.3, bf16[1,128,1024]{2,1,0:T(8,128)(2,1)} %k_ref.3, bf16[1,128,1024]{2,1,0:T(8,128)(2,1)} %v_ref.3, ...), custom_call_target="tpu_custom_call" | custom-call | bytes 2000000 | tf_op jit(solution)/shard_map/pallas_call | solution.py:308
  6.4 0.0 copy-start.6
  6.4 2.0 %collective-permute-start = (bf16[4,128,128]{2,1,0:T(8,128)(2,1)S(1)}, bf16[4,128,128]{2,1,0:T(8,128)(2,1)S(1)}, u32[]{:S(2)}, u32[]{:S(2)}) collective-permute-start(bf16[4,128,128]{2,1,0:T(8,128)(2,1)S(1)} %get-tuple-element.45), channel_id=1, source_target_pairs={{0,2},{1,3},{2,0},{3,1},{4,6},{5,7},{6,4},{7,5},{8,10},{9,11},{10,... | collective-permute-start | bytes 393224 | tf_op jit(solution)/shard_map/ppermute | solution.py:494
  8.4 0.0 collective-permute-start.1
  8.4 0.0 copy-done.2
  8.4 0.0 copy-done.3
  8.4 0.0 copy-done
  8.4 0.0 copy-done.1
  8.4 0.0 copy-done.4
  8.4 0.0 copy-done.5
  8.4 0.0 copy-done.6
  8.5 3.1 %shard_map.170 = (bf16[896,256]{1,0:T(8,128)(2,1)}, bf16[768,256]{1,0:T(8,128)(2,1)}, bf16[768,256]{1,0:T(8,128)(2,1)}, bf16[768,256]{1,0:T(8,128)(2,1)}, bf16[2...) custom-call(s32[8,8]{1,0:T(8,128)S(1)} %copy-done.4, s32[8,8]{1,0:T(8,128)S(1)} %copy-done.5, ...), custom_call_target="tpu_custom_call" | custom-call | flops 1000000000 | bytes 3000000 | tf_op jit(solution)/shard_map/pallas_call | solution.py:249
  11.5 0.0 collective-permute-done.6.rest_1_
  11.5 0.2 collective-permute-start.2
  11.8 0.0 collective-permute-done.7.rest_2_
  11.8 0.0 collective-permute-done.8.rest_3_
  11.8 1.1 %shard_map.174 = (bf16[4,128,128]{2,1,0:T(8,128)(2,1)S(1)}, bf16[4,128,128]{2,1,0:T(8,128)(2,1)S(1)}, bf16[4,128,128]{2,1,0:T(8,128)(2,1)S(1)}, bf16[4,128,128]{2,1,0:T(8,128)(2,1)S(1)}, bf16[2,128,128]{2,1,0:T(8,128)(2,1)S(1)}) custom-call(s32[8,128]{1,0:T(8,128)S(1)} %get-tuple-element.44.order, ...), custom_call_target="tpu_custom_call", output_to_operand_aliasing={{4}: (1, {})} | custom-call | flops 1000000000 | bytes 3000000 | tf_op jit(solution)/shard_map/pallas_call | solution.py:391
  12.9 2.0 %collective-permute-start.10 = (bf16[4,128,128]{2,1,0:T(8,128)(2,1)S(1)}, bf16[4,128,128]{2,1,0:T(8,128)(2,1)S(1)}, u32[]{:S(2)}, u32[]{:S(2)}) collective-permute-start(bf16[4,128,128]{2,1,0:T(8,128)(2,1)S(1)} %get-tuple-element.59), channel_id=1, source_target_pairs={{0,2},{1,3},{2,0},{3,1},{4,6},{5,7},{6,4},{7,5},{8,10},{9,11},{10,... | collective-permute-start | bytes 393224 | tf_op jit(solution)/shard_map/ppermute | solution.py:494
  14.9 0.0 collective-permute-start.11
  14.9 0.0 collective-permute-done.rest_0_
  14.9 0.2 collective-permute-start.12
  15.1 1.9 %collective-permute-done.1.rest_1_ = bf16[4,128,128]{2,1,0:T(8,128)(2,1)S(1)} collective-permute-done((bf16[4,128,128]{2,1,0:T(8,128)(2,1)S(1)}, bf16[4,128,128]{2,1,0:T(8,128)(2,1)S(1)}, u32[]{:S(2)}, u32[]{:S(2)}) %collective-permute-start.1) | collective-permute-done | bytes 131104 | tf_op jit(solution)/shard_map/ppermute | solution.py:494
  17.0 0.0 collective-permute-done.2.rest_2_
  17.0 1.1 %shard_map.172 = (bf16[4,128,128]{2,1,0:T(8,128)(2,1)S(1)}, bf16[4,128,128]{2,1,0:T(8,128)(2,1)S(1)}, bf16[4,128,128]{2,1,0:T(8,128)(2,1)S(1)}, bf16[4,128,128]{2,1,0:T(8,128)(2,1)S(1)}) custom-call(s32[8,128]{1,0:T(8,128)S(1)} %get-tuple-element.44.order, bf16[4,128,128]{2,1,0:T(8,128)(2,1)S(1)} %collective-permute-done.rest_0_, ...), custom_call_target="tpu_custom_call" | custom-call | flops 1000000000 | bytes 3000000 | tf_op jit(solution)/shard_map/pallas_call | solution.py:391
  18.1 0.5 %collective-permute-start.3 = (bf16[4,128,128]{2,1,0:T(8,128)(2,1)S(1)}, bf16[4,128,128]{2,1,0:T(8,128)(2,1)S(1)}, u32[]{:S(2)}, u32[]{:S(2)}) collective-permute-start(bf16[4,128,128]{2,1,0:T(8,128)(2,1)S(1)} %get-tuple-element.49), channel_id=1, source_target_pairs={{0,2},{1,3},{2,0},{3,1},{4,6},{5,7},{6,4},{7,5},{8,10},{9,11},{10,... | collective-permute-start | bytes 393224 | tf_op jit(solution)/shard_map/ppermute | solution.py:494
  18.7 1.5 %collective-permute-start.4 = (bf16[4,128,128]{2,1,0:T(8,128)(2,1)S(1)}, bf16[4,128,128]{2,1,0:T(8,128)(2,1)S(1)}, u32[]{:S(2)}, u32[]{:S(2)}) collective-permute-start(bf16[4,128,128]{2,1,0:T(8,128)(2,1)S(1)} %get-tuple-element.50), channel_id=1, source_target_pairs={{0,3},{1,2},{2,1},{3,0},{4,7},{5,6},{6,5},{7,4},{8,11},{9,10},{10,... | collective-permute-start | bytes 393224 | tf_op jit(solution)/shard_map/ppermute | solution.py:494
  20.2 0.0 collective-permute-done.10.refs_0_
  20.2 0.2 collective-permute-start.5
  20.3 2.3 %collective-permute-done.11.refs_1_ = bf16[4,128,128]{2,1,0:T(8,128)(2,1)S(1)} collective-permute-done((bf16[4,128,128]{2,1,0:T(8,128)(2,1)S(1)}, bf16[4,128,128]{2,1,0:T(8,128)(2,1)S(1)}, u32[]{:S(2)}, u32[]{:S(2)}) %collective-permute-start.11) | collective-permute-done | bytes 131104 | tf_op jit(solution)/shard_map/ppermute | solution.py:494
  22.6 2.6 %collective-permute-start.9 = (bf16[2,128,128]{2,1,0:T(8,128)(2,1)S(1)}, bf16[2,128,128]{2,1,0:T(8,128)(2,1)S(1)}, u32[]{:S(2)}, u32[]{:S(2)}) collective-permute-start(bf16[2,128,128]{2,1,0:T(8,128)(2,1)S(1)} %get-tuple-element.58), channel_id=1, source_target_pairs={{0,16},{4,20},{8,24},{12,28},{16,0},{20,4},{24,8},{28,12},{1,17},{... | collective-permute-start | bytes 196616 | tf_op jit(solution)/shard_map/ppermute | solution.py:509
  25.2 2.9 %shard_map.176 = (bf16[896,256]{1,0:T(8,128)(2,1)}, bf16[768,256]{1,0:T(8,128)(2,1)}, bf16[768,256]{1,0:T(8,128)(2,1)}, bf16[768,256]{1,0:T(8,128)(2,1)}) custom-call(s32[8,8]{1,0:T(8,128)S(1)} %copy-done.4, s32[8,8]{1,0:T(8,128)S(1)} %copy-done.5, ...), custom_call_target="tpu_custom_call", output_to_operand_aliasing={{0}: (6, {}), {1}: (7, {}), {2}: (8, {}), {3}: (9, {})} | custom-call | flops 1000000000 | bytes 3000000 | tf_op jit(solution)/shard_map/pallas_call | solution.py:249
  28.1 0.0 collective-permute-done.12.refs_2_
  28.1 0.9 %shard_map.175 = (bf16[1,128,1024]{2,1,0:T(8,128)(2,1)}, bf16[1,128,1024]{2,1,0:T(8,128)(2,1)}, bf16[1,128,1024]{2,1,0:T(8,128)(2,1)}, bf16[1,128,1024]{2,1,0:T(8,128)(2,1)}) custom-call(bf16[4,128,128]{2,1,0:T(8,128)(2,1)S(1)} %collective-permute-done.10.refs_0_, bf16[4,128,128]{2,1,0:T(8,128)(2,1)S(1)} %collective-permute-done.11.refs_1_, ...), custom_call_target="tpu_custom_call" | custom-call | bytes 1000000 | tf_op jit(solution)/shard_map/pallas_call | solution.py:462
  29.0 0.5 %collective-permute-done.9.refs_4_ = bf16[2,128,128]{2,1,0:T(8,128)(2,1)S(1)} collective-permute-done((bf16[2,128,128]{2,1,0:T(8,128)(2,1)S(1)}, bf16[2,128,128]{2,1,0:T(8,128)(2,1)S(1)}, u32[]{:S(2)}, u32[]{:S(2)}) %collective-permute-start.9) | collective-permute-done | bytes 65568 | tf_op jit(solution)/shard_map/ppermute | solution.py:509
  29.5 0.0 collective-permute-done.3.refs_0_
  29.5 0.0 collective-permute-done.4.refs_1_
  29.5 0.0 collective-permute-done.5.refs_2_
  29.5 1.0 %shard_map.177 = (bf16[1,128,1024]{2,1,0:T(8,128)(2,1)}, bf16[1,128,1024]{2,1,0:T(8,128)(2,1)}, bf16[1,128,1024]{2,1,0:T(8,128)(2,1)}, bf16[1,128,1024]{2,1,0:T(8,128)(2,1)}, bf16[896,256]{1,0:T(8,128)(2,1)}) custom-call(bf16[4,128,128]{2,1,0:T(8,128)(2,1)S(1)} %collective-permute-done, ...), custom_call_target="tpu_custom_call", output_to_operand_aliasing={{0}: (5, {}), {1}: (6, {}), {2}: (7, {}), {3}: (8, {}), {4}... | custom-call | bytes 1000000 | tf_op jit(solution)/shard_map/pallas_call | solution.py:462
Async XLA Ops:
  0.6 7.8 %copy-start.2 = (bf16[768,256]{1,0:T(8,128)(2,1)S(1)}, bf16[768,256]{1,0:T(8,128)(2,1)}, u32[]{:S(2)}) copy-start(bf16[768,256]{1,0:T(8,128)(2,1)} %v_hbm.3) | copy-start | bytes 1179652
  0.6 7.8 %copy-start.3 = (bf16[768,256]{1,0:T(8,128)(2,1)S(1)}, bf16[768,256]{1,0:T(8,128)(2,1)}, u32[]{:S(2)}) copy-start(bf16[768,256]{1,0:T(8,128)(2,1)} %d_hbm.3) | copy-start | bytes 1179652
  1.9 9.6 %collective-permute-start.6 = (bf16[4,128,128]{2,1,0:T(8,128)(2,1)S(1)}, bf16[4,128,128]{2,1,0:T(8,128)(2,1)S(1)}, u32[]{:S(2)}, u32[]{:S(2)}) collective-permute-start(bf16[4,128,128]{2,1,0:T(8,128)(2,1)S(1)} %get-tuple-element.54), channel_id=1, source_target_pairs={{0,2},{1,3},{2,0},{3,1},{4,6},{5,7},{6,4},{7,5},{8,10},{9,11},{10,... | collective-permute-start | bytes 393224 | tf_op jit(solution)/shard_map/ppermute | solution.py:494
  4.9 6.8 %collective-permute-start.7 = (bf16[4,128,128]{2,1,0:T(8,128)(2,1)S(1)}, bf16[4,128,128]{2,1,0:T(8,128)(2,1)S(1)}, u32[]{:S(2)}, u32[]{:S(2)}) collective-permute-start(bf16[4,128,128]{2,1,0:T(8,128)(2,1)S(1)} %get-tuple-element.55), channel_id=1, source_target_pairs={{0,3},{1,2},{2,1},{3,0},{4,7},{5,6},{6,5},{7,4},{8,11},{9,10},{10,... | collective-permute-start | bytes 393224 | tf_op jit(solution)/shard_map/ppermute | solution.py:494
  5.0 3.5 %copy-start = (bf16[768,256]{1,0:T(8,128)(2,1)S(1)}, bf16[768,256]{1,0:T(8,128)(2,1)}, u32[]{:S(2)}) copy-start(bf16[768,256]{1,0:T(8,128)(2,1)} %q_hbm.3) | copy-start | bytes 1179652
  5.0 3.5 %copy-start.1 = (bf16[768,256]{1,0:T(8,128)(2,1)S(1)}, bf16[768,256]{1,0:T(8,128)(2,1)}, u32[]{:S(2)}) copy-start(bf16[768,256]{1,0:T(8,128)(2,1)} %k_hbm.3) | copy-start | bytes 1179652
  5.0 3.5 %copy-start.4 = (s32[8,8]{1,0:T(8,128)S(1)}, s32[8,8]{1,0:T(8,128)}, u32[]{:S(2)}) copy-start(s32[8,8]{1,0:T(8,128)} %lengths.3) | copy-start | bytes 772
  5.0 3.5 %copy-start.5 = (s32[8,8]{1,0:T(8,128)S(1)}, s32[8,8]{1,0:T(8,128)}, u32[]{:S(2)}) copy-start(s32[8,8]{1,0:T(8,128)} %dests.3) | copy-start | bytes 772
  5.0 6.8 %collective-permute-start.8 = (bf16[4,128,128]{2,1,0:T(8,128)(2,1)S(1)}, bf16[4,128,128]{2,1,0:T(8,128)(2,1)S(1)}, u32[]{:S(2)}, u32[]{:S(2)}) collective-permute-start(bf16[4,128,128]{2,1,0:T(8,128)(2,1)S(1)} %get-tuple-element.56), channel_id=1, source_target_pairs={{0,1},{1,0},{2,3},{3,2},{4,5},{5,4},{6,7},{7,6},{8,9},{9,8},{10,11... | collective-permute-start | bytes 393224 | tf_op jit(solution)/shard_map/ppermute | solution.py:494
  6.4 2.1 %copy-start.6 = (s32[8]{0:T(128)S(1)}, s32[8]{0:T(128)}, u32[]{:S(2)}) copy-start(s32[8]{0:T(128)} %rest_0_.1) | copy-start | bytes 100
  6.4 8.6 %collective-permute-start = (bf16[4,128,128]{2,1,0:T(8,128)(2,1)S(1)}, bf16[4,128,128]{2,1,0:T(8,128)(2,1)S(1)}, u32[]{:S(2)}, u32[]{:S(2)}) collective-permute-start(bf16[4,128,128]{2,1,0:T(8,128)(2,1)S(1)} %get-tuple-element.45), channel_id=1, source_target_pairs={{0,2},{1,3},{2,0},{3,1},{4,6},{5,7},{6,4},{7,5},{8,10},{9,11},{10,... | collective-permute-start | bytes 393224 | tf_op jit(solution)/shard_map/ppermute | solution.py:494
  8.4 8.6 %collective-permute-start.1 = (bf16[4,128,128]{2,1,0:T(8,128)(2,1)S(1)}, bf16[4,128,128]{2,1,0:T(8,128)(2,1)S(1)}, u32[]{:S(2)}, u32[]{:S(2)}) collective-permute-start(bf16[4,128,128]{2,1,0:T(8,128)(2,1)S(1)} %get-tuple-element.46), channel_id=1, source_target_pairs={{0,3},{1,2},{2,1},{3,0},{4,7},{5,6},{6,5},{7,4},{8,11},{9,10},{10,... | collective-permute-start | bytes 393224 | tf_op jit(solution)/shard_map/ppermute | solution.py:494
  11.5 5.5 %collective-permute-start.2 = (bf16[4,128,128]{2,1,0:T(8,128)(2,1)S(1)}, bf16[4,128,128]{2,1,0:T(8,128)(2,1)S(1)}, u32[]{:S(2)}, u32[]{:S(2)}) collective-permute-start(bf16[4,128,128]{2,1,0:T(8,128)(2,1)S(1)} %get-tuple-element.47), channel_id=1, source_target_pairs={{0,1},{1,0},{2,3},{3,2},{4,5},{5,4},{6,7},{7,6},{8,9},{9,8},{10,11... | collective-permute-start | bytes 393224 | tf_op jit(solution)/shard_map/ppermute | solution.py:494
  12.9 7.3 %collective-permute-start.10 = (bf16[4,128,128]{2,1,0:T(8,128)(2,1)S(1)}, bf16[4,128,128]{2,1,0:T(8,128)(2,1)S(1)}, u32[]{:S(2)}, u32[]{:S(2)}) collective-permute-start(bf16[4,128,128]{2,1,0:T(8,128)(2,1)S(1)} %get-tuple-element.59), channel_id=1, source_target_pairs={{0,2},{1,3},{2,0},{3,1},{4,6},{5,7},{6,4},{7,5},{8,10},{9,11},{10,... | collective-permute-start | bytes 393224 | tf_op jit(solution)/shard_map/ppermute | solution.py:494
  14.9 7.7 %collective-permute-start.11 = (bf16[4,128,128]{2,1,0:T(8,128)(2,1)S(1)}, bf16[4,128,128]{2,1,0:T(8,128)(2,1)S(1)}, u32[]{:S(2)}, u32[]{:S(2)}) collective-permute-start(bf16[4,128,128]{2,1,0:T(8,128)(2,1)S(1)} %get-tuple-element.60), channel_id=1, source_target_pairs={{0,3},{1,2},{2,1},{3,0},{4,7},{5,6},{6,5},{7,4},{8,11},{9,10},{10,... | collective-permute-start | bytes 393224 | tf_op jit(solution)/shard_map/ppermute | solution.py:494
  14.9 13.1 %collective-permute-start.12 = (bf16[4,128,128]{2,1,0:T(8,128)(2,1)S(1)}, bf16[4,128,128]{2,1,0:T(8,128)(2,1)S(1)}, u32[]{:S(2)}, u32[]{:S(2)}) collective-permute-start(bf16[4,128,128]{2,1,0:T(8,128)(2,1)S(1)} %get-tuple-element.61), channel_id=1, source_target_pairs={{0,1},{1,0},{2,3},{3,2},{4,5},{5,4},{6,7},{7,6},{8,9},{9,8},{10,11... | collective-permute-start | bytes 393224 | tf_op jit(solution)/shard_map/ppermute | solution.py:494
  18.1 11.4 %collective-permute-start.3 = (bf16[4,128,128]{2,1,0:T(8,128)(2,1)S(1)}, bf16[4,128,128]{2,1,0:T(8,128)(2,1)S(1)}, u32[]{:S(2)}, u32[]{:S(2)}) collective-permute-start(bf16[4,128,128]{2,1,0:T(8,128)(2,1)S(1)} %get-tuple-element.49), channel_id=1, source_target_pairs={{0,2},{1,3},{2,0},{3,1},{4,6},{5,7},{6,4},{7,5},{8,10},{9,11},{10,... | collective-permute-start | bytes 393224 | tf_op jit(solution)/shard_map/ppermute | solution.py:494
  18.7 10.8 %collective-permute-start.4 = (bf16[4,128,128]{2,1,0:T(8,128)(2,1)S(1)}, bf16[4,128,128]{2,1,0:T(8,128)(2,1)S(1)}, u32[]{:S(2)}, u32[]{:S(2)}) collective-permute-start(bf16[4,128,128]{2,1,0:T(8,128)(2,1)S(1)} %get-tuple-element.50), channel_id=1, source_target_pairs={{0,3},{1,2},{2,1},{3,0},{4,7},{5,6},{6,5},{7,4},{8,11},{9,10},{10,... | collective-permute-start | bytes 393224 | tf_op jit(solution)/shard_map/ppermute | solution.py:494
  20.2 9.3 %collective-permute-start.5 = (bf16[4,128,128]{2,1,0:T(8,128)(2,1)S(1)}, bf16[4,128,128]{2,1,0:T(8,128)(2,1)S(1)}, u32[]{:S(2)}, u32[]{:S(2)}) collective-permute-start(bf16[4,128,128]{2,1,0:T(8,128)(2,1)S(1)} %get-tuple-element.51), channel_id=1, source_target_pairs={{0,1},{1,0},{2,3},{3,2},{4,5},{5,4},{6,7},{7,6},{8,9},{9,8},{10,11... | collective-permute-start | bytes 393224 | tf_op jit(solution)/shard_map/ppermute | solution.py:494
  22.6 6.9 %collective-permute-start.9 = (bf16[2,128,128]{2,1,0:T(8,128)(2,1)S(1)}, bf16[2,128,128]{2,1,0:T(8,128)(2,1)S(1)}, u32[]{:S(2)}, u32[]{:S(2)}) collective-permute-start(bf16[2,128,128]{2,1,0:T(8,128)(2,1)S(1)} %get-tuple-element.58), channel_id=1, source_target_pairs={{0,16},{4,20},{8,24},{12,28},{16,0},{20,4},{24,8},{28,12},{1,17},{... | collective-permute-start | bytes 196616 | tf_op jit(solution)/shard_map/ppermute | solution.py:509

commit v2 on v1

--- a/solution.py
+++ b/solution.py
@@ -99,7 +99,7 @@
     column = pl.ds(head * HEAD_DIM, HEAD_DIM)
 
     loads = [
-        pltpu.make_async_copy(ref.at[:, column], held.at[slot], in_sem.at[slot])
+        pltpu.make_async_copy(ref.at[:, column], held.at[slot], in_sem)
         for slot, ref in enumerate((q_hbm, k_hbm, v_hbm, d_hbm))
     ]
     for load in loads:
@@ -114,7 +114,7 @@
                     pltpu.make_async_copy(
                         ref.at[pl.ds(tokens - 3 * tile, 3 * tile), columns],
                         ends.at[other - 1, slot],
-                        end_sem.at[len(others)],
+                        end_sem,
                     )
                 )
         for load in others:
@@ -128,19 +128,12 @@
         start = jnp.where(place >= begin, begin, start)
     tail = lengths[rank, count - 1]
     moves = dests[rank, count - 1] != rank
-    stores = []
 
     def store(slot, low, high, target):
-        copy = pltpu.make_async_copy(
-            made.at[slot, pl.ds(low, high - low), :],
-            target.at[pl.ds(low, high - low), column],
-            out_sem.at[len(stores)],
-        )
-        copy.start()
-        stores.append(copy)
-
-    for load in loads:
-        load.wait()
+        rows = pl.ds(low, high - low)
+        pltpu.make_async_copy(made.at[slot, rows, :], target.at[rows, column], out_sem).start()
+
+    pltpu.make_async_copy(held, held, in_sem).wait()
     q_ref, k_ref, v_ref, d_ref = [held.at[slot] for slot in range(4)]
     keys_t = k_ref[...].T
     values_t = v_ref[...].T
@@ -219,9 +212,8 @@
             store(3, low, high, dv_hbm)
 
     staged(blocks, scores_of, softmax_of, products_of)
-    for load in others:
-        load.wait()
-    if head == 0:
+    if others:
+        pltpu.make_async_copy(ends, ends, end_sem).wait()
         for other in range(1, heads):
             scores = dot_rows(ends[other - 1, 1], ends[other - 1, 0, 2 * tile :, :])
             key = lax.broadcasted_iota(jnp.int32, scores.shape, 0)
@@ -231,14 +223,12 @@
             grown = jnp.exp2((scores - jnp.max(scores, axis=0, keepdims=True)) * (scale * LOG2E))
             weights = (grown * (1.0 / jnp.sum(grown, axis=0, keepdims=True))).astype(jnp.bfloat16)
             tail_ref[other] = sent(dot(weights.T, ends[other - 1, 2]).astype(jnp.bfloat16))
-    for copy in stores:
-        copy.wait()
+    pltpu.make_async_copy(made, made, out_sem).wait()
 
 
 def short_attention(head, heads, lengths, dests, arrays, before, after, order=None):
     tokens, width = arrays[0].shape
     move = tokens // 6
-    blocks = 3
     smem = pl.BlockSpec(memory_space=pltpu.SMEM)
     hbm = pl.BlockSpec(memory_space=pltpu.HBM)
     vmem = pl.BlockSpec(memory_space=pltpu.VMEM)
@@ -262,13 +252,13 @@
         scratch_shapes=[
             pltpu.VMEM((4, tokens, HEAD_DIM), jnp.bfloat16),
             pltpu.VMEM((4, tokens, HEAD_DIM), jnp.bfloat16),
-            pltpu.SemaphoreType.DMA((4,)),
-            pltpu.SemaphoreType.DMA((4 * blocks,)),
+            pltpu.SemaphoreType.DMA,
+            pltpu.SemaphoreType.DMA,
         ]
         + (
             [
                 pltpu.VMEM((max(heads - 1, 1), 3, 3 * tile, HEAD_DIM), jnp.bfloat16),
-                pltpu.SemaphoreType.DMA((max(3 * heads - 3, 1),)),
+                pltpu.SemaphoreType.DMA,
             ]
             if first
             else []
@@ -283,37 +273,32 @@
     return [step for step in range(2, ways)] + [1]
 
 
-def pack_kernel(head, ways, q_ref, k_ref, v_ref, d_ref, *rest):
-    steps = peer_order(ways) + [0]
-    outs, sem = rest[: len(steps)], rest[-1]
+def pack_kernel(parts, ways, after, q_ref, k_ref, v_ref, d_ref, *rest):
+    rest = rest[after:]
+    outs, (all_bytes, sem) = rest[: len(parts)], rest[len(parts) :]
     own = lax.axis_index("ctx")
     per = q_ref.shape[2] // ways
-    copies = []
-    for out, step in zip(outs, steps):
+    for out, (head, step) in zip(outs, parts):
         column = pl.multiple_of((own ^ step) * per + head * HEAD_DIM, HEAD_DIM)
         for slot, ref in enumerate((q_ref, k_ref, v_ref, d_ref)):
-            copies.append(
-                pltpu.make_async_copy(
-                    ref.at[0, :, pl.ds(column, HEAD_DIM)], out.at[slot], sem.at[len(copies)]
-                )
-            )
-    for copy in copies:
-        copy.start()
-    for copy in copies:
-        copy.wait()
-
-
-def pack(head, ways, arrays):
+            pltpu.make_async_copy(ref.at[0, :, pl.ds(column, HEAD_DIM)], out.at[slot], sem).start()
+    pltpu.make_async_copy(all_bytes, all_bytes, sem).wait()
+
+
+def pack(parts, ways, arrays, after=()):
     rows = arrays[0].shape[1]
     return pl.pallas_call(
-        functools.partial(pack_kernel, head, ways),
-        in_specs=[pl.BlockSpec(memory_space=pltpu.HBM)] * 4,
-        out_specs=[pl.BlockSpec(memory_space=pltpu.VMEM)] * ways,
-        out_shape=[jax.ShapeDtypeStruct((4, rows, HEAD_DIM), jnp.bfloat16)] * ways,
-        scratch_shapes=[pltpu.SemaphoreType.DMA((4 * ways,))],
+        functools.partial(pack_kernel, parts, ways, len(after)),
+        in_specs=[pl.BlockSpec(memory_space=pltpu.HBM)] * 4 + [pl.BlockSpec(memory_space=pl.ANY)] * len(after),
+        out_specs=[pl.BlockSpec(memory_space=pltpu.VMEM)] * len(parts),
+        out_shape=[jax.ShapeDtypeStruct((4, rows, HEAD_DIM), jnp.bfloat16)] * len(parts),
+        scratch_shapes=[
+            pltpu.VMEM((4 * len(parts), rows, HEAD_DIM), jnp.bfloat16),
+            pltpu.SemaphoreType.DMA,
+        ],
         compiler_params=pltpu.CompilerParams(vmem_limit_bytes=8 << 20),
         cost_estimate=pl.CostEstimate(flops=0, bytes_accessed=2 * 10**6, transcendentals=0),
-    )(*[pltpu.with_memory_space_constraint(array, pltpu.HBM) for array in arrays])
+    )(*[pltpu.with_memory_space_constraint(array, pltpu.HBM) for array in arrays], *after)
 
 
 def long_kernel(ways, linked, order, *rest):
@@ -321,7 +306,7 @@
     steps = peer_order(ways) + [0]
     arrived = rest[:ways]
     outs = rest[ways : 2 * ways]
-    held, made = rest[2 * ways + linked :]
+    held, made = rest[2 * ways :]
     scale = HEAD_DIM ** (-0.5)
     own = lax.axis_index("ctx")
     rows = arrived[0].shape[1]
@@ -391,80 +376,67 @@
     return pl.pallas_call(
         functools.partial(long_kernel, ways, len(linked)),
         in_specs=[vmem] + anywhere + [vmem] * ways,
-        out_specs=[vmem] * ways + anywhere,
-        out_shape=[piece] * ways + [jax.ShapeDtypeStruct(x.shape, x.dtype) for x in linked],
+        out_specs=[vmem] * ways,
+        out_shape=[piece] * ways,
         scratch_shapes=[
             pltpu.VMEM((4, rows * ways, HEAD_DIM), jnp.bfloat16),
             pltpu.VMEM((4, rows * ways, HEAD_DIM), jnp.bfloat16),
         ],
-        input_output_aliases={1 + i: ways + i for i in range(len(linked))},
         compiler_params=pltpu.CompilerParams(vmem_limit_bytes=16 << 20),
         cost_estimate=pl.CostEstimate(flops=10**9, bytes_accessed=3 * 10**6, transcendentals=0),
     )(order, *linked, *arrived)
 
 
-def join_kernel(ways, head, last, *refs):
-    steps = peer_order(ways) + [0]
-    pieces = refs[:ways]
-    refs = refs[ways:]
-    if last:
+def join_kernel(parts, ways, olds, with_short, *refs):
+    pieces = refs[: len(parts)]
+    refs = refs[len(parts) :]
+    if with_short:
         received, refs = refs[0], refs[1:]
-    if head > 0:
-        refs = refs[4 + int(last) :]
+    refs = refs[olds:]
     outs, refs = refs[:4], refs[4:]
-    sem = refs[-1]
+    all_bytes, sem = refs[-2:]
     own = lax.axis_index("ctx")
     per = outs[0].shape[2] // ways
-    copies = []
-    for piece, step in zip(pieces, steps):
+    for piece, (head, step) in zip(pieces, parts):
         column = pl.multiple_of((own ^ step) * per + head * HEAD_DIM, HEAD_DIM)
         for slot, out in enumerate(outs):
-            copies.append(
-                pltpu.make_async_copy(
-                    piece.at[slot], out.at[0, :, pl.ds(column, HEAD_DIM)], sem.at[len(copies)]
-                )
-            )
-    if last:
+            pltpu.make_async_copy(piece.at[slot], out.at[0, :, pl.ds(column, HEAD_DIM)], sem).start()
+    if with_short:
         short_out = refs[0]
         heads, move, _ = received.shape
+        rows = pl.ds(short_out.shape[0] - move, move)
         for other in range(heads):
-            copies.append(
-                pltpu.make_async_copy(
-                    received.at[other],
-                    short_out.at[pl.ds(short_out.shape[0] - move, move), pl.ds(other * HEAD_DIM, HEAD_DIM)],
-                    sem.at[len(copies)],
-                )
-            )
-    for copy in copies:
-        copy.start()
-    for copy in copies:
-        copy.wait()
-
-
-def join(ways, head, pieces, outs, shape, received=None, short_out=None):
-    last = received is not None
+            columns = pl.ds(other * HEAD_DIM, HEAD_DIM)
+            pltpu.make_async_copy(received.at[other], short_out.at[rows, columns], sem).start()
+    pltpu.make_async_copy(all_bytes, all_bytes, sem).wait()
+
+
+def join(parts, ways, pieces, outs, shape, received=None, short_out=None):
+    with_short = received is not None
     vmem = pl.BlockSpec(memory_space=pltpu.VMEM)
     hbm = pl.BlockSpec(memory_space=pltpu.HBM)
     operands = list(pieces)
-    in_specs = [vmem] * ways
+    in_specs = [vmem] * len(pieces)
     out_shape = [jax.ShapeDtypeStruct(shape, jnp.bfloat16)] * 4
     aliases = {}
-    if last:
+    size = 4 * len(parts) * shape[1]
+    if with_short:
         operands.append(received)
         in_specs.append(vmem)
         out_shape.append(jax.ShapeDtypeStruct(short_out.shape, jnp.bfloat16))
-    old = ([] if outs is None else list(outs)) + ([short_out] if last else [])
+        size += received.shape[0] * received.shape[1]
+    old = ([] if outs is None else list(outs)) + ([short_out] if with_short else [])
     first_out = 0 if outs is not None else 4
     for index, value in enumerate(old):
         aliases[len(operands)] = first_out + index
         operands.append(value)
         in_specs.append(hbm)
     return pl.pallas_call(
-        functools.partial(join_kernel, ways, head, last),
+        functools.partial(join_kernel, parts, ways, len(old), with_short),
         in_specs=in_specs,
         out_specs=[hbm] * len(out_shape),
         out_shape=out_shape,
-        scratch_shapes=[pltpu.SemaphoreType.DMA((4 * ways + 2,))],
+        scratch_shapes=[pltpu.VMEM((size, HEAD_DIM), jnp.bfloat16), pltpu.SemaphoreType.DMA],
         input_output_aliases=aliases,
         compiler_params=pltpu.CompilerParams(vmem_limit_bytes=8 << 20),
         cost_estimate=pl.CostEstimate(flops=0, bytes_accessed=10**6, transcendentals=0),
@@ -493,29 +465,30 @@
     def swap(value, step):
         return lax.ppermute(value, "ctx", [(i, i ^ step) for i in range(ways)])
 
-    arrived = []
-    for head in range(heads_each):
-        packed = pack(head, ways, arrays)
-        arrived.append([swap(value, step) for value, step in zip(packed, steps)] + [packed[-1]])
+    far = [step for step in steps if step != 1]
+    first = [(0, step) for step in far]
+    later = [(0, 1), (0, 0)] + [(head, step) for head in range(1, heads_each) for step in steps + [0]]
+    packed = dict(zip(first, pack(first, ways, arrays)))
+    packed.update(zip(later, pack(later, ways, arrays, (packed[first[0]],))))
+    arrived = [[swap(packed[head, step], step) for step in steps] + [packed[head, 0]] for head in range(heads_each)]
     shorts = (q_short, k_short, v_short, dout_short)
     short_heads = q_short.shape[1] // HEAD_DIM
     short = short_attention(0, short_heads, doc_lengths, doc_dest, shorts, None, None, block_order)
     (tail, table), short = short[4:], short[:4]
+    received = lax.ppermute(tail, "dp", [(i, (i + ranks // 2) % ranks) for i in range(ranks)])
     pieces = []
     for head in range(heads_each):
-        made = long_attention(ways, table, arrived[head], (tail,) if head == 0 else ())
-        if head == 0:
-            tail = made[-1]
-            received = lax.ppermute(tail, "dp", [(i, (i + ranks // 2) % ranks) for i in range(ranks)])
-        pieces.append([swap(value, step) for value, step in zip(made[: ways - 1], steps)] + [made[ways - 1]])
+        made = long_attention(ways, table, arrived[head], (pieces[-1][-1] if head else tail,))
+        pieces.append([swap(value, step) for value, step in zip(made[: ways - 1], steps)] + [made[-1]])
     for head in range(1, short_heads):
         short = short_attention(head, short_heads, doc_lengths, doc_dest, shorts, short, pieces[-1][-1])
-    outs = None
-    for head in range(heads_each - 1):
-        outs = join(ways, head, pieces[head], outs, q_long.shape)
-    out_long, dq_long, dk_long, dv_long, out_short = join(
-        ways, heads_each - 1, pieces[-1], outs, q_long.shape, received, short[0]
-    )
+    whole = {(head, step): pieces[head][index] for head in range(heads_each) for index, step in enumerate(steps + [0])}
+    final = [(heads_each - 1, step) for step in far]
+    sooner = [key for key in whole if key not in final]
+    outs = join(sooner, ways, [whole[key] for key in sooner], None, q_long.shape, received, short[0])
+    out_short = outs[4]
+    outs = join(final, ways, [whole[key] for key in final], outs[:4], q_long.shape)
+    out_long, dq_long, dk_long, dv_long = outs
     dq_short, dk_short, dv_short = short[1:]
     return (out_short, dq_short, dk_short, dv_short, out_long, dq_long, dk_long, dv_long)
 

time: 30.7 us -> 29 us (0.945)
  the two profiles are of different devices: /device:TPU:0 before, /device:TPU:1 now
where the time goes in v2:
time: 29 us; the launch traced here: 28.8 us
  starting transfers between devices  14.3 us (49%)
  Pallas kernels  11.6 us (40%)
  waiting for transfers between devices  1.99 us (7%)
  between operations  0.81 us (3%)
    ppermute x12, starting transfers between devices, swap(): return lax.ppermute(value, 'ctx', [(i, i ^ step) for i in range(ways)])  12 us
    pallas_call x2, Pallas kernels, short_attention(): pl.pallas_call(functools.partial(short_kernel, head, heads), in_specs=[sm...  5.65 us
    ppermute x1, starting transfers between devices, shards(): lax.ppermute(tail, 'dp', [(i, (i + ranks // 2) % ranks) for i in range(ra...  2.31 us
    pallas_call x2, Pallas kernels, long_attention(): pl.pallas_call(functools.partial(long_kernel, ways, len(linked)), in_spec...  2.25 us
    pallas_call x2, Pallas kernels, pack(): pl.pallas_call(functools.partial(pack_kernel, parts, ways, len(after)), i...  2.14 us
    ppermute x12, waiting for transfers between devices, swap(): return lax.ppermute(value, 'ctx', [(i, i ^ step) for i in range(ways)])  1.99 us
    pallas_call x2, Pallas kernels, join(): pl.pallas_call(functools.partial(join_kernel, parts, ways, len(old), with...  1.6 us
  transfers between devices with their start and end apart: 13, of which 2 were waited for; matrix products, arithmetic and copies ran while one was open for 0% of the time, Pallas kernels for 35%

profile of v2, /device:TPU:1, one launch (start us, length us, event | category | flops | bytes accessed | tf_op | source)
XLA Modules:
  0.0 28.8 jit_solution(15069402940269208722)
XLA Ops:
  0.6 0.0 copy-start.3
  0.6 0.0 copy-start.5
  0.7 0.9 %shard_map.171 = (bf16[4,128,128]{2,1,0:T(8,128)(2,1)S(1)}, bf16[4,128,128]{2,1,0:T(8,128)(2,1)S(1)}) custom-call(bf16[1,128,1024]{2,1,0:T(8,128)(2,1)} %q_ref.3, bf16[1,128,1024]{2,1,0:T(8,128)(2,1)} %k_ref.3, bf16[1,128,1024]{2,1,0:T(8,128)(2,1)} %v_ref.3, bf16[1,128,1024]{2,1,0:T(8,128)(2,1)} %d_ref.3), custom_call_target="tpu_custom_call" | custom-call | bytes 2000000 | tf_op jit(solution)/shard_map/pallas_call | solution.py:290
  1.6 2.7 %collective-permute-start.1 = (bf16[4,128,128]{2,1,0:T(8,128)(2,1)S(1)}, bf16[4,128,128]{2,1,0:T(8,128)(2,1)S(1)}, u32[]{:S(2)}, u32[]{:S(2)}) collective-permute-start(bf16[4,128,128]{2,1,0:T(8,128)(2,1)S(1)} %get-tuple-element.46), channel_id=1, source_target_pairs={{0,3},{1,2},{2,1},{3,0},{4,7},{5,6},{6,5},{7,4},{8,11},{9,10},{10,... | collective-permute-start | bytes 393224 | tf_op jit(solution)/shard_map/ppermute | solution.py:466
  4.3 0.0 copy-start
  4.3 0.0 copy-start.1
  4.3 0.0 copy-start.2
  4.3 0.0 collective-permute-start
  4.3 1.2 %shard_map.172 = (bf16[4,128,128]{2,1,0:T(8,128)(2,1)S(1)}, bf16[4,128,128]{2,1,0:T(8,128)(2,1)S(1)}, bf16[4,128,128]{2,1,0:T(8,128)(2,1)S(1)}, bf16[4,128,128]{...) custom-call(bf16[1,128,1024]{2,1,0:T(8,128)(2,1)} %q_ref.3, ...), custom_call_target="tpu_custom_call" | custom-call | bytes 2000000 | tf_op jit(solution)/shard_map/pallas_call | solution.py:290
  5.5 0.0 copy-start.4
  5.5 0.5 %collective-permute-start.2 = (bf16[4,128,128]{2,1,0:T(8,128)(2,1)S(1)}, bf16[4,128,128]{2,1,0:T(8,128)(2,1)S(1)}, u32[]{:S(2)}, u32[]{:S(2)}) collective-permute-start(bf16[4,128,128]{2,1,0:T(8,128)(2,1)S(1)} %get-tuple-element.47), channel_id=1, source_target_pairs={{0,1},{1,0},{2,3},{3,2},{4,5},{5,4},{6,7},{7,6},{8,9},{9,8},{10,11... | collective-permute-start | bytes 393224 | tf_op jit(solution)/shard_map/ppermute | solution.py:466
  6.0 1.1 %collective-permute-start.6 = (bf16[4,128,128]{2,1,0:T(8,128)(2,1)S(1)}, bf16[4,128,128]{2,1,0:T(8,128)(2,1)S(1)}, u32[]{:S(2)}, u32[]{:S(2)}) collective-permute-start(bf16[4,128,128]{2,1,0:T(8,128)(2,1)S(1)} %get-tuple-element.53), channel_id=1, source_target_pairs={{0,2},{1,3},{2,0},{3,1},{4,6},{5,7},{6,4},{7,5},{8,10},{9,11},{10,... | collective-permute-start | bytes 393224 | tf_op jit(solution)/shard_map/ppermute | solution.py:466
  7.1 0.0 copy-start.6
  7.1 0.7 %collective-permute-start.7 = (bf16[4,128,128]{2,1,0:T(8,128)(2,1)S(1)}, bf16[4,128,128]{2,1,0:T(8,128)(2,1)S(1)}, u32[]{:S(2)}, u32[]{:S(2)}) collective-permute-start(bf16[4,128,128]{2,1,0:T(8,128)(2,1)S(1)} %get-tuple-element.54), channel_id=1, source_target_pairs={{0,3},{1,2},{2,1},{3,0},{4,7},{5,6},{6,5},{7,4},{8,11},{9,10},{10,... | collective-permute-start | bytes 393224 | tf_op jit(solution)/shard_map/ppermute | solution.py:466
  7.7 0.5 %collective-permute-done.1.rest_2_ = bf16[4,128,128]{2,1,0:T(8,128)(2,1)S(1)} collective-permute-done((bf16[4,128,128]{2,1,0:T(8,128)(2,1)S(1)}, bf16[4,128,128]{2,1,0:T(8,128)(2,1)S(1)}, u32[]{:S(2)}, u32[]{:S(2)}) %collective-permute-start.1) | collective-permute-done | bytes 131104 | tf_op jit(solution)/shard_map/ppermute | solution.py:466
  8.3 0.0 collective-permute-start.8
  8.3 0.0 copy-done.3
  8.3 0.0 copy-done.5
  8.3 0.0 copy-done
  8.3 0.0 copy-done.1
  8.3 0.0 copy-done.2
  8.3 0.0 copy-done.4
  8.3 0.0 copy-done.6
  8.3 2.9 %shard_map.170 = (bf16[896,256]{1,0:T(8,128)(2,1)}, bf16[768,256]{1,0:T(8,128)(2,1)}, bf16[768,256]{1,0:T(8,128)(2,1)}, bf16[768,256]{1,0:T(8,128)(2,1)}, bf16[2...) custom-call(s32[8,8]{1,0:T(8,128)S(1)} %copy-done.4, s32[8,8]{1,0:T(8,128)S(1)} %copy-done.5, ...), custom_call_target="tpu_custom_call" | custom-call | flops 1000000000 | bytes 3000000 | tf_op jit(solution)/shard_map/pallas_call | solution.py:239
  11.2 0.0 collective-permute-done.rest_1_
  11.3 0.0 collective-permute-done.2.rest_3_
  11.3 1.1 %shard_map.173 = (bf16[4,128,128]{2,1,0:T(8,128)(2,1)S(1)}, bf16[4,128,128]{2,1,0:T(8,128)(2,1)S(1)}, bf16[4,128,128]{2,1,0:T(8,128)(2,1)S(1)}, bf16[4,128,128]{2,1,0:T(8,128)(2,1)S(1)}) custom-call(s32[8,128]{1,0:T(8,128)S(1)} %get-tuple-element.43.order, bf16[2,128,128]{2,1,0:T(8,128)(2,1)S(1)} %get-tuple-element.44.rest_0_, ...), custom_call_target="tpu_custom_call" | custom-call | flops 1000000000 | bytes 3000000 | tf_op jit(solution)/shard_map/pallas_call | solution.py:376
  12.4 2.0 %collective-permute-start.3 = (bf16[4,128,128]{2,1,0:T(8,128)(2,1)S(1)}, bf16[4,128,128]{2,1,0:T(8,128)(2,1)S(1)}, u32[]{:S(2)}, u32[]{:S(2)}) collective-permute-start(bf16[4,128,128]{2,1,0:T(8,128)(2,1)S(1)} %get-tuple-element.49), channel_id=1, source_target_pairs={{0,2},{1,3},{2,0},{3,1},{4,6},{5,7},{6,4},{7,5},{8,10},{9,11},{10,... | collective-permute-start | bytes 393224 | tf_op jit(solution)/shard_map/ppermute | solution.py:466
  14.4 2.3 %collective-permute-start.10 = (bf16[2,128,128]{2,1,0:T(8,128)(2,1)S(1)}, bf16[2,128,128]{2,1,0:T(8,128)(2,1)S(1)}, u32[]{:S(2)}, u32[]{:S(2)}) collective-permute-start(bf16[2,128,128]{2,1,0:T(8,128)(2,1)S(1)} %get-tuple-element.44.rest_0_), channel_id=1, source_target_pairs={{0,16},{4,20},{8,24},{12,28},{16,0},{20,4},{24,8},{28,12},{1,17},{... | collective-permute-start | bytes 196616 | tf_op jit(solution)/shard_map/ppermute | solution.py:478
  16.7 0.0 collective-permute-done.6.rest_1_
  16.7 0.7 %collective-permute-start.4 = (bf16[4,128,128]{2,1,0:T(8,128)(2,1)S(1)}, bf16[4,128,128]{2,1,0:T(8,128)(2,1)S(1)}, u32[]{:S(2)}, u32[]{:S(2)}) collective-permute-start(bf16[4,128,128]{2,1,0:T(8,128)(2,1)S(1)} %get-tuple-element.50), channel_id=1, source_target_pairs={{0,3},{1,2},{2,1},{3,0},{4,7},{5,6},{6,5},{7,4},{8,11},{9,10},{10,... | collective-permute-start | bytes 393224 | tf_op jit(solution)/shard_map/ppermute | solution.py:466
  17.4 0.0 collective-permute-done.7.rest_2_
  17.4 0.0 collective-permute-start.5
  17.4 0.0 collective-permute-done.8.rest_3_
  17.4 1.1 %shard_map.174 = (bf16[4,128,128]{2,1,0:T(8,128)(2,1)S(1)}, bf16[4,128,128]{2,1,0:T(8,128)(2,1)S(1)}, bf16[4,128,128]{2,1,0:T(8,128)(2,1)S(1)}, bf16[4,128,128]{2,1,0:T(8,128)(2,1)S(1)}) custom-call(s32[8,128]{1,0:T(8,128)S(1)} %get-tuple-element.43.order, bf16[4,128,128]{2,1,0:T(8,128)(2,1)S(1)} %get-tuple-element.52.rest_0_.refs_3_, ...), custom_call_target="tpu_custom_call" | custom-call | flops 1000000000 | bytes 3000000 | tf_op jit(solution)/shard_map/pallas_call | solution.py:376
  18.6 0.6 %collective-permute-start.9 = (bf16[4,128,128]{2,1,0:T(8,128)(2,1)S(1)}, bf16[4,128,128]{2,1,0:T(8,128)(2,1)S(1)}, u32[]{:S(2)}, u32[]{:S(2)}) collective-permute-start(bf16[4,128,128]{2,1,0:T(8,128)(2,1)S(1)} %get-tuple-element.57), channel_id=1, source_target_pairs={{0,1},{1,0},{2,3},{3,2},{4,5},{5,4},{6,7},{7,6},{8,9},{9,8},{10,11... | collective-permute-start | bytes 393224 | tf_op jit(solution)/shard_map/ppermute | solution.py:466
  19.1 0.0 collective-permute-done.10.refs_6_
  19.1 1.3 %collective-permute-start.11 = (bf16[4,128,128]{2,1,0:T(8,128)(2,1)S(1)}, bf16[4,128,128]{2,1,0:T(8,128)(2,1)S(1)}, u32[]{:S(2)}, u32[]{:S(2)}) collective-permute-start(bf16[4,128,128]{2,1,0:T(8,128)(2,1)S(1)} %get-tuple-element.68), channel_id=1, source_target_pairs={{0,2},{1,3},{2,0},{3,1},{4,6},{5,7},{6,4},{7,5},{8,10},{9,11},{10,... | collective-permute-start | bytes 393224 | tf_op jit(solution)/shard_map/ppermute | solution.py:466
  20.4 0.0 collective-permute-done.3.refs_0_
  20.4 2.5 %collective-permute-start.12 = (bf16[4,128,128]{2,1,0:T(8,128)(2,1)S(1)}, bf16[4,128,128]{2,1,0:T(8,128)(2,1)S(1)}, u32[]{:S(2)}, u32[]{:S(2)}) collective-permute-start(bf16[4,128,128]{2,1,0:T(8,128)(2,1)S(1)} %get-tuple-element.69), channel_id=1, source_target_pairs={{0,3},{1,2},{2,1},{3,0},{4,7},{5,6},{6,5},{7,4},{8,11},{9,10},{10,... | collective-permute-start | bytes 393224 | tf_op jit(solution)/shard_map/ppermute | solution.py:466
  23.0 2.7 %shard_map.175 = (bf16[896,256]{1,0:T(8,128)(2,1)}, bf16[768,256]{1,0:T(8,128)(2,1)}, bf16[768,256]{1,0:T(8,128)(2,1)}, bf16[768,256]{1,0:T(8,128)(2,1)}) custom-call(s32[8,8]{1,0:T(8,128)S(1)} %copy-done.4, s32[8,8]{1,0:T(8,128)S(1)} %copy-done.5, ...), custom_call_target="tpu_custom_call", output_to_operand_aliasing={{0}: (6, {}), {1}: (7, {}), {2}: (8, {}), {3}: (9, {})} | custom-call | flops 1000000000 | bytes 3000000 | tf_op jit(solution)/shard_map/pallas_call | solution.py:239
  25.7 0.0 collective-permute-done.4.refs_1_
  25.7 0.0 collective-permute-done.5.refs_2_
  25.7 0.0 collective-permute-done.9.refs_4_
  25.7 0.9 %shard_map.176 = (bf16[1,128,1024]{2,1,0:T(8,128)(2,1)}, bf16[1,128,1024]{2,1,0:T(8,128)(2,1)}, bf16[1,128,1024]{2,1,0:T(8,128)(2,1)}, bf16[1,128,1024]{2,1,0:T(8,128)(2,1)}, bf16[896,256]{1,0:T(8,128)(2,1)}) custom-call(bf16[4,128,128]{2,1,0:T(8,128)(2,1)S(1)} %collective-permute-done.3.refs_0_, ...), custom_call_target="tpu_custom_call", output_to_operand_aliasing={{4}: (7, {})} | custom-call | bytes 1000000 | tf_op jit(solution)/shard_map/pallas_call | solution.py:434
  26.6 0.0 collective-permute-done.11.refs_0_
  26.7 1.4 %collective-permute-done.12.refs_1_ = bf16[4,128,128]{2,1,0:T(8,128)(2,1)S(1)} collective-permute-done((bf16[4,128,128]{2,1,0:T(8,128)(2,1)S(1)}, bf16[4,128,128]{2,1,0:T(8,128)(2,1)S(1)}, u32[]{:S(2)}, u32[]{:S(2)}) %collective-permute-start.12) | collective-permute-done | bytes 131104 | tf_op jit(solution)/shard_map/ppermute | solution.py:466
  28.1 0.7 %shard_map.177 = (bf16[1,128,1024]{2,1,0:T(8,128)(2,1)}, bf16[1,128,1024]{2,1,0:T(8,128)(2,1)}, bf16[1,128,1024]{2,1,0:T(8,128)(2,1)}, bf16[1,128,1024]{2,1,0:T(8,128)(2,1)}) custom-call(bf16[4,128,128]{2,1,0:T(8,128)(2,1)S(1)} %collective-permute-done.11.refs_0_, ...), custom_call_target="tpu_custom_call", output_to_operand_aliasing={{0}: (2, {}), {1}: (3, {}), {2}: (4, {}), {3}: (5, {})} | custom-call | bytes 1000000 | tf_op jit(solution)/shard_map/pallas_call | solution.py:434
Async XLA Ops:
  0.6 7.6 %copy-start.3 = (bf16[768,256]{1,0:T(8,128)(2,1)S(1)}, bf16[768,256]{1,0:T(8,128)(2,1)}, u32[]{:S(2)}) copy-start(bf16[768,256]{1,0:T(8,128)(2,1)} %d_hbm.3) | copy-start | bytes 1179652
  0.6 7.6 %copy-start.5 = (s32[8,8]{1,0:T(8,128)S(1)}, s32[8,8]{1,0:T(8,128)}, u32[]{:S(2)}) copy-start(s32[8,8]{1,0:T(8,128)} %dests.3) | copy-start | bytes 772
  1.6 6.7 %collective-permute-start.1 = (bf16[4,128,128]{2,1,0:T(8,128)(2,1)S(1)}, bf16[4,128,128]{2,1,0:T(8,128)(2,1)S(1)}, u32[]{:S(2)}, u32[]{:S(2)}) collective-permute-start(bf16[4,128,128]{2,1,0:T(8,128)(2,1)S(1)} %get-tuple-element.46), channel_id=1, source_target_pairs={{0,3},{1,2},{2,1},{3,0},{4,7},{5,6},{6,5},{7,4},{8,11},{9,10},{10,... | collective-permute-start | bytes 393224 | tf_op jit(solution)/shard_map/ppermute | solution.py:466
  4.3 4.0 %copy-start = (bf16[768,256]{1,0:T(8,128)(2,1)S(1)}, bf16[768,256]{1,0:T(8,128)(2,1)}, u32[]{:S(2)}) copy-start(bf16[768,256]{1,0:T(8,128)(2,1)} %q_hbm.3) | copy-start | bytes 1179652
  4.3 4.0 %copy-start.1 = (bf16[768,256]{1,0:T(8,128)(2,1)S(1)}, bf16[768,256]{1,0:T(8,128)(2,1)}, u32[]{:S(2)}) copy-start(bf16[768,256]{1,0:T(8,128)(2,1)} %k_hbm.3) | copy-start | bytes 1179652
  4.3 4.0 %copy-start.2 = (bf16[768,256]{1,0:T(8,128)(2,1)S(1)}, bf16[768,256]{1,0:T(8,128)(2,1)}, u32[]{:S(2)}) copy-start(bf16[768,256]{1,0:T(8,128)(2,1)} %v_hbm.3) | copy-start | bytes 1179652
  4.3 7.0 %collective-permute-start = (bf16[4,128,128]{2,1,0:T(8,128)(2,1)S(1)}, bf16[4,128,128]{2,1,0:T(8,128)(2,1)S(1)}, u32[]{:S(2)}, u32[]{:S(2)}) collective-permute-start(bf16[4,128,128]{2,1,0:T(8,128)(2,1)S(1)} %get-tuple-element.45.rest_0_), channel_id=1, source_target_pairs={{0,2},{1,3},{2,0},{3,1},{4,6},{5,7},{6,4},{7,5},{8,10},{9,11},{10,... | collective-permute-start | bytes 393224 | tf_op jit(solution)/shard_map/ppermute | solution.py:466
  5.5 2.8 %copy-start.4 = (s32[8,8]{1,0:T(8,128)S(1)}, s32[8,8]{1,0:T(8,128)}, u32[]{:S(2)}) copy-start(s32[8,8]{1,0:T(8,128)} %lengths.3) | copy-start | bytes 772
  5.5 5.7 %collective-permute-start.2 = (bf16[4,128,128]{2,1,0:T(8,128)(2,1)S(1)}, bf16[4,128,128]{2,1,0:T(8,128)(2,1)S(1)}, u32[]{:S(2)}, u32[]{:S(2)}) collective-permute-start(bf16[4,128,128]{2,1,0:T(8,128)(2,1)S(1)} %get-tuple-element.47), channel_id=1, source_target_pairs={{0,1},{1,0},{2,3},{3,2},{4,5},{5,4},{6,7},{7,6},{8,9},{9,8},{10,11... | collective-permute-start | bytes 393224 | tf_op jit(solution)/shard_map/ppermute | solution.py:466
  6.0 10.7 %collective-permute-start.6 = (bf16[4,128,128]{2,1,0:T(8,128)(2,1)S(1)}, bf16[4,128,128]{2,1,0:T(8,128)(2,1)S(1)}, u32[]{:S(2)}, u32[]{:S(2)}) collective-permute-start(bf16[4,128,128]{2,1,0:T(8,128)(2,1)S(1)} %get-tuple-element.53), channel_id=1, source_target_pairs={{0,2},{1,3},{2,0},{3,1},{4,6},{5,7},{6,4},{7,5},{8,10},{9,11},{10,... | collective-permute-start | bytes 393224 | tf_op jit(solution)/shard_map/ppermute | solution.py:466
  7.1 1.3 %copy-start.6 = (s32[8]{0:T(128)S(1)}, s32[8]{0:T(128)}, u32[]{:S(2)}) copy-start(s32[8]{0:T(128)} %rest_0_.1) | copy-start | bytes 100
  7.1 10.3 %collective-permute-start.7 = (bf16[4,128,128]{2,1,0:T(8,128)(2,1)S(1)}, bf16[4,128,128]{2,1,0:T(8,128)(2,1)S(1)}, u32[]{:S(2)}, u32[]{:S(2)}) collective-permute-start(bf16[4,128,128]{2,1,0:T(8,128)(2,1)S(1)} %get-tuple-element.54), channel_id=1, source_target_pairs={{0,3},{1,2},{2,1},{3,0},{4,7},{5,6},{6,5},{7,4},{8,11},{9,10},{10,... | collective-permute-start | bytes 393224 | tf_op jit(solution)/shard_map/ppermute | solution.py:466
  8.3 9.2 %collective-permute-start.8 = (bf16[4,128,128]{2,1,0:T(8,128)(2,1)S(1)}, bf16[4,128,128]{2,1,0:T(8,128)(2,1)S(1)}, u32[]{:S(2)}, u32[]{:S(2)}) collective-permute-start(bf16[4,128,128]{2,1,0:T(8,128)(2,1)S(1)} %get-tuple-element.55), channel_id=1, source_target_pairs={{0,1},{1,0},{2,3},{3,2},{4,5},{5,4},{6,7},{7,6},{8,9},{9,8},{10,11... | collective-permute-start | bytes 393224 | tf_op jit(solution)/shard_map/ppermute | solution.py:466
  12.4 8.0 %collective-permute-start.3 = (bf16[4,128,128]{2,1,0:T(8,128)(2,1)S(1)}, bf16[4,128,128]{2,1,0:T(8,128)(2,1)S(1)}, u32[]{:S(2)}, u32[]{:S(2)}) collective-permute-start(bf16[4,128,128]{2,1,0:T(8,128)(2,1)S(1)} %get-tuple-element.49), channel_id=1, source_target_pairs={{0,2},{1,3},{2,0},{3,1},{4,6},{5,7},{6,4},{7,5},{8,10},{9,11},{10,... | collective-permute-start | bytes 393224 | tf_op jit(solution)/shard_map/ppermute | solution.py:466
  14.4 4.8 %collective-permute-start.10 = (bf16[2,128,128]{2,1,0:T(8,128)(2,1)S(1)}, bf16[2,128,128]{2,1,0:T(8,128)(2,1)S(1)}, u32[]{:S(2)}, u32[]{:S(2)}) collective-permute-start(bf16[2,128,128]{2,1,0:T(8,128)(2,1)S(1)} %get-tuple-element.44.rest_0_), channel_id=1, source_target_pairs={{0,16},{4,20},{8,24},{12,28},{16,0},{20,4},{24,8},{28,12},{1,17},{... | collective-permute-start | bytes 196616 | tf_op jit(solution)/shard_map/ppermute | solution.py:478
  16.7 9.0 %collective-permute-start.4 = (bf16[4,128,128]{2,1,0:T(8,128)(2,1)S(1)}, bf16[4,128,128]{2,1,0:T(8,128)(2,1)S(1)}, u32[]{:S(2)}, u32[]{:S(2)}) collective-permute-start(bf16[4,128,128]{2,1,0:T(8,128)(2,1)S(1)} %get-tuple-element.50), channel_id=1, source_target_pairs={{0,3},{1,2},{2,1},{3,0},{4,7},{5,6},{6,5},{7,4},{8,11},{9,10},{10,... | collective-permute-start | bytes 393224 | tf_op jit(solution)/shard_map/ppermute | solution.py:466
  17.4 8.3 %collective-permute-start.5 = (bf16[4,128,128]{2,1,0:T(8,128)(2,1)S(1)}, bf16[4,128,128]{2,1,0:T(8,128)(2,1)S(1)}, u32[]{:S(2)}, u32[]{:S(2)}) collective-permute-start(bf16[4,128,128]{2,1,0:T(8,128)(2,1)S(1)} %get-tuple-element.51), channel_id=1, source_target_pairs={{0,1},{1,0},{2,3},{3,2},{4,5},{5,4},{6,7},{7,6},{8,9},{9,8},{10,11... | collective-permute-start | bytes 393224 | tf_op jit(solution)/shard_map/ppermute | solution.py:466
  18.6 7.2 %collective-permute-start.9 = (bf16[4,128,128]{2,1,0:T(8,128)(2,1)S(1)}, bf16[4,128,128]{2,1,0:T(8,128)(2,1)S(1)}, u32[]{:S(2)}, u32[]{:S(2)}) collective-permute-start(bf16[4,128,128]{2,1,0:T(8,128)(2,1)S(1)} %get-tuple-element.57), channel_id=1, source_target_pairs={{0,1},{1,0},{2,3},{3,2},{4,5},{5,4},{6,7},{7,6},{8,9},{9,8},{10,11... | collective-permute-start | bytes 393224 | tf_op jit(solution)/shard_map/ppermute | solution.py:466
  19.1 7.5 %collective-permute-start.11 = (bf16[4,128,128]{2,1,0:T(8,128)(2,1)S(1)}, bf16[4,128,128]{2,1,0:T(8,128)(2,1)S(1)}, u32[]{:S(2)}, u32[]{:S(2)}) collective-permute-start(bf16[4,128,128]{2,1,0:T(8,128)(2,1)S(1)} %get-tuple-element.68), channel_id=1, source_target_pairs={{0,2},{1,3},{2,0},{3,1},{4,6},{5,7},{6,4},{7,5},{8,10},{9,11},{10,... | collective-permute-start | bytes 393224 | tf_op jit(solution)/shard_map/ppermute | solution.py:466
  20.4 7.7 %collective-permute-start.12 = (bf16[4,128,128]{2,1,0:T(8,128)(2,1)S(1)}, bf16[4,128,128]{2,1,0:T(8,128)(2,1)S(1)}, u32[]{:S(2)}, u32[]{:S(2)}) collective-permute-start(bf16[4,128,128]{2,1,0:T(8,128)(2,1)S(1)} %get-tuple-element.69), channel_id=1, source_target_pairs={{0,3},{1,2},{2,1},{3,0},{4,7},{5,6},{6,5},{7,4},{8,11},{9,10},{10,... | collective-permute-start | bytes 393224 | tf_op jit(solution)/shard_map/ppermute | solution.py:466

commit v3 on v2

--- a/solution.py
+++ b/solution.py
@@ -485,10 +485,9 @@
     whole = {(head, step): pieces[head][index] for head in range(heads_each) for index, step in enumerate(steps + [0])}
     final = [(heads_each - 1, step) for step in far]
     sooner = [key for key in whole if key not in final]
-    outs = join(sooner, ways, [whole[key] for key in sooner], None, q_long.shape, received, short[0])
-    out_short = outs[4]
-    outs = join(final, ways, [whole[key] for key in final], outs[:4], q_long.shape)
-    out_long, dq_long, dk_long, dv_long = outs
+    outs = join(sooner, ways, [whole[key] for key in sooner], None, q_long.shape)
+    outs = join(final, ways, [whole[key] for key in final], outs[:4], q_long.shape, received, short[0])
+    out_long, dq_long, dk_long, dv_long, out_short = outs
     dq_short, dk_short, dv_short = short[1:]
     return (out_short, dq_short, dk_short, dv_short, out_long, dq_long, dk_long, dv_long)
 

time: 29 us -> 30.2 us (1.041)
  the two profiles are of different devices: /device:TPU:1 before, /device:TPU:0 now
where the time goes in v3:
time: 30.2 us; the launch traced here: 30 us
  starting transfers between devices  15.4 us (51%)
  Pallas kernels  11.5 us (38%)
  waiting for transfers between devices  2.28 us (8%)
  between operations  0.76 us (3%)
    ppermute x12, starting transfers between devices, swap(): return lax.ppermute(value, 'ctx', [(i, i ^ step) for i in range(ways)])  11.9 us
    pallas_call x2, Pallas kernels, short_attention(): pl.pallas_call(functools.partial(short_kernel, head, heads), in_specs=[sm...  5.65 us
    ppermute x1, starting transfers between devices, shards(): lax.ppermute(tail, 'dp', [(i, (i + ranks // 2) % ranks) for i in range(ra...  3.46 us
    pallas_call x2, Pallas kernels, long_attention(): pl.pallas_call(functools.partial(long_kernel, ways, len(linked)), in_spec...  2.25 us
    ppermute x12, waiting for transfers between devices, swap(): return lax.ppermute(value, 'ctx', [(i, i ^ step) for i in range(ways)])  2.16 us
    pallas_call x2, Pallas kernels, pack(): pl.pallas_call(functools.partial(pack_kernel, parts, ways, len(after)), i...  2.04 us
    pallas_call x2, Pallas kernels, join(): pl.pallas_call(functools.partial(join_kernel, parts, ways, len(old), with...  1.6 us
  transfers between devices with their start and end apart: 13, of which 4 were waited for; matrix products, arithmetic and copies ran while one was open for 0% of the time, Pallas kernels for 33%

profile of v3, /device:TPU:0, one launch (start us, length us, event | category | flops | bytes accessed | tf_op | source)
XLA Modules:
  0.0 30.0 jit_solution(6104579290584967938)
XLA Ops:
  0.6 0.0 copy-start.3
  0.6 0.0 copy-start.5
  0.7 0.9 %shard_map.171 = (bf16[4,128,128]{2,1,0:T(8,128)(2,1)S(1)}, bf16[4,128,128]{2,1,0:T(8,128)(2,1)S(1)}) custom-call(bf16[1,128,1024]{2,1,0:T(8,128)(2,1)} %q_ref.3, bf16[1,128,1024]{2,1,0:T(8,128)(2,1)} %k_ref.3, bf16[1,128,1024]{2,1,0:T(8,128)(2,1)} %v_ref.3, bf16[1,128,1024]{2,1,0:T(8,128)(2,1)} %d_ref.3), custom_call_target="tpu_custom_call" | custom-call | bytes 2000000 | tf_op jit(solution)/shard_map/pallas_call | solution.py:290
  1.6 2.5 %collective-permute-start.1 = (bf16[4,128,128]{2,1,0:T(8,128)(2,1)S(1)}, bf16[4,128,128]{2,1,0:T(8,128)(2,1)S(1)}, u32[]{:S(2)}, u32[]{:S(2)}) collective-permute-start(bf16[4,128,128]{2,1,0:T(8,128)(2,1)S(1)} %get-tuple-element.46), channel_id=1, source_target_pairs={{0,3},{1,2},{2,1},{3,0},{4,7},{5,6},{6,5},{7,4},{8,11},{9,10},{10,... | collective-permute-start | bytes 393224 | tf_op jit(solution)/shard_map/ppermute | solution.py:466
  4.1 0.0 copy-start
  4.1 0.0 copy-start.1
  4.1 0.0 copy-start.2
  4.1 0.7 %collective-permute-start = (bf16[4,128,128]{2,1,0:T(8,128)(2,1)S(1)}, bf16[4,128,128]{2,1,0:T(8,128)(2,1)S(1)}, u32[]{:S(2)}, u32[]{:S(2)}) collective-permute-start(bf16[4,128,128]{2,1,0:T(8,128)(2,1)S(1)} %get-tuple-element.45.rest_0_), channel_id=1, source_target_pairs={{0,2},{1,3},{2,0},{3,1},{4,6},{5,7},{6,4},{7,5},{8,10},{9,11},{10,... | collective-permute-start | bytes 393224 | tf_op jit(solution)/shard_map/ppermute | solution.py:466
  4.8 1.1 %shard_map.172 = (bf16[4,128,128]{2,1,0:T(8,128)(2,1)S(1)}, bf16[4,128,128]{2,1,0:T(8,128)(2,1)S(1)}, bf16[4,128,128]{2,1,0:T(8,128)(2,1)S(1)}, bf16[4,128,128]{...) custom-call(bf16[1,128,1024]{2,1,0:T(8,128)(2,1)} %q_ref.3, ...), custom_call_target="tpu_custom_call" | custom-call | bytes 2000000 | tf_op jit(solution)/shard_map/pallas_call | solution.py:290
  5.9 0.0 copy-start.4
  5.9 0.2 collective-permute-start.2
  6.1 1.6 %collective-permute-start.3 = (bf16[4,128,128]{2,1,0:T(8,128)(2,1)S(1)}, bf16[4,128,128]{2,1,0:T(8,128)(2,1)S(1)}, u32[]{:S(2)}, u32[]{:S(2)}) collective-permute-start(bf16[4,128,128]{2,1,0:T(8,128)(2,1)S(1)} %get-tuple-element.50), channel_id=1, source_target_pairs={{0,2},{1,3},{2,0},{3,1},{4,6},{5,7},{6,4},{7,5},{8,10},{9,11},{10,... | collective-permute-start | bytes 393224 | tf_op jit(solution)/shard_map/ppermute | solution.py:466
  7.7 0.0 copy-start.6
  7.7 0.1 collective-permute-start.4
  7.8 0.2 collective-permute-done.1.rest_2_
  8.0 0.8 %collective-permute-start.5 = (bf16[4,128,128]{2,1,0:T(8,128)(2,1)S(1)}, bf16[4,128,128]{2,1,0:T(8,128)(2,1)S(1)}, u32[]{:S(2)}, u32[]{:S(2)}) collective-permute-start(bf16[4,128,128]{2,1,0:T(8,128)(2,1)S(1)} %get-tuple-element.52), channel_id=1, source_target_pairs={{0,1},{1,0},{2,3},{3,2},{4,5},{5,4},{6,7},{7,6},{8,9},{9,8},{10,11... | collective-permute-start | bytes 393224 | tf_op jit(solution)/shard_map/ppermute | solution.py:466
  8.8 0.0 copy-done.3
  8.8 0.0 copy-done.5
  8.8 0.0 copy-done
  8.8 0.0 copy-done.1
  8.8 0.0 copy-done.2
  8.8 0.0 copy-done.4
  8.8 0.0 copy-done.6
  8.8 2.9 %shard_map.170 = (bf16[896,256]{1,0:T(8,128)(2,1)}, bf16[768,256]{1,0:T(8,128)(2,1)}, bf16[768,256]{1,0:T(8,128)(2,1)}, bf16[768,256]{1,0:T(8,128)(2,1)}, bf16[2...) custom-call(s32[8,8]{1,0:T(8,128)S(1)} %copy-done.4, s32[8,8]{1,0:T(8,128)S(1)} %copy-done.5, ...), custom_call_target="tpu_custom_call" | custom-call | flops 1000000000 | bytes 3000000 | tf_op jit(solution)/shard_map/pallas_call | solution.py:239
  11.7 0.0 collective-permute-done.rest_1_
  11.7 0.0 collective-permute-done.2.rest_3_
  11.7 1.1 %shard_map.173 = (bf16[4,128,128]{2,1,0:T(8,128)(2,1)S(1)}, bf16[4,128,128]{2,1,0:T(8,128)(2,1)S(1)}, bf16[4,128,128]{2,1,0:T(8,128)(2,1)S(1)}, bf16[4,128,128]{2,1,0:T(8,128)(2,1)S(1)}) custom-call(s32[8,128]{1,0:T(8,128)S(1)} %get-tuple-element.43.order, bf16[2,128,128]{2,1,0:T(8,128)(2,1)S(1)} %get-tuple-element.44.rest_0_, ...), custom_call_target="tpu_custom_call" | custom-call | flops 1000000000 | bytes 3000000 | tf_op jit(solution)/shard_map/pallas_call | solution.py:376
  12.9 1.9 %collective-permute-start.9 = (bf16[4,128,128]{2,1,0:T(8,128)(2,1)S(1)}, bf16[4,128,128]{2,1,0:T(8,128)(2,1)S(1)}, u32[]{:S(2)}, u32[]{:S(2)}) collective-permute-start(bf16[4,128,128]{2,1,0:T(8,128)(2,1)S(1)} %get-tuple-element.56), channel_id=1, source_target_pairs={{0,2},{1,3},{2,0},{3,1},{4,6},{5,7},{6,4},{7,5},{8,10},{9,11},{10,... | collective-permute-start | bytes 393224 | tf_op jit(solution)/shard_map/ppermute | solution.py:466
  14.7 0.1 collective-permute-start.10
  14.8 0.0 collective-permute-done.3.rest_1_
  14.8 0.3 collective-permute-start.11
  15.1 1.3 %collective-permute-done.4.rest_2_ = bf16[4,128,128]{2,1,0:T(8,128)(2,1)S(1)} collective-permute-done((bf16[4,128,128]{2,1,0:T(8,128)(2,1)S(1)}, bf16[4,128,128]{2,1,0:T(8,128)(2,1)S(1)}, u32[]{:S(2)}, u32[]{:S(2)}) %collective-permute-start.4) | collective-permute-done | bytes 131104 | tf_op jit(solution)/shard_map/ppermute | solution.py:466
  16.4 0.0 collective-permute-done.5.rest_3_
  16.4 1.1 %shard_map.174 = (bf16[4,128,128]{2,1,0:T(8,128)(2,1)S(1)}, bf16[4,128,128]{2,1,0:T(8,128)(2,1)S(1)}, bf16[4,128,128]{2,1,0:T(8,128)(2,1)S(1)}, bf16[4,128,128]{2,1,0:T(8,128)(2,1)S(1)}) custom-call(s32[8,128]{1,0:T(8,128)S(1)} %get-tuple-element.43.order, bf16[4,128,128]{2,1,0:T(8,128)(2,1)S(1)} %get-tuple-element.49.rest_0_.refs_3_, ...), custom_call_target="tpu_custom_call" | custom-call | flops 1000000000 | bytes 3000000 | tf_op jit(solution)/shard_map/pallas_call | solution.py:376
  17.5 0.7 %collective-permute-start.12 = (bf16[4,128,128]{2,1,0:T(8,128)(2,1)S(1)}, bf16[4,128,128]{2,1,0:T(8,128)(2,1)S(1)}, u32[]{:S(2)}, u32[]{:S(2)}) collective-permute-start(bf16[4,128,128]{2,1,0:T(8,128)(2,1)S(1)} %get-tuple-element.59), channel_id=1, source_target_pairs={{0,1},{1,0},{2,3},{3,2},{4,5},{5,4},{6,7},{7,6},{8,9},{9,8},{10,11... | collective-permute-start | bytes 393224 | tf_op jit(solution)/shard_map/ppermute | solution.py:466
  18.2 2.0 %collective-permute-start.6 = (bf16[4,128,128]{2,1,0:T(8,128)(2,1)S(1)}, bf16[4,128,128]{2,1,0:T(8,128)(2,1)S(1)}, u32[]{:S(2)}, u32[]{:S(2)}) collective-permute-start(bf16[4,128,128]{2,1,0:T(8,128)(2,1)S(1)} %get-tuple-element.54), channel_id=1, source_target_pairs={{0,2},{1,3},{2,0},{3,1},{4,6},{5,7},{6,4},{7,5},{8,10},{9,11},{10,... | collective-permute-start | bytes 393224 | tf_op jit(solution)/shard_map/ppermute | solution.py:466
  20.2 0.0 collective-permute-done.9.refs_0_
  20.2 1.2 %collective-permute-start.7 = (bf16[4,128,128]{2,1,0:T(8,128)(2,1)S(1)}, bf16[4,128,128]{2,1,0:T(8,128)(2,1)S(1)}, u32[]{:S(2)}, u32[]{:S(2)}) collective-permute-start(bf16[4,128,128]{2,1,0:T(8,128)(2,1)S(1)} %get-tuple-element.55), channel_id=1, source_target_pairs={{0,3},{1,2},{2,1},{3,0},{4,7},{5,6},{6,5},{7,4},{8,11},{9,10},{10,... | collective-permute-start | bytes 393224 | tf_op jit(solution)/shard_map/ppermute | solution.py:466
  21.4 0.6 %collective-permute-done.10.refs_1_ = bf16[4,128,128]{2,1,0:T(8,128)(2,1)S(1)} collective-permute-done((bf16[4,128,128]{2,1,0:T(8,128)(2,1)S(1)}, bf16[4,128,128]{2,1,0:T(8,128)(2,1)S(1)}, u32[]{:S(2)}, u32[]{:S(2)}) %collective-permute-start.10) | collective-permute-done | bytes 131104 | tf_op jit(solution)/shard_map/ppermute | solution.py:466
  22.0 3.5 %collective-permute-start.8 = (bf16[2,128,128]{2,1,0:T(8,128)(2,1)S(1)}, bf16[2,128,128]{2,1,0:T(8,128)(2,1)S(1)}, u32[]{:S(2)}, u32[]{:S(2)}) collective-permute-start(bf16[2,128,128]{2,1,0:T(8,128)(2,1)S(1)} %get-tuple-element.44.rest_0_), channel_id=1, source_target_pairs={{0,16},{4,20},{8,24},{12,28},{16,0},{20,4},{24,8},{28,12},{1,17},{... | collective-permute-start | bytes 196616 | tf_op jit(solution)/shard_map/ppermute | solution.py:478
  25.5 2.7 %shard_map.176 = (bf16[896,256]{1,0:T(8,128)(2,1)}, bf16[768,256]{1,0:T(8,128)(2,1)}, bf16[768,256]{1,0:T(8,128)(2,1)}, bf16[768,256]{1,0:T(8,128)(2,1)}) custom-call(s32[8,8]{1,0:T(8,128)S(1)} %copy-done.4, s32[8,8]{1,0:T(8,128)S(1)} %copy-done.5, ...), custom_call_target="tpu_custom_call", output_to_operand_aliasing={{0}: (6, {}), {1}: (7, {}), {2}: (8, {}), {3}: (9, {})} | custom-call | flops 1000000000 | bytes 3000000 | tf_op jit(solution)/shard_map/pallas_call | solution.py:239
  28.2 0.0 collective-permute-done.11.refs_2_
  28.2 0.0 collective-permute-done.12.refs_4_
  28.3 0.9 %shard_map.175 = (bf16[1,128,1024]{2,1,0:T(8,128)(2,1)}, bf16[1,128,1024]{2,1,0:T(8,128)(2,1)}, bf16[1,128,1024]{2,1,0:T(8,128)(2,1)}, bf16[1,128,1024]{2,1,0:T(8,128)(2,1)}) custom-call(bf16[4,128,128]{2,1,0:T(8,128)(2,1)S(1)} %collective-permute-done.9.refs_0_, bf16[4,128,128]{2,1,0:T(8,128)(2,1)S(1)} %collective-permute-done.10.refs_1_, ...), custom_call_target="tpu_custom_call" | custom-call | bytes 1000000 | tf_op jit(solution)/shard_map/pallas_call | solution.py:434
  29.1 0.1 collective-permute-done.8.refs_2_
  29.3 0.0 collective-permute-done.6.refs_0_
  29.3 0.0 collective-permute-done.7.refs_1_
  29.3 0.7 %shard_map.177 = (bf16[1,128,1024]{2,1,0:T(8,128)(2,1)}, bf16[1,128,1024]{2,1,0:T(8,128)(2,1)}, bf16[1,128,1024]{2,1,0:T(8,128)(2,1)}, bf16[1,128,1024]{2,1,0:T(8,128)(2,1)}, bf16[896,256]{1,0:T(8,128)(2,1)}) custom-call(bf16[4,128,128]{2,1,0:T(8,128)(2,1)S(1)} %collective-permute-done, ...), custom_call_target="tpu_custom_call", output_to_operand_aliasing={{0}: (3, {}), {1}: (4, {}), {2}: (5, {}), {3}: (6, {}), {4}... | custom-call | bytes 1000000 | tf_op jit(solution)/shard_map/pallas_call | solution.py:434
Async XLA Ops:
  0.6 8.1 %copy-start.3 = (bf16[768,256]{1,0:T(8,128)(2,1)S(1)}, bf16[768,256]{1,0:T(8,128)(2,1)}, u32[]{:S(2)}) copy-start(bf16[768,256]{1,0:T(8,128)(2,1)} %d_hbm.3) | copy-start | bytes 1179652
  0.6 8.1 %copy-start.5 = (s32[8,8]{1,0:T(8,128)S(1)}, s32[8,8]{1,0:T(8,128)}, u32[]{:S(2)}) copy-start(s32[8,8]{1,0:T(8,128)} %dests.3) | copy-start | bytes 772
  1.6 6.4 %collective-permute-start.1 = (bf16[4,128,128]{2,1,0:T(8,128)(2,1)S(1)}, bf16[4,128,128]{2,1,0:T(8,128)(2,1)S(1)}, u32[]{:S(2)}, u32[]{:S(2)}) collective-permute-start(bf16[4,128,128]{2,1,0:T(8,128)(2,1)S(1)} %get-tuple-element.46), channel_id=1, source_target_pairs={{0,3},{1,2},{2,1},{3,0},{4,7},{5,6},{6,5},{7,4},{8,11},{9,10},{10,... | collective-permute-start | bytes 393224 | tf_op jit(solution)/shard_map/ppermute | solution.py:466
  4.1 4.7 %copy-start = (bf16[768,256]{1,0:T(8,128)(2,1)S(1)}, bf16[768,256]{1,0:T(8,128)(2,1)}, u32[]{:S(2)}) copy-start(bf16[768,256]{1,0:T(8,128)(2,1)} %q_hbm.3) | copy-start | bytes 1179652
  4.1 4.7 %copy-start.1 = (bf16[768,256]{1,0:T(8,128)(2,1)S(1)}, bf16[768,256]{1,0:T(8,128)(2,1)}, u32[]{:S(2)}) copy-start(bf16[768,256]{1,0:T(8,128)(2,1)} %k_hbm.3) | copy-start | bytes 1179652
  4.1 4.7 %copy-start.2 = (bf16[768,256]{1,0:T(8,128)(2,1)S(1)}, bf16[768,256]{1,0:T(8,128)(2,1)}, u32[]{:S(2)}) copy-start(bf16[768,256]{1,0:T(8,128)(2,1)} %v_hbm.3) | copy-start | bytes 1179652
  4.1 7.6 %collective-permute-start = (bf16[4,128,128]{2,1,0:T(8,128)(2,1)S(1)}, bf16[4,128,128]{2,1,0:T(8,128)(2,1)S(1)}, u32[]{:S(2)}, u32[]{:S(2)}) collective-permute-start(bf16[4,128,128]{2,1,0:T(8,128)(2,1)S(1)} %get-tuple-element.45.rest_0_), channel_id=1, source_target_pairs={{0,2},{1,3},{2,0},{3,1},{4,6},{5,7},{6,4},{7,5},{8,10},{9,11},{10,... | collective-permute-start | bytes 393224 | tf_op jit(solution)/shard_map/ppermute | solution.py:466
  5.9 2.9 %copy-start.4 = (s32[8,8]{1,0:T(8,128)S(1)}, s32[8,8]{1,0:T(8,128)}, u32[]{:S(2)}) copy-start(s32[8,8]{1,0:T(8,128)} %lengths.3) | copy-start | bytes 772
  5.9 5.8 %collective-permute-start.2 = (bf16[4,128,128]{2,1,0:T(8,128)(2,1)S(1)}, bf16[4,128,128]{2,1,0:T(8,128)(2,1)S(1)}, u32[]{:S(2)}, u32[]{:S(2)}) collective-permute-start(bf16[4,128,128]{2,1,0:T(8,128)(2,1)S(1)} %get-tuple-element.47), channel_id=1, source_target_pairs={{0,1},{1,0},{2,3},{3,2},{4,5},{5,4},{6,7},{7,6},{8,9},{9,8},{10,11... | collective-permute-start | bytes 393224 | tf_op jit(solution)/shard_map/ppermute | solution.py:466
  6.1 8.7 %collective-permute-start.3 = (bf16[4,128,128]{2,1,0:T(8,128)(2,1)S(1)}, bf16[4,128,128]{2,1,0:T(8,128)(2,1)S(1)}, u32[]{:S(2)}, u32[]{:S(2)}) collective-permute-start(bf16[4,128,128]{2,1,0:T(8,128)(2,1)S(1)} %get-tuple-element.50), channel_id=1, source_target_pairs={{0,2},{1,3},{2,0},{3,1},{4,6},{5,7},{6,4},{7,5},{8,10},{9,11},{10,... | collective-permute-start | bytes 393224 | tf_op jit(solution)/shard_map/ppermute | solution.py:466
  7.7 1.1 %copy-start.6 = (s32[8]{0:T(128)S(1)}, s32[8]{0:T(128)}, u32[]{:S(2)}) copy-start(s32[8]{0:T(128)} %rest_0_.1) | copy-start | bytes 100
  7.7 8.7 %collective-permute-start.4 = (bf16[4,128,128]{2,1,0:T(8,128)(2,1)S(1)}, bf16[4,128,128]{2,1,0:T(8,128)(2,1)S(1)}, u32[]{:S(2)}, u32[]{:S(2)}) collective-permute-start(bf16[4,128,128]{2,1,0:T(8,128)(2,1)S(1)} %get-tuple-element.51), channel_id=1, source_target_pairs={{0,3},{1,2},{2,1},{3,0},{4,7},{5,6},{6,5},{7,4},{8,11},{9,10},{10,... | collective-permute-start | bytes 393224 | tf_op jit(solution)/shard_map/ppermute | solution.py:466
  8.0 8.4 %collective-permute-start.5 = (bf16[4,128,128]{2,1,0:T(8,128)(2,1)S(1)}, bf16[4,128,128]{2,1,0:T(8,128)(2,1)S(1)}, u32[]{:S(2)}, u32[]{:S(2)}) collective-permute-start(bf16[4,128,128]{2,1,0:T(8,128)(2,1)S(1)} %get-tuple-element.52), channel_id=1, source_target_pairs={{0,1},{1,0},{2,3},{3,2},{4,5},{5,4},{6,7},{7,6},{8,9},{9,8},{10,11... | collective-permute-start | bytes 393224 | tf_op jit(solution)/shard_map/ppermute | solution.py:466
  12.9 7.3 %collective-permute-start.9 = (bf16[4,128,128]{2,1,0:T(8,128)(2,1)S(1)}, bf16[4,128,128]{2,1,0:T(8,128)(2,1)S(1)}, u32[]{:S(2)}, u32[]{:S(2)}) collective-permute-start(bf16[4,128,128]{2,1,0:T(8,128)(2,1)S(1)} %get-tuple-element.56), channel_id=1, source_target_pairs={{0,2},{1,3},{2,0},{3,1},{4,6},{5,7},{6,4},{7,5},{8,10},{9,11},{10,... | collective-permute-start | bytes 393224 | tf_op jit(solution)/shard_map/ppermute | solution.py:466
  14.7 7.3 %collective-permute-start.10 = (bf16[4,128,128]{2,1,0:T(8,128)(2,1)S(1)}, bf16[4,128,128]{2,1,0:T(8,128)(2,1)S(1)}, u32[]{:S(2)}, u32[]{:S(2)}) collective-permute-start(bf16[4,128,128]{2,1,0:T(8,128)(2,1)S(1)} %get-tuple-element.57), channel_id=1, source_target_pairs={{0,3},{1,2},{2,1},{3,0},{4,7},{5,6},{6,5},{7,4},{8,11},{9,10},{10,... | collective-permute-start | bytes 393224 | tf_op jit(solution)/shard_map/ppermute | solution.py:466
  14.8 13.4 %collective-permute-start.11 = (bf16[4,128,128]{2,1,0:T(8,128)(2,1)S(1)}, bf16[4,128,128]{2,1,0:T(8,128)(2,1)S(1)}, u32[]{:S(2)}, u32[]{:S(2)}) collective-permute-start(bf16[4,128,128]{2,1,0:T(8,128)(2,1)S(1)} %get-tuple-element.58), channel_id=1, source_target_pairs={{0,1},{1,0},{2,3},{3,2},{4,5},{5,4},{6,7},{7,6},{8,9},{9,8},{10,11... | collective-permute-start | bytes 393224 | tf_op jit(solution)/shard_map/ppermute | solution.py:466
  17.5 10.7 %collective-permute-start.12 = (bf16[4,128,128]{2,1,0:T(8,128)(2,1)S(1)}, bf16[4,128,128]{2,1,0:T(8,128)(2,1)S(1)}, u32[]{:S(2)}, u32[]{:S(2)}) collective-permute-start(bf16[4,128,128]{2,1,0:T(8,128)(2,1)S(1)} %get-tuple-element.59), channel_id=1, source_target_pairs={{0,1},{1,0},{2,3},{3,2},{4,5},{5,4},{6,7},{7,6},{8,9},{9,8},{10,11... | collective-permute-start | bytes 393224 | tf_op jit(solution)/shard_map/ppermute | solution.py:466
  18.2 11.1 %collective-permute-start.6 = (bf16[4,128,128]{2,1,0:T(8,128)(2,1)S(1)}, bf16[4,128,128]{2,1,0:T(8,128)(2,1)S(1)}, u32[]{:S(2)}, u32[]{:S(2)}) collective-permute-start(bf16[4,128,128]{2,1,0:T(8,128)(2,1)S(1)} %get-tuple-element.54), channel_id=1, source_target_pairs={{0,2},{1,3},{2,0},{3,1},{4,6},{5,7},{6,4},{7,5},{8,10},{9,11},{10,... | collective-permute-start | bytes 393224 | tf_op jit(solution)/shard_map/ppermute | solution.py:466
  20.2 9.1 %collective-permute-start.7 = (bf16[4,128,128]{2,1,0:T(8,128)(2,1)S(1)}, bf16[4,128,128]{2,1,0:T(8,128)(2,1)S(1)}, u32[]{:S(2)}, u32[]{:S(2)}) collective-permute-start(bf16[4,128,128]{2,1,0:T(8,128)(2,1)S(1)} %get-tuple-element.55), channel_id=1, source_target_pairs={{0,3},{1,2},{2,1},{3,0},{4,7},{5,6},{6,5},{7,4},{8,11},{9,10},{10,... | collective-permute-start | bytes 393224 | tf_op jit(solution)/shard_map/ppermute | solution.py:466
  22.0 7.2 %collective-permute-start.8 = (bf16[2,128,128]{2,1,0:T(8,128)(2,1)S(1)}, bf16[2,128,128]{2,1,0:T(8,128)(2,1)S(1)}, u32[]{:S(2)}, u32[]{:S(2)}) collective-permute-start(bf16[2,128,128]{2,1,0:T(8,128)(2,1)S(1)} %get-tuple-element.44.rest_0_), channel_id=1, source_target_pairs={{0,16},{4,20},{8,24},{12,28},{16,0},{20,4},{24,8},{28,12},{1,17},{... | collective-permute-start | bytes 196616 | tf_op jit(solution)/shard_map/ppermute | solution.py:478

commit v4 on v3

--- a/solution.py
+++ b/solution.py
@@ -27,10 +27,15 @@
     return dot_rows(keys, queries), dot_rows(values, douts)
 
 
-def softmax_stage(scores, dprobs, tile, columns, mask_tile, scale):
+def softmax_stage(scores, dprobs, values_t, douts_t, tile, columns, mask_tile, scale):
     key_tiles = scores.shape[0] // tile
+    zero = jnp.zeros((tile, tile), jnp.bfloat16)
+
+    def column(tiles, first, last):
+        return jnp.concatenate([zero] * first + tiles + [zero] * (key_tiles - last), axis=0)
+
+    probs = []
     weight_cols = []
-    grad_cols = []
     for b, (first, last) in enumerate(columns):
         lanes = slice(b * tile, (b + 1) * tile)
         s_tiles = []
@@ -44,22 +49,25 @@
         total = sum(jnp.sum(e, axis=0, keepdims=True) for e in e_tiles)
         inverse = 1.0 / total
         p_tiles = [e * inverse for e in e_tiles]
-        d_tiles = [dprobs[j * tile : (j + 1) * tile, lanes] for j in range(first, last)]
-        delta = sum(jnp.sum(p * d, axis=0, keepdims=True) for p, d in zip(p_tiles, d_tiles))
-        w_tiles = [p.astype(jnp.bfloat16) for p in p_tiles]
-        g_tiles = [(p * (d - delta)).astype(jnp.bfloat16) for p, d in zip(p_tiles, d_tiles)]
-        zero = jnp.zeros((tile, tile), jnp.bfloat16)
-        before = [zero] * first
-        after = [zero] * (key_tiles - last)
-        weight_cols.append(jnp.concatenate(before + w_tiles + after, axis=0))
-        grad_cols.append(jnp.concatenate(before + g_tiles + after, axis=0))
-    return jnp.concatenate(weight_cols, axis=1), jnp.concatenate(grad_cols, axis=1)
-
-
-def product_stage(weights, grads, queries, douts, keys_t, values_t, scale):
-    attended = dot(values_t, weights).astype(jnp.bfloat16).T
+        probs.append(p_tiles)
+        weight_cols.append(column([p.astype(jnp.bfloat16) for p in p_tiles], first, last))
+    weights = jnp.concatenate(weight_cols, axis=1)
+    attended_t = dot(values_t, weights).astype(jnp.bfloat16)
+    delta = jnp.sum(attended_t.astype(jnp.float32) * douts_t.astype(jnp.float32), axis=0, keepdims=True)
+    grad_cols = []
+    for b, (first, last) in enumerate(columns):
+        lanes = slice(b * tile, (b + 1) * tile)
+        g_tiles = [
+            (p * (dprobs[j * tile : (j + 1) * tile, lanes] - delta[:, lanes])).astype(jnp.bfloat16)
+            for j, p in zip(range(first, last), probs[b])
+        ]
+        grad_cols.append(column(g_tiles, first, last))
+    return weights, jnp.concatenate(grad_cols, axis=1), attended_t
+
+
+def product_stage(weights, grads, attended_t, queries, douts, keys_t, scale):
     grad_q = (dot(keys_t, grads) * scale).astype(jnp.bfloat16).T
-    return attended, grad_q, dot(grads, queries), dot(weights, douts)
+    return attended_t.T, grad_q, dot(grads, queries), dot(weights, douts)
 
 
 def staged(blocks, scores_of, softmax_of, products_of, ahead=1):
@@ -137,6 +145,7 @@
     q_ref, k_ref, v_ref, d_ref = [held.at[slot] for slot in range(4)]
     keys_t = k_ref[...].T
     values_t = v_ref[...].T
+    douts_t = d_ref[...].T
     blocks = tokens // span
     pending = {}
 
@@ -168,19 +177,22 @@
             return jnp.where(allowed, s, NEG)
 
         columns = [(max(0, offset + b - 2), offset + b + 1) for b in range(2)]
-        return softmax_stage(scores, dprobs, tile, columns, mask_tile, scale)
-
-    def products_of(block, weights, grads):
+        keys = slice(key_low(block), low + span)
+        return softmax_stage(
+            scores, dprobs, values_t[:, keys], douts_t[:, low : low + span], tile, columns, mask_tile, scale
+        )
+
+    def products_of(block, weights, grads, attended_t):
         low = block * span
         high = low + span
         keys = slice(key_low(block), high)
         attended, grad_q, grad_k, grad_v = product_stage(
             weights,
             grads,
+            attended_t,
             q_ref[low:high, :],
             d_ref[low:high, :],
             keys_t[:, keys],
-            values_t[:, keys],
             scale,
         )
         made[1, low:high, :] = grad_q
@@ -327,6 +339,7 @@
     blocks = total // span
     keys_t = held[1].T
     values_t = held[2].T
+    douts_t = held[3].T
     sum_k = [None] * blocks
     sum_v = [None] * blocks
 
@@ -341,12 +354,15 @@
             return causal(s, tile) if j == first + b else s
 
         columns = [(0, first + b + 1) for b in range(span // tile)]
-        return softmax_stage(scores, dprobs, tile, columns, mask_tile, scale)
-
-    def products_of(block, weights, grads):
+        low, high = block * span, (block + 1) * span
+        return softmax_stage(
+            scores, dprobs, values_t[:, :high], douts_t[:, low:high], tile, columns, mask_tile, scale
+        )
+
+    def products_of(block, weights, grads, attended_t):
         low, high = block * span, (block + 1) * span
         attended, grad_q, grad_k, grad_v = product_stage(
-            weights, grads, held[0, low:high, :], held[3, low:high, :], keys_t[:, :high], values_t[:, :high], scale
+            weights, grads, attended_t, held[0, low:high, :], held[3, low:high, :], keys_t[:, :high], scale
         )
         made[0, low:high, :] = attended
         made[1, low:high, :] = grad_q

time: 30.2 us -> 30.4 us (level)
  Pallas kernels: 11.5 us -> 12.4 us
  waiting for transfers between devices: 2.28 us -> 1.77 us
    pallas_call x2, Pallas kernels: 5.65 us -> 6.12 us  [short_attention(): pl.pallas_call(functools.partial(short_kernel, head, heads), in_specs=[sm...]
    pallas_call x2, Pallas kernels: 2.25 us -> 2.64 us  [long_attention(): pl.pallas_call(functools.partial(long_kernel, ways, len(linked)), in_spec...]
    ppermute x12, waiting for transfers between devices: 2.16 us -> 1.77 us  [swap(): return lax.ppermute(value, 'ctx', [(i, i ^ step) for i in range(ways)])]
  transfers between devices with their start and end apart: 13 -> 13, of which waited for: 4 -> 3; matrix products, arithmetic and copies ran while one was open for 0% -> 0% of each run, Pallas kernels for 33% -> 36%
where the time goes in v4:
time: 30.4 us; the launch traced here: 30.2 us
  starting transfers between devices  15.2 us (50%)
  Pallas kernels  12.4 us (41%)
  waiting for transfers between devices  1.77 us (6%)
  between operations  0.8 us (3%)
    ppermute x12, starting transfers between devices, swap(): return lax.ppermute(value, 'ctx', [(i, i ^ step) for i in range(ways)])  11.7 us
    pallas_call x2, Pallas kernels, short_attention(): pl.pallas_call(functools.partial(short_kernel, head, heads), in_specs=[sm...  6.12 us
    ppermute x1, starting transfers between devices, shards(): lax.ppermute(tail, 'dp', [(i, (i + ranks // 2) % ranks) for i in range(ra...  3.46 us
    pallas_call x2, Pallas kernels, long_attention(): pl.pallas_call(functools.partial(long_kernel, ways, len(linked)), in_spec...  2.64 us
    pallas_call x2, Pallas kernels, pack(): pl.pallas_call(functools.partial(pack_kernel, parts, ways, len(after)), i...  2.04 us
    ppermute x12, waiting for transfers between devices, swap(): return lax.ppermute(value, 'ctx', [(i, i ^ step) for i in range(ways)])  1.77 us
    pallas_call x2, Pallas kernels, join(): pl.pallas_call(functools.partial(join_kernel, parts, ways, len(old), with...  1.61 us
  transfers between devices with their start and end apart: 13, of which 3 were waited for; matrix products, arithmetic and copies ran while one was open for 0% of the time, Pallas kernels for 36%

profile of v4, /device:TPU:0, one launch (start us, length us, event | category | flops | bytes accessed | tf_op | source)
XLA Modules:
  0.0 30.2 jit_solution(6113191699640963449)
XLA Ops:
  0.6 0.0 copy-start.3
  0.6 0.0 copy-start.5
  0.7 0.9 %shard_map.171 = (bf16[4,128,128]{2,1,0:T(8,128)(2,1)S(1)}, bf16[4,128,128]{2,1,0:T(8,128)(2,1)S(1)}) custom-call(bf16[1,128,1024]{2,1,0:T(8,128)(2,1)} %q_ref.3, bf16[1,128,1024]{2,1,0:T(8,128)(2,1)} %k_ref.3, bf16[1,128,1024]{2,1,0:T(8,128)(2,1)} %v_ref.3, bf16[1,128,1024]{2,1,0:T(8,128)(2,1)} %d_ref.3), custom_call_target="tpu_custom_call" | custom-call | bytes 2000000 | tf_op jit(solution)/shard_map/pallas_call | solution.py:302
  1.6 2.5 %collective-permute-start.1 = (bf16[4,128,128]{2,1,0:T(8,128)(2,1)S(1)}, bf16[4,128,128]{2,1,0:T(8,128)(2,1)S(1)}, u32[]{:S(2)}, u32[]{:S(2)}) collective-permute-start(bf16[4,128,128]{2,1,0:T(8,128)(2,1)S(1)} %get-tuple-element.46), channel_id=1, source_target_pairs={{0,3},{1,2},{2,1},{3,0},{4,7},{5,6},{6,5},{7,4},{8,11},{9,10},{10,... | collective-permute-start | bytes 393224 | tf_op jit(solution)/shard_map/ppermute | solution.py:482
  4.1 0.0 copy-start
  4.1 0.0 copy-start.1
  4.1 0.0 copy-start.2
  4.1 0.7 %collective-permute-start = (bf16[4,128,128]{2,1,0:T(8,128)(2,1)S(1)}, bf16[4,128,128]{2,1,0:T(8,128)(2,1)S(1)}, u32[]{:S(2)}, u32[]{:S(2)}) collective-permute-start(bf16[4,128,128]{2,1,0:T(8,128)(2,1)S(1)} %get-tuple-element.45.rest_0_), channel_id=1, source_target_pairs={{0,2},{1,3},{2,0},{3,1},{4,6},{5,7},{6,4},{7,5},{8,10},{9,11},{10,... | collective-permute-start | bytes 393224 | tf_op jit(solution)/shard_map/ppermute | solution.py:482
  4.8 1.1 %shard_map.172 = (bf16[4,128,128]{2,1,0:T(8,128)(2,1)S(1)}, bf16[4,128,128]{2,1,0:T(8,128)(2,1)S(1)}, bf16[4,128,128]{2,1,0:T(8,128)(2,1)S(1)}, bf16[4,128,128]{...) custom-call(bf16[1,128,1024]{2,1,0:T(8,128)(2,1)} %q_ref.3, ...), custom_call_target="tpu_custom_call" | custom-call | bytes 2000000 | tf_op jit(solution)/shard_map/pallas_call | solution.py:302
  5.9 0.0 copy-start.4
  5.9 0.2 collective-permute-start.2
  6.1 1.6 %collective-permute-start.3 = (bf16[4,128,128]{2,1,0:T(8,128)(2,1)S(1)}, bf16[4,128,128]{2,1,0:T(8,128)(2,1)S(1)}, u32[]{:S(2)}, u32[]{:S(2)}) collective-permute-start(bf16[4,128,128]{2,1,0:T(8,128)(2,1)S(1)} %get-tuple-element.50), channel_id=1, source_target_pairs={{0,2},{1,3},{2,0},{3,1},{4,6},{5,7},{6,4},{7,5},{8,10},{9,11},{10,... | collective-permute-start | bytes 393224 | tf_op jit(solution)/shard_map/ppermute | solution.py:482
  7.7 0.0 copy-start.6
  7.7 0.1 collective-permute-start.4
  7.8 0.2 collective-permute-done.1.rest_2_
  8.0 0.8 %collective-permute-start.5 = (bf16[4,128,128]{2,1,0:T(8,128)(2,1)S(1)}, bf16[4,128,128]{2,1,0:T(8,128)(2,1)S(1)}, u32[]{:S(2)}, u32[]{:S(2)}) collective-permute-start(bf16[4,128,128]{2,1,0:T(8,128)(2,1)S(1)} %get-tuple-element.52), channel_id=1, source_target_pairs={{0,1},{1,0},{2,3},{3,2},{4,5},{5,4},{6,7},{7,6},{8,9},{9,8},{10,11... | collective-permute-start | bytes 393224 | tf_op jit(solution)/shard_map/ppermute | solution.py:482
  8.8 0.0 copy-done.3
  8.8 0.0 copy-done.5
  8.8 0.0 copy-done
  8.8 0.0 copy-done.1
  8.8 0.0 copy-done.2
  8.8 0.0 copy-done.4
  8.8 0.0 copy-done.6
  8.8 3.1 %shard_map.170 = (bf16[896,256]{1,0:T(8,128)(2,1)}, bf16[768,256]{1,0:T(8,128)(2,1)}, bf16[768,256]{1,0:T(8,128)(2,1)}, bf16[768,256]{1,0:T(8,128)(2,1)}, bf16[2...) custom-call(s32[8,8]{1,0:T(8,128)S(1)} %copy-done.4, s32[8,8]{1,0:T(8,128)S(1)} %copy-done.5, ...), custom_call_target="tpu_custom_call" | custom-call | flops 1000000000 | bytes 3000000 | tf_op jit(solution)/shard_map/pallas_call | solution.py:251
  11.9 0.0 collective-permute-done.rest_1_
  11.9 0.0 collective-permute-done.2.rest_3_
  11.9 1.3 %shard_map.173 = (bf16[4,128,128]{2,1,0:T(8,128)(2,1)S(1)}, bf16[4,128,128]{2,1,0:T(8,128)(2,1)S(1)}, bf16[4,128,128]{2,1,0:T(8,128)(2,1)S(1)}, bf16[4,128,128]{2,1,0:T(8,128)(2,1)S(1)}) custom-call(s32[8,128]{1,0:T(8,128)S(1)} %get-tuple-element.43.order, bf16[2,128,128]{2,1,0:T(8,128)(2,1)S(1)} %get-tuple-element.44.rest_0_, ...), custom_call_target="tpu_custom_call" | custom-call | flops 1000000000 | bytes 3000000 | tf_op jit(solution)/shard_map/pallas_call | solution.py:392
  13.3 1.9 %collective-permute-start.9 = (bf16[4,128,128]{2,1,0:T(8,128)(2,1)S(1)}, bf16[4,128,128]{2,1,0:T(8,128)(2,1)S(1)}, u32[]{:S(2)}, u32[]{:S(2)}) collective-permute-start(bf16[4,128,128]{2,1,0:T(8,128)(2,1)S(1)} %get-tuple-element.56), channel_id=1, source_target_pairs={{0,2},{1,3},{2,0},{3,1},{4,6},{5,7},{6,4},{7,5},{8,10},{9,11},{10,... | collective-permute-start | bytes 393224 | tf_op jit(solution)/shard_map/ppermute | solution.py:482
  15.1 0.1 collective-permute-start.10
  15.2 0.0 collective-permute-done.3.rest_1_
  15.2 0.3 collective-permute-start.11
  15.5 0.9 %collective-permute-done.4.rest_2_ = bf16[4,128,128]{2,1,0:T(8,128)(2,1)S(1)} collective-permute-done((bf16[4,128,128]{2,1,0:T(8,128)(2,1)S(1)}, bf16[4,128,128]{2,1,0:T(8,128)(2,1)S(1)}, u32[]{:S(2)}, u32[]{:S(2)}) %collective-permute-start.4) | collective-permute-done | bytes 131104 | tf_op jit(solution)/shard_map/ppermute | solution.py:482
  16.4 0.0 collective-permute-done.5.rest_3_
  16.4 1.3 %shard_map.174 = (bf16[4,128,128]{2,1,0:T(8,128)(2,1)S(1)}, bf16[4,128,128]{2,1,0:T(8,128)(2,1)S(1)}, bf16[4,128,128]{2,1,0:T(8,128)(2,1)S(1)}, bf16[4,128,128]{2,1,0:T(8,128)(2,1)S(1)}) custom-call(s32[8,128]{1,0:T(8,128)S(1)} %get-tuple-element.43.order, bf16[4,128,128]{2,1,0:T(8,128)(2,1)S(1)} %get-tuple-element.49.rest_0_.refs_3_, ...), custom_call_target="tpu_custom_call" | custom-call | flops 1000000000 | bytes 3000000 | tf_op jit(solution)/shard_map/pallas_call | solution.py:392
  17.7 0.3 collective-permute-start.12
  18.0 2.4 %collective-permute-start.6 = (bf16[4,128,128]{2,1,0:T(8,128)(2,1)S(1)}, bf16[4,128,128]{2,1,0:T(8,128)(2,1)S(1)}, u32[]{:S(2)}, u32[]{:S(2)}) collective-permute-start(bf16[4,128,128]{2,1,0:T(8,128)(2,1)S(1)} %get-tuple-element.54), channel_id=1, source_target_pairs={{0,2},{1,3},{2,0},{3,1},{4,6},{5,7},{6,4},{7,5},{8,10},{9,11},{10,... | collective-permute-start | bytes 393224 | tf_op jit(solution)/shard_map/ppermute | solution.py:482
  20.4 0.0 collective-permute-done.9.refs_0_
  20.4 1.0 %collective-permute-start.7 = (bf16[4,128,128]{2,1,0:T(8,128)(2,1)S(1)}, bf16[4,128,128]{2,1,0:T(8,128)(2,1)S(1)}, u32[]{:S(2)}, u32[]{:S(2)}) collective-permute-start(bf16[4,128,128]{2,1,0:T(8,128)(2,1)S(1)} %get-tuple-element.55), channel_id=1, source_target_pairs={{0,3},{1,2},{2,1},{3,0},{4,7},{5,6},{6,5},{7,4},{8,11},{9,10},{10,... | collective-permute-start | bytes 393224 | tf_op jit(solution)/shard_map/ppermute | solution.py:482
  21.4 0.6 %collective-permute-done.10.refs_1_ = bf16[4,128,128]{2,1,0:T(8,128)(2,1)S(1)} collective-permute-done((bf16[4,128,128]{2,1,0:T(8,128)(2,1)S(1)}, bf16[4,128,128]{2,1,0:T(8,128)(2,1)S(1)}, u32[]{:S(2)}, u32[]{:S(2)}) %collective-permute-start.10) | collective-permute-done | bytes 131104 | tf_op jit(solution)/shard_map/ppermute | solution.py:482
  22.0 3.5 %collective-permute-start.8 = (bf16[2,128,128]{2,1,0:T(8,128)(2,1)S(1)}, bf16[2,128,128]{2,1,0:T(8,128)(2,1)S(1)}, u32[]{:S(2)}, u32[]{:S(2)}) collective-permute-start(bf16[2,128,128]{2,1,0:T(8,128)(2,1)S(1)} %get-tuple-element.44.rest_0_), channel_id=1, source_target_pairs={{0,16},{4,20},{8,24},{12,28},{16,0},{20,4},{24,8},{28,12},{1,17},{... | collective-permute-start | bytes 196616 | tf_op jit(solution)/shard_map/ppermute | solution.py:494
  25.5 3.0 %shard_map.176 = (bf16[896,256]{1,0:T(8,128)(2,1)}, bf16[768,256]{1,0:T(8,128)(2,1)}, bf16[768,256]{1,0:T(8,128)(2,1)}, bf16[768,256]{1,0:T(8,128)(2,1)}) custom-call(s32[8,8]{1,0:T(8,128)S(1)} %copy-done.4, s32[8,8]{1,0:T(8,128)S(1)} %copy-done.5, ...), custom_call_target="tpu_custom_call", output_to_operand_aliasing={{0}: (6, {}), {1}: (7, {}), {2}: (8, {}), {3}: (9, {})} | custom-call | flops 1000000000 | bytes 3000000 | tf_op jit(solution)/shard_map/pallas_call | solution.py:251
  28.5 0.0 collective-permute-done.11.refs_2_
  28.5 0.0 collective-permute-done.12.refs_4_
  28.5 0.9 %shard_map.175 = (bf16[1,128,1024]{2,1,0:T(8,128)(2,1)}, bf16[1,128,1024]{2,1,0:T(8,128)(2,1)}, bf16[1,128,1024]{2,1,0:T(8,128)(2,1)}, bf16[1,128,1024]{2,1,0:T(8,128)(2,1)}) custom-call(bf16[4,128,128]{2,1,0:T(8,128)(2,1)S(1)} %collective-permute-done.9.refs_0_, bf16[4,128,128]{2,1,0:T(8,128)(2,1)S(1)} %collective-permute-done.10.refs_1_, ...), custom_call_target="tpu_custom_call" | custom-call | bytes 1000000 | tf_op jit(solution)/shard_map/pallas_call | solution.py:450
  29.4 0.0 collective-permute-done.8.refs_2_
  29.4 0.0 collective-permute-done.6.refs_0_
  29.5 0.0 collective-permute-done.7.refs_1_
  29.5 0.7 %shard_map.177 = (bf16[1,128,1024]{2,1,0:T(8,128)(2,1)}, bf16[1,128,1024]{2,1,0:T(8,128)(2,1)}, bf16[1,128,1024]{2,1,0:T(8,128)(2,1)}, bf16[1,128,1024]{2,1,0:T(8,128)(2,1)}, bf16[896,256]{1,0:T(8,128)(2,1)}) custom-call(bf16[4,128,128]{2,1,0:T(8,128)(2,1)S(1)} %collective-permute-done, ...), custom_call_target="tpu_custom_call", output_to_operand_aliasing={{0}: (3, {}), {1}: (4, {}), {2}: (5, {}), {3}: (6, {}), {4}... | custom-call | bytes 1000000 | tf_op jit(solution)/shard_map/pallas_call | solution.py:450
Async XLA Ops:
  0.6 8.1 %copy-start.3 = (bf16[768,256]{1,0:T(8,128)(2,1)S(1)}, bf16[768,256]{1,0:T(8,128)(2,1)}, u32[]{:S(2)}) copy-start(bf16[768,256]{1,0:T(8,128)(2,1)} %d_hbm.3) | copy-start | bytes 1179652
  0.6 8.1 %copy-start.5 = (s32[8,8]{1,0:T(8,128)S(1)}, s32[8,8]{1,0:T(8,128)}, u32[]{:S(2)}) copy-start(s32[8,8]{1,0:T(8,128)} %dests.3) | copy-start | bytes 772
  1.6 6.4 %collective-permute-start.1 = (bf16[4,128,128]{2,1,0:T(8,128)(2,1)S(1)}, bf16[4,128,128]{2,1,0:T(8,128)(2,1)S(1)}, u32[]{:S(2)}, u32[]{:S(2)}) collective-permute-start(bf16[4,128,128]{2,1,0:T(8,128)(2,1)S(1)} %get-tuple-element.46), channel_id=1, source_target_pairs={{0,3},{1,2},{2,1},{3,0},{4,7},{5,6},{6,5},{7,4},{8,11},{9,10},{10,... | collective-permute-start | bytes 393224 | tf_op jit(solution)/shard_map/ppermute | solution.py:482
  4.1 4.7 %copy-start = (bf16[768,256]{1,0:T(8,128)(2,1)S(1)}, bf16[768,256]{1,0:T(8,128)(2,1)}, u32[]{:S(2)}) copy-start(bf16[768,256]{1,0:T(8,128)(2,1)} %q_hbm.3) | copy-start | bytes 1179652
  4.1 4.7 %copy-start.1 = (bf16[768,256]{1,0:T(8,128)(2,1)S(1)}, bf16[768,256]{1,0:T(8,128)(2,1)}, u32[]{:S(2)}) copy-start(bf16[768,256]{1,0:T(8,128)(2,1)} %k_hbm.3) | copy-start | bytes 1179652
  4.1 4.7 %copy-start.2 = (bf16[768,256]{1,0:T(8,128)(2,1)S(1)}, bf16[768,256]{1,0:T(8,128)(2,1)}, u32[]{:S(2)}) copy-start(bf16[768,256]{1,0:T(8,128)(2,1)} %v_hbm.3) | copy-start | bytes 1179652
  4.1 7.8 %collective-permute-start = (bf16[4,128,128]{2,1,0:T(8,128)(2,1)S(1)}, bf16[4,128,128]{2,1,0:T(8,128)(2,1)S(1)}, u32[]{:S(2)}, u32[]{:S(2)}) collective-permute-start(bf16[4,128,128]{2,1,0:T(8,128)(2,1)S(1)} %get-tuple-element.45.rest_0_), channel_id=1, source_target_pairs={{0,2},{1,3},{2,0},{3,1},{4,6},{5,7},{6,4},{7,5},{8,10},{9,11},{10,... | collective-permute-start | bytes 393224 | tf_op jit(solution)/shard_map/ppermute | solution.py:482
  5.9 2.9 %copy-start.4 = (s32[8,8]{1,0:T(8,128)S(1)}, s32[8,8]{1,0:T(8,128)}, u32[]{:S(2)}) copy-start(s32[8,8]{1,0:T(8,128)} %lengths.3) | copy-start | bytes 772
  5.9 6.0 %collective-permute-start.2 = (bf16[4,128,128]{2,1,0:T(8,128)(2,1)S(1)}, bf16[4,128,128]{2,1,0:T(8,128)(2,1)S(1)}, u32[]{:S(2)}, u32[]{:S(2)}) collective-permute-start(bf16[4,128,128]{2,1,0:T(8,128)(2,1)S(1)} %get-tuple-element.47), channel_id=1, source_target_pairs={{0,1},{1,0},{2,3},{3,2},{4,5},{5,4},{6,7},{7,6},{8,9},{9,8},{10,11... | collective-permute-start | bytes 393224 | tf_op jit(solution)/shard_map/ppermute | solution.py:482
  6.1 9.1 %collective-permute-start.3 = (bf16[4,128,128]{2,1,0:T(8,128)(2,1)S(1)}, bf16[4,128,128]{2,1,0:T(8,128)(2,1)S(1)}, u32[]{:S(2)}, u32[]{:S(2)}) collective-permute-start(bf16[4,128,128]{2,1,0:T(8,128)(2,1)S(1)} %get-tuple-element.50), channel_id=1, source_target_pairs={{0,2},{1,3},{2,0},{3,1},{4,6},{5,7},{6,4},{7,5},{8,10},{9,11},{10,... | collective-permute-start | bytes 393224 | tf_op jit(solution)/shard_map/ppermute | solution.py:482
  7.7 1.1 %copy-start.6 = (s32[8]{0:T(128)S(1)}, s32[8]{0:T(128)}, u32[]{:S(2)}) copy-start(s32[8]{0:T(128)} %rest_0_.1) | copy-start | bytes 100
  7.7 8.7 %collective-permute-start.4 = (bf16[4,128,128]{2,1,0:T(8,128)(2,1)S(1)}, bf16[4,128,128]{2,1,0:T(8,128)(2,1)S(1)}, u32[]{:S(2)}, u32[]{:S(2)}) collective-permute-start(bf16[4,128,128]{2,1,0:T(8,128)(2,1)S(1)} %get-tuple-element.51), channel_id=1, source_target_pairs={{0,3},{1,2},{2,1},{3,0},{4,7},{5,6},{6,5},{7,4},{8,11},{9,10},{10,... | collective-permute-start | bytes 393224 | tf_op jit(solution)/shard_map/ppermute | solution.py:482
  8.0 8.4 %collective-permute-start.5 = (bf16[4,128,128]{2,1,0:T(8,128)(2,1)S(1)}, bf16[4,128,128]{2,1,0:T(8,128)(2,1)S(1)}, u32[]{:S(2)}, u32[]{:S(2)}) collective-permute-start(bf16[4,128,128]{2,1,0:T(8,128)(2,1)S(1)} %get-tuple-element.52), channel_id=1, source_target_pairs={{0,1},{1,0},{2,3},{3,2},{4,5},{5,4},{6,7},{7,6},{8,9},{9,8},{10,11... | collective-permute-start | bytes 393224 | tf_op jit(solution)/shard_map/ppermute | solution.py:482
  13.3 7.1 %collective-permute-start.9 = (bf16[4,128,128]{2,1,0:T(8,128)(2,1)S(1)}, bf16[4,128,128]{2,1,0:T(8,128)(2,1)S(1)}, u32[]{:S(2)}, u32[]{:S(2)}) collective-permute-start(bf16[4,128,128]{2,1,0:T(8,128)(2,1)S(1)} %get-tuple-element.56), channel_id=1, source_target_pairs={{0,2},{1,3},{2,0},{3,1},{4,6},{5,7},{6,4},{7,5},{8,10},{9,11},{10,... | collective-permute-start | bytes 393224 | tf_op jit(solution)/shard_map/ppermute | solution.py:482
  15.1 6.9 %collective-permute-start.10 = (bf16[4,128,128]{2,1,0:T(8,128)(2,1)S(1)}, bf16[4,128,128]{2,1,0:T(8,128)(2,1)S(1)}, u32[]{:S(2)}, u32[]{:S(2)}) collective-permute-start(bf16[4,128,128]{2,1,0:T(8,128)(2,1)S(1)} %get-tuple-element.57), channel_id=1, source_target_pairs={{0,3},{1,2},{2,1},{3,0},{4,7},{5,6},{6,5},{7,4},{8,11},{9,10},{10,... | collective-permute-start | bytes 393224 | tf_op jit(solution)/shard_map/ppermute | solution.py:482
  15.2 13.3 %collective-permute-start.11 = (bf16[4,128,128]{2,1,0:T(8,128)(2,1)S(1)}, bf16[4,128,128]{2,1,0:T(8,128)(2,1)S(1)}, u32[]{:S(2)}, u32[]{:S(2)}) collective-permute-start(bf16[4,128,128]{2,1,0:T(8,128)(2,1)S(1)} %get-tuple-element.58), channel_id=1, source_target_pairs={{0,1},{1,0},{2,3},{3,2},{4,5},{5,4},{6,7},{7,6},{8,9},{9,8},{10,11... | collective-permute-start | bytes 393224 | tf_op jit(solution)/shard_map/ppermute | solution.py:482
  17.7 10.8 %collective-permute-start.12 = (bf16[4,128,128]{2,1,0:T(8,128)(2,1)S(1)}, bf16[4,128,128]{2,1,0:T(8,128)(2,1)S(1)}, u32[]{:S(2)}, u32[]{:S(2)}) collective-permute-start(bf16[4,128,128]{2,1,0:T(8,128)(2,1)S(1)} %get-tuple-element.59), channel_id=1, source_target_pairs={{0,1},{1,0},{2,3},{3,2},{4,5},{5,4},{6,7},{7,6},{8,9},{9,8},{10,11... | collective-permute-start | bytes 393224 | tf_op jit(solution)/shard_map/ppermute | solution.py:482
  18.0 11.4 %collective-permute-start.6 = (bf16[4,128,128]{2,1,0:T(8,128)(2,1)S(1)}, bf16[4,128,128]{2,1,0:T(8,128)(2,1)S(1)}, u32[]{:S(2)}, u32[]{:S(2)}) collective-permute-start(bf16[4,128,128]{2,1,0:T(8,128)(2,1)S(1)} %get-tuple-element.54), channel_id=1, source_target_pairs={{0,2},{1,3},{2,0},{3,1},{4,6},{5,7},{6,4},{7,5},{8,10},{9,11},{10,... | collective-permute-start | bytes 393224 | tf_op jit(solution)/shard_map/ppermute | solution.py:482
  20.4 9.1 %collective-permute-start.7 = (bf16[4,128,128]{2,1,0:T(8,128)(2,1)S(1)}, bf16[4,128,128]{2,1,0:T(8,128)(2,1)S(1)}, u32[]{:S(2)}, u32[]{:S(2)}) collective-permute-start(bf16[4,128,128]{2,1,0:T(8,128)(2,1)S(1)} %get-tuple-element.55), channel_id=1, source_target_pairs={{0,3},{1,2},{2,1},{3,0},{4,7},{5,6},{6,5},{7,4},{8,11},{9,10},{10,... | collective-permute-start | bytes 393224 | tf_op jit(solution)/shard_map/ppermute | solution.py:482
  22.0 7.4 %collective-permute-start.8 = (bf16[2,128,128]{2,1,0:T(8,128)(2,1)S(1)}, bf16[2,128,128]{2,1,0:T(8,128)(2,1)S(1)}, u32[]{:S(2)}, u32[]{:S(2)}) collective-permute-start(bf16[2,128,128]{2,1,0:T(8,128)(2,1)S(1)} %get-tuple-element.44.rest_0_), channel_id=1, source_target_pairs={{0,16},{4,20},{8,24},{12,28},{16,0},{20,4},{24,8},{28,12},{1,17},{... | collective-permute-start | bytes 196616 | tf_op jit(solution)/shard_map/ppermute | solution.py:494

commit v5 on v4

--- a/solution.py
+++ b/solution.py
@@ -301,7 +301,8 @@
     rows = arrays[0].shape[1]
     return pl.pallas_call(
         functools.partial(pack_kernel, parts, ways, len(after)),
-        in_specs=[pl.BlockSpec(memory_space=pltpu.HBM)] * 4 + [pl.BlockSpec(memory_space=pl.ANY)] * len(after),
+        in_specs=[pl.BlockSpec(memory_space=pl.ANY if after else pltpu.HBM)] * 4
+        + [pl.BlockSpec(memory_space=pl.ANY)] * len(after),
         out_specs=[pl.BlockSpec(memory_space=pltpu.VMEM)] * len(parts),
         out_shape=[jax.ShapeDtypeStruct((4, rows, HEAD_DIM), jnp.bfloat16)] * len(parts),
         scratch_shapes=[
@@ -310,7 +311,7 @@
         ],
         compiler_params=pltpu.CompilerParams(vmem_limit_bytes=8 << 20),
         cost_estimate=pl.CostEstimate(flops=0, bytes_accessed=2 * 10**6, transcendentals=0),
-    )(*[pltpu.with_memory_space_constraint(array, pltpu.HBM) for array in arrays], *after)
+    )(*[array if after else pltpu.with_memory_space_constraint(array, pltpu.HBM) for array in arrays], *after)
 
 
 def long_kernel(ways, linked, order, *rest):

time: 30.4 us -> 30.7 us (level)
  waiting for transfers between devices: 1.77 us -> 3.5 us
  starting transfers between devices: 15.2 us -> 13.6 us
  local copies, waits for them, and re-layouts: 0.03 us -> 1.04 us
  Pallas kernels: 12.4 us -> 11.6 us
    ppermute x12, waiting for transfers between devices: 1.77 us -> 3.05 us  [swap(): return lax.ppermute(value, 'ctx', [(i, i ^ step) for i in range(ways)])]
    unnamed x14 -> x24, local copies, waits for them, and re-layouts: 0.03 us -> 1.04 us
    ppermute x1, starting transfers between devices: 3.46 us -> 2.59 us  [shards(): lax.ppermute(tail, 'dp', [(i, (i + ranks // 2) % ranks) for i in range(ra...]
    pallas_call x2, Pallas kernels: 2.04 us -> 1.23 us  [pack(): pl.pallas_call(functools.partial(pack_kernel, parts, ways, len(after)), i...]
    ppermute x12, starting transfers between devices: 11.7 us -> 11 us  [swap(): return lax.ppermute(value, 'ctx', [(i, i ^ step) for i in range(ways)])]
    ppermute x1, waiting for transfers between devices: 0.01 us -> 0.44 us  [shards(): lax.ppermute(tail, 'dp', [(i, (i + ranks // 2) % ranks) for i in range(ra...]
  transfers between devices with their start and end apart: 13 -> 13, of which waited for: 3 -> 4; matrix products, arithmetic and copies ran while one was open for 0% -> 0% of each run, Pallas kernels for 36% -> 32%
where the time goes in v5:
time: 30.7 us; the launch traced here: 30.6 us
  starting transfers between devices  13.6 us (44%)
  Pallas kernels  11.6 us (38%)
  waiting for transfers between devices  3.5 us (11%)
  local copies, waits for them, and re-layouts  1.04 us (3%)
  between operations  0.81 us (3%)
    ppermute x12, starting transfers between devices, swap(): return lax.ppermute(value, 'ctx', [(i, i ^ step) for i in range(ways)])  11 us
    pallas_call x2, Pallas kernels, short_attention(): pl.pallas_call(functools.partial(short_kernel, head, heads), in_specs=[sm...  6.12 us
    ppermute x12, waiting for transfers between devices, swap(): return lax.ppermute(value, 'ctx', [(i, i ^ step) for i in range(ways)])  3.05 us
    pallas_call x2, Pallas kernels, long_attention(): pl.pallas_call(functools.partial(long_kernel, ways, len(linked)), in_spec...  2.64 us
    ppermute x1, starting transfers between devices, shards(): lax.ppermute(tail, 'dp', [(i, (i + ranks // 2) % ranks) for i in range(ra...  2.59 us
    pallas_call x2, Pallas kernels, join(): pl.pallas_call(functools.partial(join_kernel, parts, ways, len(old), with...  1.6 us
    pallas_call x2, Pallas kernels, pack(): pl.pallas_call(functools.partial(pack_kernel, parts, ways, len(after)), i...  1.23 us
    unnamed x24, local copies, waits for them, and re-layouts  1.04 us
  transfers between devices with their start and end apart: 13, of which 4 were waited for; matrix products, arithmetic and copies ran while one was open for 0% of the time, Pallas kernels for 32%

profile of v5, /device:TPU:0, one launch (start us, length us, event | category | flops | bytes accessed | tf_op | source)
XLA Modules:
  0.0 30.6 jit_solution(4357273380782367919)
XLA Ops:
  0.6 0.0 copy-start.3
  0.6 0.0 copy-start.2
  0.7 0.0 copy-start.1
  0.7 0.0 copy-start
  0.7 0.0 copy-start.10
  0.7 1.0 %shard_map.171 = (bf16[4,128,128]{2,1,0:T(8,128)(2,1)S(1)}, bf16[4,128,128]{2,1,0:T(8,128)(2,1)S(1)}) custom-call(bf16[1,128,1024]{2,1,0:T(8,128)(2,1)} %q_ref.3, bf16[1,128,1024]{2,1,0:T(8,128)(2,1)} %k_ref.3, bf16[1,128,1024]{2,1,0:T(8,128)(2,1)} %v_ref.3, bf16[1,128,1024]{2,1,0:T(8,128)(2,1)} %d_ref.3), custom_call_target="tpu_custom_call" | custom-call | bytes 2000000 | tf_op jit(solution)/shard_map/pallas_call | solution.py:302
  1.7 2.5 %collective-permute-start.1 = (bf16[4,128,128]{2,1,0:T(8,128)(2,1)S(1)}, bf16[4,128,128]{2,1,0:T(8,128)(2,1)S(1)}, u32[]{:S(2)}, u32[]{:S(2)}) collective-permute-start(bf16[4,128,128]{2,1,0:T(8,128)(2,1)S(1)} %get-tuple-element.46), channel_id=1, source_target_pairs={{0,3},{1,2},{2,1},{3,0},{4,7},{5,6},{6,5},{7,4},{8,11},{9,10},{10,... | collective-permute-start | bytes 393224 | tf_op jit(solution)/shard_map/ppermute | solution.py:483
  4.2 0.0 copy-start.4
  4.2 0.0 copy-start.5
  4.2 0.0 copy-start.6
  4.2 0.7 %collective-permute-start = (bf16[4,128,128]{2,1,0:T(8,128)(2,1)S(1)}, bf16[4,128,128]{2,1,0:T(8,128)(2,1)S(1)}, u32[]{:S(2)}, u32[]{:S(2)}) collective-permute-start(bf16[4,128,128]{2,1,0:T(8,128)(2,1)S(1)} %get-tuple-element.45.rest_0_), channel_id=1, source_target_pairs={{0,2},{1,3},{2,0},{3,1},{4,6},{5,7},{6,4},{7,5},{8,10},{9,11},{10,... | collective-permute-start | bytes 393224 | tf_op jit(solution)/shard_map/ppermute | solution.py:483
  4.8 0.0 copy-done.3
  4.8 0.0 copy-done.2
  4.8 0.0 copy-done.1
  4.8 0.0 copy-done
  4.8 0.3 shard_map.172
  5.1 0.0 copy-start.9
  5.1 0.1 collective-permute-start.2
  5.2 1.7 %collective-permute-start.3 = (bf16[4,128,128]{2,1,0:T(8,128)(2,1)S(1)}, bf16[4,128,128]{2,1,0:T(8,128)(2,1)S(1)}, u32[]{:S(2)}, u32[]{:S(2)}) collective-permute-start(bf16[4,128,128]{2,1,0:T(8,128)(2,1)S(1)} %get-tuple-element.50), channel_id=1, source_target_pairs={{0,2},{1,3},{2,0},{3,1},{4,6},{5,7},{6,4},{7,5},{8,10},{9,11},{10,... | collective-permute-start | bytes 393224 | tf_op jit(solution)/shard_map/ppermute | solution.py:483
  7.0 0.0 copy-start.11
  7.0 0.1 collective-permute-start.4
  7.1 1.0 %collective-permute-done.1.rest_2_ = bf16[4,128,128]{2,1,0:T(8,128)(2,1)S(1)} collective-permute-done((bf16[4,128,128]{2,1,0:T(8,128)(2,1)S(1)}, bf16[4,128,128]{2,1,0:T(8,128)(2,1)S(1)}, u32[]{:S(2)}, u32[]{:S(2)}) %collective-permute-start.1) | collective-permute-done | bytes 131104 | tf_op jit(solution)/shard_map/ppermute | solution.py:483
  8.0 0.8 %collective-permute-start.5 = (bf16[4,128,128]{2,1,0:T(8,128)(2,1)S(1)}, bf16[4,128,128]{2,1,0:T(8,128)(2,1)S(1)}, u32[]{:S(2)}, u32[]{:S(2)}) collective-permute-start(bf16[4,128,128]{2,1,0:T(8,128)(2,1)S(1)} %get-tuple-element.52), channel_id=1, source_target_pairs={{0,1},{1,0},{2,3},{3,2},{4,5},{5,4},{6,7},{7,6},{8,9},{9,8},{10,11... | collective-permute-start | bytes 393224 | tf_op jit(solution)/shard_map/ppermute | solution.py:483
  8.8 0.0 copy-done.10
  8.8 0.0 copy-done.4
  8.8 0.0 copy-done.5
  8.8 0.0 copy-done.6
  8.8 0.0 copy-done.9
  8.8 0.0 copy-done.11
  8.9 0.0 copy-start.7
  8.9 1.0 %copy-done.7 = bf16[768,256]{1,0:T(8,128)(2,1)S(1)} copy-done((bf16[768,256]{1,0:T(8,128)(2,1)S(1)}, bf16[768,256]{1,0:T(8,128)(2,1)}, u32[]{:S(2)}) %copy-start.7) | copy-done | bytes 393240
  9.9 3.1 %shard_map.170 = (bf16[896,256]{1,0:T(8,128)(2,1)}, bf16[768,256]{1,0:T(8,128)(2,1)}, bf16[768,256]{1,0:T(8,128)(2,1)}, bf16[768,256]{1,0:T(8,128)(2,1)}, bf16[2...) custom-call(s32[8,8]{1,0:T(8,128)S(1)} %copy-done.9, s32[8,8]{1,0:T(8,128)S(1)} %copy-done.10, ...), custom_call_target="tpu_custom_call" | custom-call | flops 1000000000 | bytes 3000000 | tf_op jit(solution)/shard_map/pallas_call | solution.py:251
  13.0 0.0 collective-permute-done.rest_1_
  13.0 0.0 collective-permute-done.2.rest_3_
  13.0 1.3 %shard_map.173 = (bf16[4,128,128]{2,1,0:T(8,128)(2,1)S(1)}, bf16[4,128,128]{2,1,0:T(8,128)(2,1)S(1)}, bf16[4,128,128]{2,1,0:T(8,128)(2,1)S(1)}, bf16[4,128,128]{2,1,0:T(8,128)(2,1)S(1)}) custom-call(s32[8,128]{1,0:T(8,128)S(1)} %get-tuple-element.43.order, bf16[2,128,128]{2,1,0:T(8,128)(2,1)S(1)} %get-tuple-element.44.rest_0_, ...), custom_call_target="tpu_custom_call" | custom-call | flops 1000000000 | bytes 3000000 | tf_op jit(solution)/shard_map/pallas_call | solution.py:393
  14.3 1.9 %collective-permute-start.9 = (bf16[4,128,128]{2,1,0:T(8,128)(2,1)S(1)}, bf16[4,128,128]{2,1,0:T(8,128)(2,1)S(1)}, u32[]{:S(2)}, u32[]{:S(2)}) collective-permute-start(bf16[4,128,128]{2,1,0:T(8,128)(2,1)S(1)} %get-tuple-element.56), channel_id=1, source_target_pairs={{0,2},{1,3},{2,0},{3,1},{4,6},{5,7},{6,4},{7,5},{8,10},{9,11},{10,... | collective-permute-start | bytes 393224 | tf_op jit(solution)/shard_map/ppermute | solution.py:483
  16.2 0.1 collective-permute-start.10
  16.2 0.0 collective-permute-done.3.rest_1_
  16.3 0.3 collective-permute-start.11
  16.5 0.0 collective-permute-done.4.rest_2_
  16.5 0.0 collective-permute-done.5.rest_3_
  16.5 0.0 copy-start.8
  16.5 1.3 %shard_map.174 = (bf16[4,128,128]{2,1,0:T(8,128)(2,1)S(1)}, bf16[4,128,128]{2,1,0:T(8,128)(2,1)S(1)}, bf16[4,128,128]{2,1,0:T(8,128)(2,1)S(1)}, bf16[4,128,128]{2,1,0:T(8,128)(2,1)S(1)}) custom-call(s32[8,128]{1,0:T(8,128)S(1)} %get-tuple-element.43.order, bf16[4,128,128]{2,1,0:T(8,128)(2,1)S(1)} %get-tuple-element.49.rest_0_.refs_3_, ...), custom_call_target="tpu_custom_call" | custom-call | flops 1000000000 | bytes 3000000 | tf_op jit(solution)/shard_map/pallas_call | solution.py:393
  17.8 0.3 %collective-permute-start.12 = (bf16[4,128,128]{2,1,0:T(8,128)(2,1)S(1)}, bf16[4,128,128]{2,1,0:T(8,128)(2,1)S(1)}, u32[]{:S(2)}, u32[]{:S(2)}) collective-permute-start(bf16[4,128,128]{2,1,0:T(8,128)(2,1)S(1)} %get-tuple-element.59), channel_id=1, source_target_pairs={{0,1},{1,0},{2,3},{3,2},{4,5},{5,4},{6,7},{7,6},{8,9},{9,8},{10,11... | collective-permute-start | bytes 393224 | tf_op jit(solution)/shard_map/ppermute | solution.py:483
  18.2 2.3 %collective-permute-start.6 = (bf16[4,128,128]{2,1,0:T(8,128)(2,1)S(1)}, bf16[4,128,128]{2,1,0:T(8,128)(2,1)S(1)}, u32[]{:S(2)}, u32[]{:S(2)}) collective-permute-start(bf16[4,128,128]{2,1,0:T(8,128)(2,1)S(1)} %get-tuple-element.54), channel_id=1, source_target_pairs={{0,2},{1,3},{2,0},{3,1},{4,6},{5,7},{6,4},{7,5},{8,10},{9,11},{10,... | collective-permute-start | bytes 393224 | tf_op jit(solution)/shard_map/ppermute | solution.py:483
  20.4 0.3 collective-permute-done.9.refs_0_
  20.7 0.4 %collective-permute-start.7 = (bf16[4,128,128]{2,1,0:T(8,128)(2,1)S(1)}, bf16[4,128,128]{2,1,0:T(8,128)(2,1)S(1)}, u32[]{:S(2)}, u32[]{:S(2)}) collective-permute-start(bf16[4,128,128]{2,1,0:T(8,128)(2,1)S(1)} %get-tuple-element.55), channel_id=1, source_target_pairs={{0,3},{1,2},{2,1},{3,0},{4,7},{5,6},{6,5},{7,4},{8,11},{9,10},{10,... | collective-permute-start | bytes 393224 | tf_op jit(solution)/shard_map/ppermute | solution.py:483
  21.1 1.7 %collective-permute-done.10.refs_1_ = bf16[4,128,128]{2,1,0:T(8,128)(2,1)S(1)} collective-permute-done((bf16[4,128,128]{2,1,0:T(8,128)(2,1)S(1)}, bf16[4,128,128]{2,1,0:T(8,128)(2,1)S(1)}, u32[]{:S(2)}, u32[]{:S(2)}) %collective-permute-start.10) | collective-permute-done | bytes 131104 | tf_op jit(solution)/shard_map/ppermute | solution.py:483
  22.9 2.6 %collective-permute-start.8 = (bf16[2,128,128]{2,1,0:T(8,128)(2,1)S(1)}, bf16[2,128,128]{2,1,0:T(8,128)(2,1)S(1)}, u32[]{:S(2)}, u32[]{:S(2)}) collective-permute-start(bf16[2,128,128]{2,1,0:T(8,128)(2,1)S(1)} %get-tuple-element.44.rest_0_), channel_id=1, source_target_pairs={{0,16},{4,20},{8,24},{12,28},{16,0},{20,4},{24,8},{28,12},{1,17},{... | collective-permute-start | bytes 196616 | tf_op jit(solution)/shard_map/ppermute | solution.py:495
  25.5 0.0 copy-done.8
  25.5 3.0 %shard_map.176 = (bf16[896,256]{1,0:T(8,128)(2,1)}, bf16[768,256]{1,0:T(8,128)(2,1)}, bf16[768,256]{1,0:T(8,128)(2,1)}, bf16[768,256]{1,0:T(8,128)(2,1)}) custom-call(s32[8,8]{1,0:T(8,128)S(1)} %copy-done.9, s32[8,8]{1,0:T(8,128)S(1)} %copy-done.10, ...), custom_call_target="tpu_custom_call", output_to_operand_aliasing={{0}: (6, {}), {1}: (7, {}), {2}: (8, {}), {3}: (9, {})} | custom-call | flops 1000000000 | bytes 3000000 | tf_op jit(solution)/shard_map/pallas_call | solution.py:251
  28.5 0.0 collective-permute-done.11.refs_2_
  28.5 0.0 collective-permute-done.12.refs_4_
  28.5 0.9 %shard_map.175 = (bf16[1,128,1024]{2,1,0:T(8,128)(2,1)}, bf16[1,128,1024]{2,1,0:T(8,128)(2,1)}, bf16[1,128,1024]{2,1,0:T(8,128)(2,1)}, bf16[1,128,1024]{2,1,0:T(8,128)(2,1)}) custom-call(bf16[4,128,128]{2,1,0:T(8,128)(2,1)S(1)} %collective-permute-done.9.refs_0_, bf16[4,128,128]{2,1,0:T(8,128)(2,1)S(1)} %collective-permute-done.10.refs_1_, ...), custom_call_target="tpu_custom_call" | custom-call | bytes 1000000 | tf_op jit(solution)/shard_map/pallas_call | solution.py:451
  29.4 0.4 %collective-permute-done.8.refs_2_ = bf16[2,128,128]{2,1,0:T(8,128)(2,1)S(1)} collective-permute-done((bf16[2,128,128]{2,1,0:T(8,128)(2,1)S(1)}, bf16[2,128,128]{2,1,0:T(8,128)(2,1)S(1)}, u32[]{:S(2)}, u32[]{:S(2)}) %collective-permute-start.8) | collective-permute-done | bytes 65568 | tf_op jit(solution)/shard_map/ppermute | solution.py:495
  29.8 0.0 collective-permute-done.6.refs_0_
  29.8 0.0 collective-permute-done.7.refs_1_
  29.8 0.7 %shard_map.177 = (bf16[1,128,1024]{2,1,0:T(8,128)(2,1)}, bf16[1,128,1024]{2,1,0:T(8,128)(2,1)}, bf16[1,128,1024]{2,1,0:T(8,128)(2,1)}, bf16[1,128,1024]{2,1,0:T(8,128)(2,1)}, bf16[896,256]{1,0:T(8,128)(2,1)}) custom-call(bf16[4,128,128]{2,1,0:T(8,128)(2,1)S(1)} %collective-permute-done, ...), custom_call_target="tpu_custom_call", output_to_operand_aliasing={{0}: (3, {}), {1}: (4, {}), {2}: (5, {}), {3}: (6, {}), {4}... | custom-call | bytes 1000000 | tf_op jit(solution)/shard_map/pallas_call | solution.py:451
Async XLA Ops:
  0.6 4.2 %copy-start.3 = (bf16[1,128,1024]{2,1,0:T(8,128)(2,1)S(1)}, bf16[1,128,1024]{2,1,0:T(8,128)(2,1)}, u32[]{:S(2)}) copy-start(bf16[1,128,1024]{2,1,0:T(8,128)(2,1)} %d_ref.3) | copy-start | bytes 786436
  0.6 4.2 %copy-start.2 = (bf16[1,128,1024]{2,1,0:T(8,128)(2,1)S(1)}, bf16[1,128,1024]{2,1,0:T(8,128)(2,1)}, u32[]{:S(2)}) copy-start(bf16[1,128,1024]{2,1,0:T(8,128)(2,1)} %v_ref.3) | copy-start | bytes 786436
  0.7 4.2 %copy-start.1 = (bf16[1,128,1024]{2,1,0:T(8,128)(2,1)S(1)}, bf16[1,128,1024]{2,1,0:T(8,128)(2,1)}, u32[]{:S(2)}) copy-start(bf16[1,128,1024]{2,1,0:T(8,128)(2,1)} %k_ref.3) | copy-start | bytes 786436
  0.7 4.2 %copy-start = (bf16[1,128,1024]{2,1,0:T(8,128)(2,1)S(1)}, bf16[1,128,1024]{2,1,0:T(8,128)(2,1)}, u32[]{:S(2)}) copy-start(bf16[1,128,1024]{2,1,0:T(8,128)(2,1)} %q_ref.3) | copy-start | bytes 786436
  0.7 8.1 %copy-start.10 = (s32[8,8]{1,0:T(8,128)S(1)}, s32[8,8]{1,0:T(8,128)}, u32[]{:S(2)}) copy-start(s32[8,8]{1,0:T(8,128)} %dests.3) | copy-start | bytes 772
  1.7 6.4 %collective-permute-start.1 = (bf16[4,128,128]{2,1,0:T(8,128)(2,1)S(1)}, bf16[4,128,128]{2,1,0:T(8,128)(2,1)S(1)}, u32[]{:S(2)}, u32[]{:S(2)}) collective-permute-start(bf16[4,128,128]{2,1,0:T(8,128)(2,1)S(1)} %get-tuple-element.46), channel_id=1, source_target_pairs={{0,3},{1,2},{2,1},{3,0},{4,7},{5,6},{6,5},{7,4},{8,11},{9,10},{10,... | collective-permute-start | bytes 393224 | tf_op jit(solution)/shard_map/ppermute | solution.py:483
  4.2 4.7 %copy-start.4 = (bf16[768,256]{1,0:T(8,128)(2,1)S(1)}, bf16[768,256]{1,0:T(8,128)(2,1)}, u32[]{:S(2)}) copy-start(bf16[768,256]{1,0:T(8,128)(2,1)} %q_hbm.3) | copy-start | bytes 1179652
  4.2 4.7 %copy-start.5 = (bf16[768,256]{1,0:T(8,128)(2,1)S(1)}, bf16[768,256]{1,0:T(8,128)(2,1)}, u32[]{:S(2)}) copy-start(bf16[768,256]{1,0:T(8,128)(2,1)} %k_hbm.3) | copy-start | bytes 1179652
  4.2 4.7 %copy-start.6 = (bf16[768,256]{1,0:T(8,128)(2,1)S(1)}, bf16[768,256]{1,0:T(8,128)(2,1)}, u32[]{:S(2)}) copy-start(bf16[768,256]{1,0:T(8,128)(2,1)} %v_hbm.3) | copy-start | bytes 1179652
  4.2 8.8 %collective-permute-start = (bf16[4,128,128]{2,1,0:T(8,128)(2,1)S(1)}, bf16[4,128,128]{2,1,0:T(8,128)(2,1)S(1)}, u32[]{:S(2)}, u32[]{:S(2)}) collective-permute-start(bf16[4,128,128]{2,1,0:T(8,128)(2,1)S(1)} %get-tuple-element.45.rest_0_), channel_id=1, source_target_pairs={{0,2},{1,3},{2,0},{3,1},{4,6},{5,7},{6,4},{7,5},{8,10},{9,11},{10,... | collective-permute-start | bytes 393224 | tf_op jit(solution)/shard_map/ppermute | solution.py:483
  5.1 3.7 %copy-start.9 = (s32[8,8]{1,0:T(8,128)S(1)}, s32[8,8]{1,0:T(8,128)}, u32[]{:S(2)}) copy-start(s32[8,8]{1,0:T(8,128)} %lengths.3) | copy-start | bytes 772
  5.1 7.8 %collective-permute-start.2 = (bf16[4,128,128]{2,1,0:T(8,128)(2,1)S(1)}, bf16[4,128,128]{2,1,0:T(8,128)(2,1)S(1)}, u32[]{:S(2)}, u32[]{:S(2)}) collective-permute-start(bf16[4,128,128]{2,1,0:T(8,128)(2,1)S(1)} %get-tuple-element.47), channel_id=1, source_target_pairs={{0,1},{1,0},{2,3},{3,2},{4,5},{5,4},{6,7},{7,6},{8,9},{9,8},{10,11... | collective-permute-start | bytes 393224 | tf_op jit(solution)/shard_map/ppermute | solution.py:483
  5.2 11.0 %collective-permute-start.3 = (bf16[4,128,128]{2,1,0:T(8,128)(2,1)S(1)}, bf16[4,128,128]{2,1,0:T(8,128)(2,1)S(1)}, u32[]{:S(2)}, u32[]{:S(2)}) collective-permute-start(bf16[4,128,128]{2,1,0:T(8,128)(2,1)S(1)} %get-tuple-element.50), channel_id=1, source_target_pairs={{0,2},{1,3},{2,0},{3,1},{4,6},{5,7},{6,4},{7,5},{8,10},{9,11},{10,... | collective-permute-start | bytes 393224 | tf_op jit(solution)/shard_map/ppermute | solution.py:483
  7.0 1.9 %copy-start.11 = (s32[8]{0:T(128)S(1)}, s32[8]{0:T(128)}, u32[]{:S(2)}) copy-start(s32[8]{0:T(128)} %rest_0_.1) | copy-start | bytes 100
  7.0 9.6 %collective-permute-start.4 = (bf16[4,128,128]{2,1,0:T(8,128)(2,1)S(1)}, bf16[4,128,128]{2,1,0:T(8,128)(2,1)S(1)}, u32[]{:S(2)}, u32[]{:S(2)}) collective-permute-start(bf16[4,128,128]{2,1,0:T(8,128)(2,1)S(1)} %get-tuple-element.51), channel_id=1, source_target_pairs={{0,3},{1,2},{2,1},{3,0},{4,7},{5,6},{6,5},{7,4},{8,11},{9,10},{10,... | collective-permute-start | bytes 393224 | tf_op jit(solution)/shard_map/ppermute | solution.py:483
  8.0 8.5 %collective-permute-start.5 = (bf16[4,128,128]{2,1,0:T(8,128)(2,1)S(1)}, bf16[4,128,128]{2,1,0:T(8,128)(2,1)S(1)}, u32[]{:S(2)}, u32[]{:S(2)}) collective-permute-start(bf16[4,128,128]{2,1,0:T(8,128)(2,1)S(1)} %get-tuple-element.52), channel_id=1, source_target_pairs={{0,1},{1,0},{2,3},{3,2},{4,5},{5,4},{6,7},{7,6},{8,9},{9,8},{10,11... | collective-permute-start | bytes 393224 | tf_op jit(solution)/shard_map/ppermute | solution.py:483
  8.9 1.0 %copy-start.7 = (bf16[768,256]{1,0:T(8,128)(2,1)S(1)}, bf16[768,256]{1,0:T(8,128)(2,1)}, u32[]{:S(2)}) copy-start(bf16[768,256]{1,0:T(8,128)(2,1)} %d_hbm.3) | copy-start | bytes 1179652
  14.3 6.4 %collective-permute-start.9 = (bf16[4,128,128]{2,1,0:T(8,128)(2,1)S(1)}, bf16[4,128,128]{2,1,0:T(8,128)(2,1)S(1)}, u32[]{:S(2)}, u32[]{:S(2)}) collective-permute-start(bf16[4,128,128]{2,1,0:T(8,128)(2,1)S(1)} %get-tuple-element.56), channel_id=1, source_target_pairs={{0,2},{1,3},{2,0},{3,1},{4,6},{5,7},{6,4},{7,5},{8,10},{9,11},{10,... | collective-permute-start | bytes 393224 | tf_op jit(solution)/shard_map/ppermute | solution.py:483
  16.2 6.7 %collective-permute-start.10 = (bf16[4,128,128]{2,1,0:T(8,128)(2,1)S(1)}, bf16[4,128,128]{2,1,0:T(8,128)(2,1)S(1)}, u32[]{:S(2)}, u32[]{:S(2)}) collective-permute-start(bf16[4,128,128]{2,1,0:T(8,128)(2,1)S(1)} %get-tuple-element.57), channel_id=1, source_target_pairs={{0,3},{1,2},{2,1},{3,0},{4,7},{5,6},{6,5},{7,4},{8,11},{9,10},{10,... | collective-permute-start | bytes 393224 | tf_op jit(solution)/shard_map/ppermute | solution.py:483
  16.3 12.2 %collective-permute-start.11 = (bf16[4,128,128]{2,1,0:T(8,128)(2,1)S(1)}, bf16[4,128,128]{2,1,0:T(8,128)(2,1)S(1)}, u32[]{:S(2)}, u32[]{:S(2)}) collective-permute-start(bf16[4,128,128]{2,1,0:T(8,128)(2,1)S(1)} %get-tuple-element.58), channel_id=1, source_target_pairs={{0,1},{1,0},{2,3},{3,2},{4,5},{5,4},{6,7},{7,6},{8,9},{9,8},{10,11... | collective-permute-start | bytes 393224 | tf_op jit(solution)/shard_map/ppermute | solution.py:483
  16.5 8.9 %copy-start.8 = (bf16[768,256]{1,0:T(8,128)(2,1)S(1)}, bf16[768,256]{1,0:T(8,128)(2,1)}, u32[]{:S(2)}) copy-start(bf16[768,256]{1,0:T(8,128)(2,1)} %d_hbm.3) | copy-start | bytes 1179652
  17.8 10.7 %collective-permute-start.12 = (bf16[4,128,128]{2,1,0:T(8,128)(2,1)S(1)}, bf16[4,128,128]{2,1,0:T(8,128)(2,1)S(1)}, u32[]{:S(2)}, u32[]{:S(2)}) collective-permute-start(bf16[4,128,128]{2,1,0:T(8,128)(2,1)S(1)} %get-tuple-element.59), channel_id=1, source_target_pairs={{0,1},{1,0},{2,3},{3,2},{4,5},{5,4},{6,7},{7,6},{8,9},{9,8},{10,11... | collective-permute-start | bytes 393224 | tf_op jit(solution)/shard_map/ppermute | solution.py:483
  18.2 11.7 %collective-permute-start.6 = (bf16[4,128,128]{2,1,0:T(8,128)(2,1)S(1)}, bf16[4,128,128]{2,1,0:T(8,128)(2,1)S(1)}, u32[]{:S(2)}, u32[]{:S(2)}) collective-permute-start(bf16[4,128,128]{2,1,0:T(8,128)(2,1)S(1)} %get-tuple-element.54), channel_id=1, source_target_pairs={{0,2},{1,3},{2,0},{3,1},{4,6},{5,7},{6,4},{7,5},{8,10},{9,11},{10,... | collective-permute-start | bytes 393224 | tf_op jit(solution)/shard_map/ppermute | solution.py:483
  20.7 9.1 %collective-permute-start.7 = (bf16[4,128,128]{2,1,0:T(8,128)(2,1)S(1)}, bf16[4,128,128]{2,1,0:T(8,128)(2,1)S(1)}, u32[]{:S(2)}, u32[]{:S(2)}) collective-permute-start(bf16[4,128,128]{2,1,0:T(8,128)(2,1)S(1)} %get-tuple-element.55), channel_id=1, source_target_pairs={{0,3},{1,2},{2,1},{3,0},{4,7},{5,6},{6,5},{7,4},{8,11},{9,10},{10,... | collective-permute-start | bytes 393224 | tf_op jit(solution)/shard_map/ppermute | solution.py:483
  22.9 7.0 %collective-permute-start.8 = (bf16[2,128,128]{2,1,0:T(8,128)(2,1)S(1)}, bf16[2,128,128]{2,1,0:T(8,128)(2,1)S(1)}, u32[]{:S(2)}, u32[]{:S(2)}) collective-permute-start(bf16[2,128,128]{2,1,0:T(8,128)(2,1)S(1)} %get-tuple-element.44.rest_0_), channel_id=1, source_target_pairs={{0,16},{4,20},{8,24},{12,28},{16,0},{20,4},{24,8},{28,12},{1,17},{... | collective-permute-start | bytes 196616 | tf_op jit(solution)/shard_map/ppermute | solution.py:495
